TPU v7x, 32 devices: a whole 2x2x4 slice. The times are simulated.
32 devices in a mesh: fsdp: 2 (over y), ctx: 8 (over z, core), tp: 2 (over x).
Axes of the slice: x: 2, y: 2, z: 4, core: 2. Of those that a mesh axis runs over, the one named last changes fastest.
Arguments:
- tokens: bfloat16 [2, 2048, 1280], P(None, ('fsdp', 'ctx')), may hold values from -6 to 6
- lengths: int32 [2, 2, 3], P('fsdp'), may hold values from 128 to 512, as said below
- attn_gain: bfloat16 [1280], P(('fsdp', 'ctx')), may hold values from 0.5 to 1.5
- w_query: bfloat16 [1280, 1280], P(('fsdp', 'ctx'), 'tp'), may hold values from -0.15625 to 0.15625
- w_key: bfloat16 [1280, 320], P(('fsdp', 'ctx')), may hold values from -0.15625 to 0.15625
- w_value: bfloat16 [1280, 320], P(('fsdp', 'ctx')), may hold values from -0.15625 to 0.15625
- w_out: bfloat16 [1280, 1280], P('tp', ('fsdp', 'ctx')), may hold values from -2.5 to 2.5
- ffn_gain: bfloat16 [1280], P(('fsdp', 'ctx')), may hold values from 0.5 to 1.5
- w_gate: bfloat16 [1280, 3584], P(('fsdp', 'ctx'), 'tp'), may hold values from -0.15625 to 0.15625
- w_up: bfloat16 [1280, 3584], P(('fsdp', 'ctx'), 'tp'), may hold values from -0.15625 to 0.15625
- w_down: bfloat16 [3584, 1280], P('tp', ('fsdp', 'ctx')), may hold values from -0.1875 to 0.1875
- cotangent: bfloat16 [2, 2048, 1280], P(None, ('fsdp', 'ctx')), may hold values from -6 to 6
Outputs:
- output: bfloat16 [2, 2048, 1280], P(None, ('fsdp', 'ctx'))
- input_grad: float32 [2, 2048, 1280], P(None, ('fsdp', 'ctx'))
- grad_attn_gain: float32 [1280], P(('fsdp', 'ctx'))
- grad_query: float32 [1280, 1280], P(('fsdp', 'ctx'), 'tp')
- grad_key: float32 [1280, 320], P(('fsdp', 'ctx', 'tp'))
- grad_value: float32 [1280, 320], P(('fsdp', 'ctx', 'tp'))
- grad_out: float32 [1280, 1280], P('tp', ('fsdp', 'ctx'))
- grad_ffn_gain: float32 [1280], P(('fsdp', 'ctx'))
- grad_gate: float32 [1280, 3584], P(('fsdp', 'ctx'), 'tp')
- grad_up: float32 [1280, 3584], P(('fsdp', 'ctx'), 'tp')
- grad_down: float32 [3584, 1280], P('tp', ('fsdp', 'ctx'))
Inputs may be any that keep to these rules, and one draw needn't show every extreme that they name: Each row holds 3 document lengths; exactly one of them is 512, the others lie between 128 and 256; the rows of the micro-batch after the last document are padding.
All inputs are finite; a program needn't handle non-finite values.
Results may differ from a plain program's by a relative error of at most 0.019.
Values may be sent and summed in bfloat16 or wider, within the bound.
A program may use at most 192 MiB of HBM per device.

v0:
```python
import math

import jax
import jax.numpy as jnp
from jax import lax
from jax.sharding import PartitionSpec as P

H = 20
KV = 5
HD = 64


EPSILON = 1e-05
THETA = 10000.0
MASKED = -1e30


def layout(lengths_row, total_rows):
    ending = jnp.cumsum(lengths_row)
    opening = ending - lengths_row
    doc_count = lengths_row.shape[0]
    places = jnp.arange(total_rows, dtype=jnp.int32)
    segment = jnp.sum((places[:, None] >= ending[None, :]).astype(jnp.int32), axis=1)
    firsts = jnp.concatenate([opening, ending[-1:]])
    labels = jnp.arange(doc_count + 1, dtype=jnp.int32)
    begins = jnp.sum(jnp.where(segment[:, None] == labels[None, :], firsts[None, :], 0), axis=1)
    return (segment, places - begins, segment < doc_count)


def rotary(position, head_size):
    halves = head_size // 2
    inverse = jnp.exp(jnp.arange(halves, dtype=jnp.float32) * (-2.0 * math.log(THETA) / head_size))
    angles = position.astype(jnp.float32)[:, None] * inverse[None, :]
    cos_table = jnp.cos(angles)
    sin_table = jnp.sin(angles)
    return (
        jnp.concatenate([cos_table, cos_table], axis=1),
        jnp.concatenate([sin_table, sin_table], axis=1),
    )


def turn(tensor, cos_table, sin_table):
    halves = tensor.shape[-1] // 2
    rotated = jnp.concatenate([-tensor[..., halves:], tensor[..., :halves]], axis=-1)
    return tensor * cos_table[:, None, :] + rotated * sin_table[:, None, :]


def turn_back(tensor, cos_table, sin_table):
    halves = tensor.shape[-1] // 2
    shifted = tensor * sin_table[:, None, :]
    rotated = jnp.concatenate([shifted[..., halves:], -shifted[..., :halves]], axis=-1)
    return tensor * cos_table[:, None, :] + rotated


def norm_back(values, factor, gain_vec, grad_in):
    scaled = gain_vec * grad_in
    return factor * scaled - values * factor**3 * jnp.mean(scaled * values, axis=-1, keepdims=True)


def collect(attn_gain, w_query, w_key, w_value, w_out, ffn_gain, w_gate, w_up, w_down):
    return (
        lax.all_gather(attn_gain, ("fsdp", "ctx"), axis=0, tiled=True),
        lax.all_gather(w_query, ("fsdp", "ctx"), axis=0, tiled=True),
        lax.all_gather(w_key, ("fsdp", "ctx"), axis=0, tiled=True),
        lax.all_gather(w_value, ("fsdp", "ctx"), axis=0, tiled=True),
        lax.all_gather(w_out, ("fsdp", "ctx"), axis=1, tiled=True),
        lax.all_gather(ffn_gain, ("fsdp", "ctx"), axis=0, tiled=True),
        lax.all_gather(w_gate, ("fsdp", "ctx"), axis=0, tiled=True),
        lax.all_gather(w_up, ("fsdp", "ctx"), axis=0, tiled=True),
        lax.all_gather(w_down, ("fsdp", "ctx"), axis=1, tiled=True),
    )


def collect_again(attn_gain, w_query, w_key, w_value, w_out, ffn_gain, w_gate, w_up, w_down):
    return (
        lax.all_gather(attn_gain, ("fsdp", "ctx"), axis=0, tiled=True),
        lax.all_gather(w_query, ("fsdp", "ctx"), axis=0, tiled=True),
        lax.all_gather(w_key, ("fsdp", "ctx"), axis=0, tiled=True),
        lax.all_gather(w_value, ("fsdp", "ctx"), axis=0, tiled=True),
        lax.all_gather(w_out, ("fsdp", "ctx"), axis=1, tiled=True),
        lax.all_gather(ffn_gain, ("fsdp", "ctx"), axis=0, tiled=True),
        lax.all_gather(w_gate, ("fsdp", "ctx"), axis=0, tiled=True),
        lax.all_gather(w_up, ("fsdp", "ctx"), axis=0, tiled=True),
        lax.all_gather(w_down, ("fsdp", "ctx"), axis=1, tiled=True),
    )


def reduce_grads(main_part, pair_part):
    shares = (
        lax.psum_scatter(main_part[0], ("fsdp", "ctx"), scatter_dimension=0, tiled=True),
        lax.psum_scatter(main_part[1], ("fsdp", "ctx"), scatter_dimension=0, tiled=True),
        lax.psum_scatter(main_part[2], ("fsdp", "ctx"), scatter_dimension=1, tiled=True),
        lax.psum_scatter(main_part[3], ("fsdp", "ctx"), scatter_dimension=0, tiled=True),
        lax.psum_scatter(main_part[4], ("fsdp", "ctx"), scatter_dimension=0, tiled=True),
        lax.psum_scatter(main_part[5], ("fsdp", "ctx"), scatter_dimension=0, tiled=True),
        lax.psum_scatter(main_part[6], ("fsdp", "ctx"), scatter_dimension=1, tiled=True),
    )
    pairs = (
        lax.psum_scatter(pair_part[0], ("fsdp", "ctx", "tp"), scatter_dimension=0, tiled=True),
        lax.psum_scatter(pair_part[1], ("fsdp", "ctx", "tp"), scatter_dimension=0, tiled=True),
    )
    return (shares, pairs)


def block_allowed(segment_rows, places_rows, segment_all, block_at, key_block):
    segment_keys = lax.dynamic_slice_in_dim(segment_all, block_at * key_block, key_block)
    place_keys = block_at * key_block + jnp.arange(key_block, dtype=jnp.int32)
    return (segment_rows[:, None] == segment_keys[None, :]) & (
        place_keys[None, :] <= places_rows[:, None]
    )


def sweep(visit, initial, block_count, useful):

    def advance(block_at, state):
        return lax.cond(
            useful(block_at),
            lambda current: visit(block_at, current),
            lambda current: current,
            state,
        )

    return lax.fori_loop(0, block_count, advance, initial)


def shards(
    tokens,
    lengths,
    attn_gain,
    w_query,
    w_key,
    w_value,
    w_out,
    ffn_gain,
    w_gate,
    w_up,
    w_down,
    cotangent,
):
    f32 = jnp.float32
    b16 = jnp.bfloat16
    micro_count = tokens.shape[0]
    tok_rows = tokens.shape[1]
    model_width = tokens.shape[2]
    ctx_count = lax.axis_size("ctx")
    tp_count = lax.axis_size("tp")
    ctx_at = lax.axis_index("ctx")
    tp_at = lax.axis_index("tp")
    total_rows = tok_rows * ctx_count
    half_rows = tok_rows // tp_count
    local_heads = w_query.shape[1] // HD
    kv_width = KV * HD
    scaling = 1.0 / math.sqrt(HD)
    key_block = min(512, total_rows)
    block_count = total_rows // key_block
    heads_global = tp_at * local_heads + jnp.arange(local_heads, dtype=jnp.int32)
    select = heads_global[:, None] // (H // KV) == jnp.arange(KV, dtype=jnp.int32)[None, :]
    select_low = select.astype(b16)
    select_high = select.astype(f32)
    row_offset = tp_at * half_rows
    start_row = ctx_at * tok_rows
    places_mine = start_row + jnp.arange(tok_rows, dtype=jnp.int32)
    outputs_list = []
    input_list = []
    main_total = None
    pair_total = None
    for micro_at in range(micro_count):
        gathered = collect(
            attn_gain, w_query, w_key, w_value, w_out, ffn_gain, w_gate, w_up, w_down
        )
        (
            gain_first,
            query_full,
            key_full,
            value_full,
            out_full,
            gain_second,
            gate_full,
            up_full,
            down_full,
        ) = gathered
        inputs = tokens[micro_at].astype(f32)
        segment_all, position_all, live_all = layout(lengths[0, micro_at], total_rows)
        segment_mine = lax.dynamic_slice_in_dim(segment_all, start_row, tok_rows)
        position_mine = lax.dynamic_slice_in_dim(position_all, start_row, tok_rows)
        live_mine = lax.dynamic_slice_in_dim(live_all, start_row, tok_rows)
        cos_table, sin_table = rotary(position_mine, HD)
        rms_first = lax.rsqrt(jnp.mean(inputs * inputs, axis=-1, keepdims=True) + EPSILON)
        normed_first = (inputs * rms_first * gain_first.astype(f32)).astype(b16)
        queries = jnp.dot(normed_first, query_full, preferred_element_type=f32).reshape(
            tok_rows, local_heads, HD
        )
        queries = turn(queries, cos_table, sin_table).astype(b16)
        key_lin = jnp.dot(normed_first, key_full, preferred_element_type=f32).reshape(
            tok_rows, KV, HD
        )
        key_rot = turn(key_lin, cos_table, sin_table).astype(b16).reshape(tok_rows, kv_width)
        value_rot = jnp.dot(normed_first, value_full, preferred_element_type=f32).astype(b16)
        keys_all, values_all = (
            lax.all_gather(key_rot, "ctx", axis=0, tiled=True),
            lax.all_gather(value_rot, "ctx", axis=0, tiled=True),
        )
        keys_local = jnp.einsum(
            "tjd,hj->thd",
            keys_all.reshape(total_rows, KV, HD),
            select_low,
            preferred_element_type=f32,
        ).astype(b16)
        values_local = jnp.einsum(
            "tjd,hj->thd",
            values_all.reshape(total_rows, KV, HD),
            select_low,
            preferred_element_type=f32,
        ).astype(b16)

        def useful(block_at):
            return jnp.any(
                block_allowed(segment_mine, places_mine, segment_all, block_at, key_block)
            )

        def logits_of(block_at):
            key_rows = lax.dynamic_slice_in_dim(keys_local, block_at * key_block, key_block)
            raw_scores = (
                jnp.einsum("qhd,khd->hqk", queries, key_rows, preferred_element_type=f32) * scaling
            )
            allowed = block_allowed(segment_mine, places_mine, segment_all, block_at, key_block)
            return jnp.where(allowed[None], raw_scores, MASKED)

        def statistic(block_at, state):
            top_score, mass_sum = state
            logits = logits_of(block_at)
            new_top = jnp.maximum(top_score, jnp.max(logits, axis=-1))
            mass_sum = mass_sum * jnp.exp(top_score - new_top) + jnp.sum(
                jnp.exp(logits - new_top[..., None]), axis=-1
            )
            return (new_top, mass_sum)

        start_state = (
            jnp.full((local_heads, tok_rows), MASKED, f32),
            jnp.zeros((local_heads, tok_rows), f32),
        )
        top_score, mass_sum = sweep(statistic, start_state, block_count, useful)

        def probable(block_at):
            return jnp.exp(logits_of(block_at) - top_score[..., None]) / mass_sum[..., None]

        def accumulate(block_at, running):
            probs_low = probable(block_at).astype(b16)
            value_rows = lax.dynamic_slice_in_dim(values_local, block_at * key_block, key_block)
            return running + jnp.einsum(
                "hqk,khd->qhd", probs_low, value_rows, preferred_element_type=f32
            )

        attended = sweep(
            accumulate, jnp.zeros((tok_rows, local_heads, HD), f32), block_count, useful
        )
        attended_low = attended.reshape(tok_rows, local_heads * HD).astype(b16)
        branch = lax.psum(
            jnp.dot(attended_low, out_full, preferred_element_type=f32).astype(jnp.bfloat16), "tp"
        ).astype(jnp.float32)
        hidden = inputs + branch
        rms_second = lax.rsqrt(jnp.mean(hidden * hidden, axis=-1, keepdims=True) + EPSILON)
        normed_second = (hidden * rms_second * gain_second.astype(f32)).astype(b16)
        gate_pre = jnp.dot(normed_second, gate_full, preferred_element_type=f32)
        upward = jnp.dot(normed_second, up_full, preferred_element_type=f32)
        sigmoid_gate = jax.nn.sigmoid(gate_pre)
        silu_gate = jax.nn.silu(gate_pre)
        active = (silu_gate * upward).astype(b16)
        mixed = lax.psum(
            jnp.dot(active, down_full, preferred_element_type=f32).astype(jnp.bfloat16), "tp"
        ).astype(jnp.float32)
        outputs_list.append((hidden + mixed).astype(b16))
        gathered = collect_again(
            attn_gain, w_query, w_key, w_value, w_out, ffn_gain, w_gate, w_up, w_down
        )
        (
            gain_first,
            query_full,
            key_full,
            value_full,
            out_full,
            gain_second,
            gate_full,
            up_full,
            down_full,
        ) = gathered
        grad_rows = cotangent[micro_at].astype(f32) * live_mine[:, None].astype(f32)
        grad_low = grad_rows.astype(b16)
        grad_down = jnp.einsum("tf,td->fd", active, grad_low, preferred_element_type=f32)
        grad_active = jnp.einsum("td,fd->tf", grad_low, down_full, preferred_element_type=f32)
        grad_gate_pre = (
            grad_active * upward * sigmoid_gate * (1.0 + gate_pre * (1.0 - sigmoid_gate))
        ).astype(b16)
        grad_upward = (grad_active * silu_gate).astype(b16)
        grad_gate = jnp.einsum(
            "te,tf->ef", normed_second, grad_gate_pre, preferred_element_type=f32
        )
        grad_up = jnp.einsum("te,tf->ef", normed_second, grad_upward, preferred_element_type=f32)
        grad_normed_second = jnp.einsum(
            "tf,ef->te", grad_gate_pre, gate_full, preferred_element_type=f32
        ) + jnp.einsum("tf,ef->te", grad_upward, up_full, preferred_element_type=f32)
        grad_normed_second = lax.psum(grad_normed_second.astype(jnp.bfloat16), "tp").astype(
            jnp.float32
        )
        grad_gain_second = jnp.sum(grad_normed_second * hidden * rms_second, axis=0)
        grad_hidden = grad_rows + norm_back(
            hidden, rms_second, gain_second.astype(f32), grad_normed_second
        )
        grad_branch = grad_hidden.astype(b16)
        grad_out = jnp.einsum("te,td->ed", attended_low, grad_branch, preferred_element_type=f32)
        grad_att = (
            jnp.einsum("td,ed->te", grad_branch, out_full, preferred_element_type=f32)
            .astype(b16)
            .reshape(tok_rows, local_heads, HD)
        )
        delta_rows = jnp.sum(grad_att.astype(f32) * attended, axis=-1).T

        def backward_visit(block_at, state):
            grad_queries, grad_keys, grad_values = state
            first_row = block_at * key_block
            key_rows = lax.dynamic_slice_in_dim(keys_local, first_row, key_block)
            value_rows = lax.dynamic_slice_in_dim(values_local, first_row, key_block)
            probs = probable(block_at)
            probs_low = probs.astype(b16)
            grad_probs = jnp.einsum(
                "qhd,khd->hqk", grad_att, value_rows, preferred_element_type=f32
            )
            grad_logits = (probs * (grad_probs - delta_rows[..., None])).astype(b16)
            grad_queries = (
                grad_queries
                + jnp.einsum("hqk,khd->qhd", grad_logits, key_rows, preferred_element_type=f32)
                * scaling
            )
            key_part = (
                jnp.einsum("hqk,qhd->khd", grad_logits, queries, preferred_element_type=f32)
                * scaling
            )
            value_part = jnp.einsum("hqk,qhd->khd", probs_low, grad_att, preferred_element_type=f32)
            grad_keys = lax.dynamic_update_slice_in_dim(grad_keys, key_part, first_row, 0)
            grad_values = lax.dynamic_update_slice_in_dim(grad_values, value_part, first_row, 0)
            return (grad_queries, grad_keys, grad_values)

        back_state = (
            jnp.zeros((tok_rows, local_heads, HD), f32),
            jnp.zeros((total_rows, local_heads, HD), f32),
            jnp.zeros((total_rows, local_heads, HD), f32),
        )
        grad_queries, grad_keys, grad_values = sweep(
            backward_visit, back_state, block_count, useful
        )
        key_heads = jnp.einsum(
            "thd,hj->tjd", grad_keys, select_high, precision=lax.Precision.HIGHEST
        ).reshape(total_rows, kv_width)
        value_heads = jnp.einsum(
            "thd,hj->tjd", grad_values, select_high, precision=lax.Precision.HIGHEST
        ).reshape(total_rows, kv_width)
        key_sum, value_sum = (
            lax.psum_scatter(
                key_heads.astype(jnp.bfloat16), ("ctx", "tp"), scatter_dimension=0, tiled=True
            ).astype(jnp.float32),
            lax.psum_scatter(
                value_heads.astype(jnp.bfloat16), ("ctx", "tp"), scatter_dimension=0, tiled=True
            ).astype(jnp.float32),
        )
        cos_half = lax.dynamic_slice_in_dim(cos_table, row_offset, half_rows)
        sin_half = lax.dynamic_slice_in_dim(sin_table, row_offset, half_rows)
        grad_key_lin = (
            turn_back(key_sum.reshape(half_rows, KV, HD), cos_half, sin_half)
            .astype(b16)
            .reshape(half_rows, kv_width)
        )
        grad_value_lin = value_sum.astype(b16)
        normed_half = lax.dynamic_slice_in_dim(normed_first, row_offset, half_rows)
        grad_key = jnp.einsum("te,tk->ek", normed_half, grad_key_lin, preferred_element_type=f32)
        grad_value = jnp.einsum(
            "te,tk->ek", normed_half, grad_value_lin, preferred_element_type=f32
        )
        grad_normed_pair = jnp.einsum(
            "tk,ek->te", grad_key_lin, key_full, preferred_element_type=f32
        ) + jnp.einsum("tk,ek->te", grad_value_lin, value_full, preferred_element_type=f32)
        grad_query_lin = (
            turn_back(grad_queries, cos_table, sin_table)
            .astype(b16)
            .reshape(tok_rows, local_heads * HD)
        )
        grad_query = jnp.einsum(
            "te,tq->eq", normed_first, grad_query_lin, preferred_element_type=f32
        )
        grad_normed_first = jnp.einsum(
            "tq,eq->te", grad_query_lin, query_full, preferred_element_type=f32
        )
        grad_normed_first = grad_normed_first + lax.dynamic_update_slice_in_dim(
            jnp.zeros((tok_rows, model_width), f32), grad_normed_pair, row_offset, 0
        )
        grad_normed_first = lax.psum(grad_normed_first.astype(jnp.bfloat16), "tp").astype(
            jnp.float32
        )
        grad_gain_first = jnp.sum(grad_normed_first * inputs * rms_first, axis=0)
        input_list.append(
            grad_hidden + norm_back(inputs, rms_first, gain_first.astype(f32), grad_normed_first)
        )
        main_part = (
            grad_gain_first,
            grad_query,
            grad_out,
            grad_gain_second,
            grad_gate,
            grad_up,
            grad_down,
        )
        pair_part = (grad_key, grad_value)
        main_part, pair_part = reduce_grads(main_part, pair_part)
        if main_total is None:
            main_total = main_part
            pair_total = pair_part
        else:
            main_total = jax.tree.map(jnp.add, main_total, main_part)
            pair_total = jax.tree.map(jnp.add, pair_total, pair_part)
    return (
        jnp.stack(outputs_list),
        jnp.stack(input_list),
        main_total[0],
        main_total[1],
        pair_total[0],
        pair_total[1],
        main_total[2],
        main_total[3],
        main_total[4],
        main_total[5],
        main_total[6],
    )


def solution(mesh):
    placed = (
        P(None, ("fsdp", "ctx"), None),
        P("fsdp", None, None),
        P(("fsdp", "ctx")),
        P(("fsdp", "ctx"), "tp"),
        P(("fsdp", "ctx"), None),
        P(("fsdp", "ctx"), None),
        P("tp", ("fsdp", "ctx")),
        P(("fsdp", "ctx")),
        P(("fsdp", "ctx"), "tp"),
        P(("fsdp", "ctx"), "tp"),
        P("tp", ("fsdp", "ctx")),
        P(None, ("fsdp", "ctx"), None),
    )
    return jax.shard_map(
        shards,
        mesh=mesh,
        in_specs=placed,
        out_specs=(
            P(None, ("fsdp", "ctx"), None),
            P(None, ("fsdp", "ctx"), None),
            P(("fsdp", "ctx")),
            P(("fsdp", "ctx"), "tp"),
            P(("fsdp", "ctx", "tp"), None),
            P(("fsdp", "ctx", "tp"), None),
            P("tp", ("fsdp", "ctx")),
            P(("fsdp", "ctx")),
            P(("fsdp", "ctx"), "tp"),
            P(("fsdp", "ctx"), "tp"),
            P("tp", ("fsdp", "ctx")),
        ),
        check_vma=False,
    )
```

profile of v0, /device:TPU:0, one launch (start us, length us, event | category | flops | bytes accessed | tf_op | source)
XLA Modules:
  0.0 1490.9 jit_solution(6876496791607598735)
XLA Ops:
  15.5 36.7 %all-reduce.7 = (bf16[1280]{0:T(1024)(128)(2,1)S(1)}, bf16[1280]{0:T(1024)(128)(2,1)}) all-reduce(bf16[1280]{0:T(1024)(128)(2,1)S(1)} %dynamic-update-slice.2, bf16[1280]{0:T(1024)(128)(2,1)S(1)} %dynamic-update-slice.3), channel_id=1, replica_groups=mesh['fsdp'=2,'ctx'=8,'tp'=2] {'fsdp','ctx'}, use_global_device_ids=true, to_apply=%add | all-reduce | flops 2560 | bytes 10240
  53.5 25.1 %all_gather.29 = bf16[1280,320]{1,0:T(8,128)(2,1)S(1)} all-gather(bf16[80,320]{1,0:T(8,128)(2,1)} %param.40), channel_id=1, replica_groups=mesh['fsdp'=2,'ctx'=8,'tp'=2] {'fsdp','ctx'}, dimensions={0}, use_global_device_ids=true | all-gather | bytes 870400 | tf_op jit(solution)/shard_map/all_gather | solution.py:64
  81.7 25.4 %all_gather.27 = bf16[1280,320]{1,0:T(8,128)(2,1)S(1)} all-gather(bf16[80,320]{1,0:T(8,128)(2,1)S(1)} %copy-done.94), channel_id=1, replica_groups=mesh['fsdp'=2,'ctx'=8,'tp'=2] {'fsdp','ctx'}, dimensions={0}, use_global_device_ids=true | all-gather | bytes 870400 | tf_op jit(solution)/shard_map/all_gather | solution.py:65
  107.7 14.9 all_gather.37
  129.0 14.9 all_gather.38
  146.0 14.9 all_gather.28
  164.2 15.1 %all_gather.30 = bf16[1024,320]{0,1:T(8,128)(2,1)S(1)} all-gather(bf16[128,320]{0,1:T(8,128)(2,1)S(1)} %bitcast.431), channel_id=1, replica_groups=mesh['fsdp'=2,'ctx'=8,'tp'=2] {'ctx'}, dimensions={0}, use_global_device_ids=true | all-gather | bytes 737280 | tf_op jit(solution)/shard_map/all_gather | solution.py:200
  229.6 39.6 %all-reduce.19.cloned.1.call-done = (bf16[128,1280]{1,0:T(8,128)(2,1)}, bf16[128,1280]{1,0:T(8,128)(2,1)}) async-done(((bf16[128,1280]{1,0:T(8,128)(2,1)}, bf16[128,1280]{1,0:T(8,128)(2,1)}), (bf16[128,1280]{1,0:T(8,128)(2,1)}, bf16[128,1280]{1,0:T(8,128)(2,1)})) %all-reduce.19.cloned.1.call-update) | async-done | bytes 655376 | tf_op jit(solution)/shard_map/psum | solution.py:258
  272.0 52.0 %all-gather.10.cloned.1.call-done = bf16[1280,1792]{1,0:T(8,128)(2,1)} async-done(((bf16[80,1792]{1,0:T(8,128)(2,1)}), bf16[1280,1792]{1,0:T(8,128)(2,1)}) %all-gather.10.cloned.1.call-update) | async-done | bytes 4587536 | tf_op jit(solution)/shard_map/all_gather | solution.py:68
  328.1 49.2 %all-gather.12.cloned.1.call-done = bf16[1280,1792]{1,0:T(8,128)(2,1)} async-done(((bf16[80,1792]{1,0:T(8,128)(2,1)}), bf16[1280,1792]{1,0:T(8,128)(2,1)}) %all-gather.12.cloned.1.call-update) | async-done | bytes 4587536 | tf_op jit(solution)/shard_map/all_gather | solution.py:69
  385.8 44.8 %all-gather.14.cloned.1.call-done = bf16[1792,1280]{0,1:T(8,128)(2,1)} async-done(((bf16[1792,80]{0,1:T(8,128)(2,1)}), bf16[1792,1280]{0,1:T(8,128)(2,1)}) %all-gather.14.cloned.1.call-update) | async-done | bytes 4587536 | tf_op jit(solution)/shard_map/all_gather | solution.py:70
  453.0 22.7 %all-reduce.17.cloned.1.call-done = (bf16[128,1280]{1,0:T(8,128)(2,1)}, bf16[128,1280]{1,0:T(8,128)(2,1)}) async-done(((bf16[128,1280]{1,0:T(8,128)(2,1)}, bf16[128,1280]{1,0:T(8,128)(2,1)}), (bf16[128,1280]{1,0:T(8,128)(2,1)}, bf16[128,1280]{1,0:T(8,128)(2,1)})) %all-reduce.17.cloned.1.call-update) | async-done | bytes 655376 | tf_op jit(solution)/shard_map/psum | solution.py:302
  550.7 17.2 %reduce-scatter.38.cloned.1.call-done = bf16[64,320]{1,0:T(8,128)(2,1)} async-done(((bf16[1024,320]{1,0:T(8,128)(2,1)}), bf16[64,320]{1,0:T(8,128)(2,1)}) %reduce-scatter.38.cloned.1.call-update) | async-done | bytes 40976
  569.4 57.8 %reduce-scatter.40.cloned.1.call-done = bf16[64,320]{1,0:T(8,128)(2,1)} async-done(((bf16[1024,320]{1,0:T(8,128)(2,1)}), bf16[64,320]{1,0:T(8,128)(2,1)}) %reduce-scatter.40.cloned.1.call-update) | async-done | bytes 40976
  631.2 55.2 %reduce-scatter.34.cloned.1.call-done = bf16[64,320]{1,0:T(8,128)(2,1)} async-done(((bf16[1024,320]{1,0:T(8,128)(2,1)}), bf16[64,320]{1,0:T(8,128)(2,1)}) %reduce-scatter.34.cloned.1.call-update) | async-done | bytes 40976
  688.6 57.2 %reduce-scatter.36.cloned.1.call-done = bf16[64,320]{1,0:T(8,128)(2,1)} async-done(((bf16[1024,320]{1,0:T(8,128)(2,1)}), bf16[64,320]{1,0:T(8,128)(2,1)}) %reduce-scatter.36.cloned.1.call-update) | async-done | bytes 40976
  796.5 61.1 %all-reduce.6 = (f32[1280]{0:T(1024)S(1)}, f32[1280]{0:T(1024)S(1)}) all-reduce(f32[1280]{0:T(1024)S(1)} %add.647, f32[1280]{0:T(1024)S(1)} %add.652), channel_id=15, replica_groups=mesh['fsdp'=2,'ctx'=8,'tp'=2] {'fsdp','ctx'}, use_global_device_ids=true, to_apply=%region_63.64.clone | all-reduce | flops 2560 | bytes 20480
  862.7 37.1 %reduce-scatter.42.cloned.1.call-done = f32[40,320]{1,0:T(8,128)} async-done(((f32[1280,320]{1,0:T(8,128)}), f32[40,320]{1,0:T(8,128)}) %reduce-scatter.42.cloned.1.call-update) | async-done | bytes 51216
  899.8 103.5 %reduce-scatter.44.cloned.1.call-done = f32[40,320]{1,0:T(8,128)} async-done(((f32[1280,320]{1,0:T(8,128)}), f32[40,320]{1,0:T(8,128)}) %reduce-scatter.44.cloned.1.call-update) | async-done | bytes 51216
  1003.3 70.3 %reduce-scatter.24.cloned.1.call-done = f32[80,640]{1,0:T(8,128)} async-done(((f32[1280,640]{1,0:T(8,128)}), f32[80,640]{1,0:T(8,128)}) %reduce-scatter.24.cloned.1.call-update) | async-done | bytes 204816 | tf_op jit(solution)/shard_map/reduce_scatter | solution.py:91
  1073.6 70.1 %reduce-scatter.26.cloned.1.call-done = f32[640,80]{0,1:T(8,128)} async-done(((f32[640,1280]{0,1:T(8,128)}), f32[640,80]{0,1:T(8,128)}) %reduce-scatter.26.cloned.1.call-update) | async-done | bytes 204816 | tf_op jit(solution)/shard_map/reduce_scatter | solution.py:92
  1143.7 112.8 %reduce-scatter.28.cloned.1.call-done = f32[80,1792]{1,0:T(8,128)} async-done(((f32[1280,1792]{1,0:T(8,128)}), f32[80,1792]{1,0:T(8,128)}) %reduce-scatter.28.cloned.1.call-update) | async-done | bytes 573456 | tf_op jit(solution)/shard_map/reduce_scatter | solution.py:94
  1256.5 113.6 %reduce-scatter.30.cloned.1.call-done = f32[80,1792]{1,0:T(8,128)} async-done(((f32[1280,1792]{1,0:T(8,128)}), f32[80,1792]{1,0:T(8,128)}) %reduce-scatter.30.cloned.1.call-update) | async-done | bytes 573456 | tf_op jit(solution)/shard_map/reduce_scatter | solution.py:95
  1370.1 113.8 %reduce-scatter.32.cloned.1.call-done = f32[1792,80]{0,1:T(8,128)} async-done(((f32[1792,1280]{0,1:T(8,128)}), f32[1792,80]{0,1:T(8,128)}) %reduce-scatter.32.cloned.1.call-update) | async-done | bytes 573456 | tf_op jit(solution)/shard_map/reduce_scatter | solution.py:96
  (550 shorter events, 317.4 us)
Async XLA Ops:
  7.2 173.7 %all-gather.6.cloned.1.call-start = ((), (), s32[]{:S(2)}) async-start(), calls=%async_computation.11 | async-start | bytes 1740800 | tf_op jit(solution)/shard_map/all_gather | solution.py:63
  7.9 213.2 %all-gather.8.cloned.1.call-start = ((), (), s32[]{:S(2)}) async-start(), calls=%async_computation.12 | async-start | bytes 1740800 | tf_op jit(solution)/shard_map/all_gather | solution.py:66
  8.7 260.6 %all-reduce.19.cloned.1.call-start = ((), (), s32[]{:S(2)}) async-start(), calls=%async_computation.29 | async-start | bytes 1310720 | tf_op jit(solution)/shard_map/psum | solution.py:258
  52.2 132.2 %copy-start.76 = (f32[1280]{0:T(1024)}, f32[1280]{0:T(1024)S(1)}, u32[]{:S(2)}) copy-start(f32[1280]{0:T(1024)S(1)} %convert_element_type.367) | copy-start | bytes 15364
  226.8 97.2 %all-gather.10.cloned.1.call-start = ((), (), s32[]{:S(2)}) async-start(), calls=%async_computation.13 | async-start | bytes 4874240 | tf_op jit(solution)/shard_map/all_gather | solution.py:68
  227.3 149.9 %all-gather.12.cloned.1.call-start = ((), (), s32[]{:S(2)}) async-start(), calls=%async_computation.14 | async-start | bytes 4874240 | tf_op jit(solution)/shard_map/all_gather | solution.py:69
  227.9 202.6 %all-gather.14.cloned.1.call-start = ((), (), s32[]{:S(2)}) async-start(), calls=%async_computation.15 | async-start | bytes 4874240 | tf_op jit(solution)/shard_map/all_gather | solution.py:70
  228.5 247.1 %all-reduce.17.cloned.1.call-start = ((), (), s32[]{:S(2)}) async-start(), calls=%async_computation.28 | async-start | bytes 1310720 | tf_op jit(solution)/shard_map/psum | solution.py:302
  228.9 249.0 %copy-start.106 = (f32[128]{0:T(128)}, f32[128]{0:T(128)S(1)}, u32[]{:S(2)}) copy-start(f32[128]{0:T(128)S(1)} %get-tuple-element.1987) | copy-start | bytes 1540
  228.9 249.0 %copy-start.108 = (f32[128]{0:T(128)}, f32[128]{0:T(128)S(1)}, u32[]{:S(2)}) copy-start(f32[128]{0:T(128)S(1)} %get-tuple-element.1988) | copy-start | bytes 1540
  445.4 122.5 %reduce-scatter.38.cloned.1.call-start = ((), (), s32[]{:S(2)}) async-start(), calls=%async_computation.23 | async-start | bytes 835584
  504.0 123.2 %reduce-scatter.40.cloned.1.call-start = ((), (), s32[]{:S(2)}) async-start(), calls=%async_computation.24 | async-start | bytes 835584
  517.5 168.9 %reduce-scatter.34.cloned.1.call-start = ((), (), s32[]{:S(2)}) async-start(), calls=%async_computation.21 | async-start | bytes 835584
  542.5 203.3 %reduce-scatter.36.cloned.1.call-start = ((), (), s32[]{:S(2)}) async-start(), calls=%async_computation.22 | async-start | bytes 835584
  544.5 250.6 %all-reduce.15.cloned.1.call-start = ((), (), s32[]{:S(2)}) async-start(), calls=%async_computation.27 | async-start | bytes 2621440 | tf_op jit(solution)/shard_map/psum | solution.py:269
  568.9 118.5 %copy-start.91 = (f32[64,64]{0,1:T(8,128)S(1)}, f32[64,64]{0,1:T(8,128)}, u32[]{:S(2)}) copy-start(f32[64,64]{0,1:T(8,128)} %fusion.223) | copy-start | bytes 49156
  569.0 118.5 %copy-start.92 = (f32[64,64]{0,1:T(8,128)S(1)}, f32[64,64]{0,1:T(8,128)}, u32[]{:S(2)}) copy-start(f32[64,64]{0,1:T(8,128)} %fusion.224) | copy-start | bytes 49156
  750.0 149.8 %reduce-scatter.42.cloned.1.call-start = ((), (), s32[]{:S(2)}) async-start(), calls=%async_computation.25 | async-start | bytes 2027520
  752.4 250.9 %reduce-scatter.44.cloned.1.call-start = ((), (), s32[]{:S(2)}) async-start(), calls=%async_computation.26 | async-start | bytes 2027520
  754.9 318.7 %reduce-scatter.24.cloned.1.call-start = ((), (), s32[]{:S(2)}) async-start(), calls=%async_computation.16 | async-start | bytes 3481600 | tf_op jit(solution)/shard_map/reduce_scatter | solution.py:91
  758.1 385.6 %reduce-scatter.26.cloned.1.call-start = ((), (), s32[]{:S(2)}) async-start(), calls=%async_computation.17 | async-start | bytes 3481600 | tf_op jit(solution)/shard_map/reduce_scatter | solution.py:92
  762.3 494.2 %reduce-scatter.28.cloned.1.call-start = ((), (), s32[]{:S(2)}) async-start(), calls=%async_computation.18 | async-start | bytes 9748480 | tf_op jit(solution)/shard_map/reduce_scatter | solution.py:94
  769.8 600.3 %reduce-scatter.30.cloned.1.call-start = ((), (), s32[]{:S(2)}) async-start(), calls=%async_computation.19 | async-start | bytes 9748480 | tf_op jit(solution)/shard_map/reduce_scatter | solution.py:95
  777.1 706.8 %reduce-scatter.32.cloned.1.call-start = ((), (), s32[]{:S(2)}) async-start(), calls=%async_computation.20 | async-start | bytes 9748480 | tf_op jit(solution)/shard_map/reduce_scatter | solution.py:96
  (112 other events, 1573.0 us)
Sparse Core Ops, SparseCore 0:
  10.2 42.7 all-gather.5
  55.3 40.3 all-gather.7
  226.9 42.3 all-reduce.18
  271.4 52.5 all-gather.9
  326.2 51.0 all-gather.11
  379.4 51.0 all-gather.13
  445.6 30.0 all-reduce.16
  504.1 63.7 reduce-scatter.37
  571.5 55.7 reduce-scatter.39
  630.6 55.7 reduce-scatter.33
  690.0 55.7 reduce-scatter.35
  750.1 44.9 all-reduce.14
  800.9 98.8 reduce-scatter.41
  905.5 97.7 reduce-scatter.43
  1007.6 66.0 reduce-scatter.23
  1077.9 65.8 reduce-scatter.25
  1148.3 108.1 reduce-scatter.27
  1261.0 109.0 reduce-scatter.29
  1374.8 109.0 reduce-scatter.31
where the time goes:
time: 1500 us; the launch traced here: 1490 us
  waiting for transfers between devices  1030 us (69%)
  blocking collectives  208 us (14%)
  matrix products  127 us (8%)
  local copies, waits for them, and re-layouts  52.9 us (4%)
  other arithmetic  46.4 us (3%)
  between operations  17.3 us (1%)
    unnamed x25, waiting for transfers between devices  331 us
    reduce_scatter x1, waiting for transfers between devices, reduce_grads(): lax.psum_scatter(main_part[6], ('fsdp', 'ctx'), scatter_dimension=1, tile...  114 us
    reduce_scatter x1, waiting for transfers between devices, reduce_grads(): lax.psum_scatter(main_part[5], ('fsdp', 'ctx'), scatter_dimension=0, tile...  114 us
    reduce_scatter x1, waiting for transfers between devices, reduce_grads(): lax.psum_scatter(main_part[4], ('fsdp', 'ctx'), scatter_dimension=0, tile...  113 us
    unnamed x2, blocking collectives  97.8 us
    reduce_scatter x1, waiting for transfers between devices, reduce_grads(): lax.psum_scatter(main_part[1], ('fsdp', 'ctx'), scatter_dimension=0, tile...  70.3 us
    reduce_scatter x1, waiting for transfers between devices, reduce_grads(): lax.psum_scatter(main_part[2], ('fsdp', 'ctx'), scatter_dimension=1, tile...  70.1 us
    all_gather x1, waiting for transfers between devices, collect(): lax.all_gather(w_gate, ('fsdp', 'ctx'), axis=0, tiled=True)  52 us
  transfers between devices with their start and end apart: 19, of which 17 were waited for; matrix products, arithmetic and copies ran while one was open for 11% of the time, Pallas kernels for 0%

commit v1 on v0

--- a/solution.py
+++ b/solution.py
@@ -1,8 +1,11 @@
+import functools
 import math
 
 import jax
 import jax.numpy as jnp
 from jax import lax
+from jax.experimental import pallas as pl
+from jax.experimental.pallas import tpu as pltpu
 from jax.sharding import PartitionSpec as P
 
 H = 20
@@ -431,6 +434,539 @@
     )
 
 
+F32 = jnp.float32
+B16 = jnp.bfloat16
+HD = 64
+EPSILON = 1e-05
+THETA = 10000.0
+MASKED = -1e30
+SCALE = 1.0 / math.sqrt(HD)
+VMEM = pltpu.VMEM
+
+def nn(a, b): return lax.dot_general(a, b, (((1,), (0,)), ((), ())), preferred_element_type=F32)
+def nt(a, b): return lax.dot_general(a, b, (((1,), (1,)), ((), ())), preferred_element_type=F32)
+def tn(a, b): return lax.dot_general(a, b, (((0,), (0,)), ((), ())), preferred_element_type=F32)
+
+def lanes(shape): return lax.broadcasted_iota(jnp.int32, shape, len(shape) - 1)
+
+def rope(t, cos, sin):
+    low = lanes(t.shape) % 64 < 32
+    rot = jnp.where(low, -pltpu.roll(t, 96, 1), pltpu.roll(t, 32, 1))
+    return t * cos + rot * sin
+
+def rope_back(u, cos, sin):
+    low = lanes(u.shape) % 64 < 32
+    us = u * sin
+    return u * cos + jnp.where(low, pltpu.roll(us, 96, 1), -pltpu.roll(us, 32, 1))
+
+def rms(v): return lax.rsqrt(jnp.mean(v * v, axis=-1, keepdims=True) + EPSILON)
+
+def norm_back(v, r, gain, d):
+    s = gain * d
+    return r * s - v * (r * r * r) * jnp.mean(s * v, axis=-1, keepdims=True)
+
+def project(x_ref, gain_ref, a_ref, cos_ref, sin_ref, n1_ref, q_ref, kv_ref):
+    x = x_ref[...].astype(F32)
+    n1 = (x * rms(x) * gain_ref[...]).astype(B16)
+    n1_ref[...] = n1
+    lin = nn(n1, a_ref[...])
+    qw = q_ref.shape[1]
+    cos, sin = cos_ref[...], sin_ref[...]
+    for i in range(lin.shape[1] // 128):
+        tile = lin[:, 128 * i:128 * (i + 1)]
+        j = i - qw // 128
+        if j <= 0:
+            tile = rope(tile, cos, sin)
+        elif j == 1:
+            tile = jnp.where(lanes(tile.shape) < 64, rope(tile, cos, sin), tile)
+        if j < 0: q_ref[:, 128 * i:128 * (i + 1)] = tile.astype(B16)
+        else: kv_ref[:, 128 * j:128 * (j + 1)] = tile.astype(B16)
+
+def doubled(tile, which):
+    t = tile.astype(F32)
+    r = pltpu.roll(t, 64, 1)
+    low = lanes(t.shape) < 64
+    return (jnp.where(low, t, r) if which == 0 else jnp.where(low, r, t)).astype(B16)
+
+def window_start(t, nblk): return jnp.maximum(t - nblk + 1, 0)
+
+def window(kvall_ref, w0, nblk, m, rows, tile):
+    return jnp.concatenate([kvall_ref[w0 + b, m * rows:(m + 1) * rows, 128 * tile:128 * (tile + 1)] for b in range(nblk)], axis=0)
+
+def heads_kv(kvall_ref, w0, nblk, m, rows):
+    k01 = window(kvall_ref, w0, nblk, m, rows, 0)
+    k2v2 = window(kvall_ref, w0, nblk, m, rows, 1)
+    v01 = window(kvall_ref, w0, nblk, m, rows, 2)
+    ks = [doubled(k01, 0), doubled(k01, 1), doubled(k2v2, 0)]
+    vs = [doubled(v01, 0), doubled(v01, 1), doubled(k2v2, 1)]
+    return ks, vs
+
+def pick(group, p, tp):
+    a, b = p // 2, (p + 1) // 2
+    return group[a] if a == b else jnp.where(tp == 0, group[a], group[b])
+
+def stacked(head):
+    low = lanes(head.shape) < 64
+    zero = jnp.zeros_like(head)
+    return jnp.concatenate([jnp.where(low, head, zero), jnp.where(low, zero, head)], axis=0)
+
+def allowed_of(begin, row0, key0, rows, keys):
+    i = row0 + lax.broadcasted_iota(jnp.int32, (rows, keys), 0)
+    j = key0 + lax.broadcasted_iota(jnp.int32, (rows, keys), 1)
+    return (j <= i) & (j >= begin)
+
+def attention(micros, rows, nblk, q_ref, kvall_ref, begin_ref, wo_ref, ao_ref, pr_ref, part_ref):
+    t = lax.axis_index("ctx"); tp = lax.axis_index("tp")
+    w0 = window_start(t, nblk)
+    keys = nblk * rows
+    pairs = q_ref.shape[1] // 128
+    for m in range(micros):
+        sl = slice(m * rows, (m + 1) * rows)
+        ks, vs = heads_kv(kvall_ref, w0, nblk, m, rows)
+        ok = allowed_of(begin_ref[sl, :1], t * rows, w0 * rows, rows, keys)
+        for p in range(pairs):
+            kb = stacked(pick(ks, p, tp)); vb = stacked(pick(vs, p, tp))
+            s = nt(q_ref[sl, 128 * p:128 * (p + 1)], kb) * SCALE
+            halves = []
+            for h in range(2):
+                sh = jnp.where(ok, s[:, h * keys:(h + 1) * keys], MASKED)
+                e = jnp.exp(sh - jnp.max(sh, axis=-1, keepdims=True))
+                halves.append((e / jnp.sum(e, axis=-1, keepdims=True)).astype(B16))
+            pr = jnp.concatenate(halves, axis=1)
+            pr_ref[m * pairs + p] = pr
+            ao_ref[sl, 128 * p:128 * (p + 1)] = nn(pr, vb).astype(B16)
+    part_ref[...] = nt(ao_ref[...], wo_ref[...]).astype(B16)
+
+def feed(x_ref, p1_ref, r1_ref, gain_ref, wg_ref, wu_ref, wd_ref, hid_ref, n2_ref, gate_ref, up_ref, act_ref, part_ref):
+    hid = x_ref[...].astype(F32) + (p1_ref[...].astype(F32) + r1_ref[...].astype(F32))
+    hid_ref[...] = hid
+    n2 = (hid * rms(hid) * gain_ref[...]).astype(B16)
+    n2_ref[...] = n2
+    gate = nn(n2, wg_ref[...]); up = nn(n2, wu_ref[...])
+    gate_ref[...] = gate; up_ref[...] = up
+    act = (gate * jax.nn.sigmoid(gate) * up).astype(B16)
+    act_ref[...] = act
+    part_ref[...] = nt(act, wd_ref[...]).astype(B16)
+
+def feed_back(ct_ref, live_ref, gate_ref, up_ref, act_ref, n2_ref, wg_ref, wu_ref, wd_ref, g_ref, dpart_ref, gg_ref, gu_ref, gd_ref):
+    g = (ct_ref[...].astype(F32) * live_ref[:, :1]).astype(B16)
+    g_ref[...] = g
+    da = nn(g, wd_ref[...])
+    gate = gate_ref[...]; up = up_ref[...]
+    sg = jax.nn.sigmoid(gate)
+    dgate = (da * up * sg * (1.0 + gate * (1.0 - sg))).astype(B16)
+    dup = (da * (gate * sg)).astype(B16)
+    dpart_ref[...] = (nt(dgate, wg_ref[...]) + nt(dup, wu_ref[...])).astype(B16)
+    gd_ref[...] = tn(g, act_ref[...]).astype(B16)
+    gg_ref[...] = tn(n2_ref[...], dgate).astype(B16)
+    gu_ref[...] = tn(n2_ref[...], dup).astype(B16)
+
+def attention_back(micros, rows, nblk, g_ref, p_ref, r_ref, hid_ref, gain_ref, q_ref, kvall_ref, wo_ref, ao_ref, pr_ref,
+                   dh_ref, go_ref, gain_out_ref, dq_ref, dkv_ref, do_ref):
+    t = lax.axis_index("ctx"); tp = lax.axis_index("tp")
+    w0 = window_start(t, nblk)
+    keys = nblk * rows
+    pairs = q_ref.shape[1] // 128
+    dn2 = p_ref[...].astype(F32) + r_ref[...].astype(F32)
+    hid = hid_ref[...]
+    r2 = rms(hid)
+    gain_out_ref[...] = jnp.broadcast_to(jnp.sum(dn2 * hid * r2, axis=0, keepdims=True), gain_out_ref.shape)
+    dh = g_ref[...].astype(F32) + norm_back(hid, r2, gain_ref[...], dn2)
+    dh_ref[...] = dh
+    db = dh.astype(B16)
+    go_ref[...] = tn(db, ao_ref[...]).astype(B16)
+    do_ref[...] = nn(db, wo_ref[...]).astype(B16)
+    dkv_ref[...] = jnp.zeros_like(dkv_ref)
+    for m in range(micros):
+        sl = slice(m * rows, (m + 1) * rows)
+        ks, vs = heads_kv(kvall_ref, w0, nblk, m, rows)
+        dks = [jnp.zeros((keys, 128), F32) for _ in range(3)]
+        dvs = [jnp.zeros((keys, 128), F32) for _ in range(3)]
+        for p in range(pairs):
+            kb = stacked(pick(ks, p, tp)); vb = stacked(pick(vs, p, tp))
+            qt = q_ref[sl, 128 * p:128 * (p + 1)]
+            dot_ = do_ref[sl, 128 * p:128 * (p + 1)]
+            pr = pr_ref[m * pairs + p]
+            dp = nt(dot_, vb)
+            halves = []
+            for h in range(2):
+                ph = pr[:, h * keys:(h + 1) * keys].astype(F32)
+                dph = dp[:, h * keys:(h + 1) * keys]
+                delta = jnp.sum(ph * dph, axis=-1, keepdims=True)
+                halves.append((ph * (dph - delta)).astype(B16))
+            ds = jnp.concatenate(halves, axis=1)
+            dq_ref[sl, 128 * p:128 * (p + 1)] = nn(ds, kb) * SCALE
+            dkb = tn(ds, qt) * SCALE
+            dvb = tn(pr, dot_)
+            low = lanes((keys, 128)) < 64
+            dk = jnp.where(low, dkb[:keys], dkb[keys:])
+            dv = jnp.where(low, dvb[:keys], dvb[keys:])
+            a, b = p // 2, (p + 1) // 2
+            if a == b:
+                dks[a] = dks[a] + dk; dvs[a] = dvs[a] + dv
+            else:
+                first = (tp == 0).astype(F32); second = 1.0 - first
+                dks[a] = dks[a] + dk * first; dvs[a] = dvs[a] + dv * first
+                dks[b] = dks[b] + dk * second; dvs[b] = dvs[b] + dv * second
+        low = lanes((keys, 128)) < 64
+        def full(v): return v + pltpu.roll(v, 64, 1)
+        dk0, dk1, dk2 = [full(v) for v in dks]
+        dv0, dv1, dv2 = [full(v) for v in dvs]
+        tiles = [jnp.where(low, dk0, dk1), jnp.where(low, dk2, dv2), jnp.where(low, dv0, dv1)]
+        for b in range(nblk):
+            for i in range(3):
+                dkv_ref[w0 + b, m * rows:(m + 1) * rows, 128 * i:128 * (i + 1)] = tiles[i][b * rows:(b + 1) * rows].astype(B16)
+
+def project_back(dq_ref, dkv_ref, cos_ref, sin_ref, n1_ref, a_ref, ga_ref, part_ref, dl_ref):
+    cos, sin = cos_ref[...], sin_ref[...]
+    qt = dq_ref.shape[1] // 128
+    for i in range(dl_ref.shape[1] // 128):
+        j = i - qt
+        tile = dq_ref[:, 128 * i:128 * (i + 1)] if j < 0 else dkv_ref[:, 128 * j:128 * (j + 1)].astype(F32)
+        if j <= 0: tile = rope_back(tile, cos, sin)
+        elif j == 1: tile = jnp.where(lanes(tile.shape) < 64, rope_back(tile, cos, sin), tile)
+        dl_ref[:, 128 * i:128 * (i + 1)] = tile.astype(B16)
+    dl = dl_ref[...]
+    part_ref[...] = nt(dl, a_ref[...]).astype(B16)
+    ga_ref[...] = tn(n1_ref[...], dl).astype(B16)
+
+def input_back(x_ref, p_ref, r_ref, dh_ref, gain_ref, dx_ref, gain_out_ref):
+    x = x_ref[...].astype(F32)
+    r1 = rms(x)
+    dn1 = p_ref[...].astype(F32) + r_ref[...].astype(F32)
+    gain_out_ref[...] = jnp.broadcast_to(jnp.sum(dn1 * x * r1, axis=0, keepdims=True), gain_out_ref.shape)
+    dx_ref[...] = dh_ref[...] + norm_back(x, r1, gain_ref[...], dn1)
+
+MESHT = pl.DeviceIdType.MESH
+
+def ag_body(nf, nz, chunks, n_mat, *refs):
+    shards = refs[:n_mat]; outs = refs[n_mat:2*n_mat]
+    send_sem, recv_sem, loc_sem = refs[2*n_mat:]
+    y = lax.axis_index("fsdp") if nf > 1 else 0
+    t = lax.axis_index("ctx")
+    z = t // 2; c = lax.rem(t, 2)
+    nc = 2 * nz
+    barrier = pltpu.get_barrier_semaphore()
+    def sig(**dev):
+        pl.semaphore_signal(barrier, inc=1, device_id=dev, device_id_type=MESHT)
+    @pl.when(z > 0)
+    def _(): sig(ctx=t - 2)
+    @pl.when(z < nz - 1)
+    def _(): sig(ctx=t + 2)
+    sig(ctx=t + 1 - 2 * c)
+    for p in range(1, nf): sig(fsdp=lax.rem(y + p, nf))
+    @pl.when((z > 0) & (z < nz - 1))
+    def _(): pl.semaphore_wait(barrier, 2 + nf)
+    @pl.when((z == 0) | (z == nz - 1))
+    def _(): pl.semaphore_wait(barrier, 1 + nf)
+
+    def shard(yy, zz, cc): return yy * nc + zz * 2 + cc
+    def at(k, s):
+        m, c0, cn = chunks[k]
+        return outs[m].at[s, :, pl.ds(c0, cn)]
+    def send(k, s, slot, dev, src=None):
+        pltpu.make_async_remote_copy(src_ref=at(k, s) if src is None else src, dst_ref=at(k, s),
+            send_sem=send_sem.at[k, slot], recv_sem=recv_sem.at[k, s], device_id=dev, device_id_type=MESHT).start()
+    def rcopy(k, s, slot):
+        return pltpu.make_async_remote_copy(src_ref=at(k, s), dst_ref=at(k, s),
+            send_sem=send_sem.at[k, slot], recv_sem=recv_sem.at[k, s], device_id=dict(ctx=t + 1 - 2 * c), device_id_type=MESHT)
+    nslots = [0]
+    def new(n=1):
+        v = nslots[0]; nslots[0] += n; return v
+    S_ownL, S_ownR, S_ownC = new(), new(), new()
+    S_ownY = new(nf - 1)
+    S_z = {}
+    for d in range(1, nz):
+        for side in (0, 1):
+            S_z[(side, d)] = (new(), new(), new(nf - 1))
+    S_yc = {(p, zz): new() for p in range(1, nf) for zz in range(nz)}
+    me = shard(y, z, c)
+    sib = dict(ctx=t + 1 - 2 * c)
+    def ydev(p): return dict(fsdp=lax.rem(y + p, nf))
+    K = len(chunks)
+    own_local = []
+    for k in range(K):
+        m, c0, cn = chunks[k]
+        src = shards[m].at[:, pl.ds(c0, cn)]
+        for p in range(1, nf): send(k, me, S_ownY + p - 1, ydev(p), src)
+        @pl.when(z > 0)
+        def _(): send(k, me, S_ownL, dict(ctx=t - 2), src)
+        @pl.when(z < nz - 1)
+        def _(): send(k, me, S_ownR, dict(ctx=t + 2), src)
+        send(k, me, S_ownC, sib, src)
+    for m in range(n_mat):
+        pltpu.make_async_copy(shards[m], outs[m].at[me], loc_sem.at[m]).start()
+    for k in range(K):
+        for d in range(1, nz):
+            for side in (0, 1):
+                ok = (z >= d) if side == 0 else (z + d <= nz - 1)
+                more = (z < nz - 1) if side == 0 else (z > 0)
+                zz = z - d if side == 0 else z + d
+                s = shard(y, zz, c)
+                sf, sc, sy = S_z[(side, d)]
+                @pl.when(ok)
+                def _():
+                    rcopy(k, s, 0).wait_recv()
+                    @pl.when(more)
+                    def _(): send(k, s, sf, dict(ctx=t + 2 if side == 0 else t - 2))
+                    for p in range(1, nf): send(k, s, sy + p - 1, ydev(p))
+                    send(k, s, sc, sib)
+        for p in range(1, nf):
+            yy = lax.rem(y + nf - p, nf)
+            for zz in range(nz):
+                s = shard(yy, zz, c)
+                rcopy(k, s, 0).wait_recv()
+                send(k, s, S_yc[(p, zz)], sib)
+    for k in range(K):
+        for yy in range(nf):
+            for zz in range(nz):
+                rcopy(k, shard(yy, zz, 1 - c), 0).wait_recv()
+        for p in range(1, nf): rcopy(k, me, S_ownY + p - 1).wait_send()
+        @pl.when(z > 0)
+        def _(): rcopy(k, me, S_ownL).wait_send()
+        @pl.when(z < nz - 1)
+        def _(): rcopy(k, me, S_ownR).wait_send()
+        rcopy(k, me, S_ownC).wait_send()
+        for d in range(1, nz):
+            for side in (0, 1):
+                ok = (z >= d) if side == 0 else (z + d <= nz - 1)
+                more = (z < nz - 1) if side == 0 else (z > 0)
+                sf, sc, sy = S_z[(side, d)]
+                @pl.when(ok)
+                def _():
+                    @pl.when(more)
+                    def _(): rcopy(k, me, sf).wait_send()
+                    for p in range(1, nf): rcopy(k, me, sy + p - 1).wait_send()
+                    rcopy(k, me, sc).wait_send()
+        for p in range(1, nf):
+            for zz in range(nz):
+                rcopy(k, me, S_yc[(p, zz)]).wait_send()
+    for m in range(n_mat):
+        pltpu.make_async_copy(shards[m], outs[m].at[me], loc_sem.at[m]).wait()
+
+def n_slots(nf, nz):
+    return 3 + (nf - 1) + 2 * (nz - 1) * (2 + nf - 1) + (nf - 1) * nz
+
+def all_gather_weights(nf, nz, shards, chunks, cid=0, space=pl.ANY, name="weights_gather"):
+    ns = nf * nz * 2
+    n = len(shards)
+    return pl.pallas_call(
+        functools.partial(ag_body, nf, nz, chunks, n),
+        out_shape=[jax.ShapeDtypeStruct((ns,) + s.shape, s.dtype) for s in shards],
+        in_specs=[pl.BlockSpec(memory_space=pltpu.VMEM)] * n,
+        out_specs=[pl.BlockSpec(memory_space=space)] * n,
+        scratch_shapes=[pltpu.SemaphoreType.DMA((len(chunks), n_slots(nf, nz))), pltpu.SemaphoreType.DMA((len(chunks), ns)), pltpu.SemaphoreType.DMA((n,))],
+        compiler_params=pltpu.CompilerParams(collective_id=cid, has_side_effects=True, vmem_limit_bytes=60 << 20),
+        name=name,
+    )(*shards)
+
+MESHT = pl.DeviceIdType.MESH
+
+def rs_body(nf, nz, chunks, n_mat, *refs):
+    nb = nf * nz
+    ins = refs[:n_mat]; outs = refs[n_mat:2*n_mat]
+    own = refs[2*n_mat:3*n_mat]; crecv = refs[3*n_mat:4*n_mat]; zrecv = refs[4*n_mat:5*n_mat]
+    rest = refs[5*n_mat:]
+    if nf > 1:
+        yrecv = rest[:n_mat]; rest = rest[n_mat:]
+    lsem, cs, cr, ys, yr, zs, zr = rest
+    y = lax.axis_index("fsdp") if nf > 1 else 0
+    t = lax.axis_index("ctx")
+    z = t // 2; c = lax.rem(t, 2)
+    sib = dict(ctx=t + 1 - 2 * c)
+    barrier = pltpu.get_barrier_semaphore()
+    pl.semaphore_signal(barrier, inc=1, device_id=sib, device_id_type=MESHT)
+    for p in range(1, nf):
+        pl.semaphore_signal(barrier, inc=1, device_id=dict(fsdp=lax.rem(y + p, nf)), device_id_type=MESHT)
+    def zdev(p): return lax.rem(z + p, nz)
+    for p in range(1, nz):
+        pl.semaphore_signal(barrier, inc=1, device_id=dict(ctx=zdev(p) * 2 + c), device_id_type=MESHT)
+    pl.semaphore_wait(barrier, nf + nz - 1)
+    def remote(src, dst, ss, rs, dev):
+        return pltpu.make_async_remote_copy(src_ref=src, dst_ref=dst, send_sem=ss, recv_sem=rs, device_id=dev, device_id_type=MESHT)
+    def ccopy(k):
+        m, c0, cn = chunks[k]
+        return remote(ins[m].at[:, 1 - c, :, pl.ds(c0, cn)], crecv[m].at[:, :, pl.ds(c0, cn)], cs.at[k], cr.at[k], sib)
+    def lcopy(k):
+        m, c0, cn = chunks[k]
+        return pltpu.make_async_copy(ins[m].at[:, c, :, pl.ds(c0, cn)], own[m].at[:, :, pl.ds(c0, cn)], lsem.at[k])
+    def ycopy(k, p):
+        m, c0, cn = chunks[k]
+        yy = lax.rem(y + p, nf)
+        return remote(own[m].at[pl.ds(yy * nz, nz), :, pl.ds(c0, cn)], yrecv[m].at[p - 1, :, :, pl.ds(c0, cn)], ys.at[k, p - 1], yr.at[k, p - 1], dict(fsdp=yy))
+    def zcopy(k, p):
+        m, c0, cn = chunks[k]
+        return remote(own[m].at[y * nz + zdev(p), :, pl.ds(c0, cn)], zrecv[m].at[p - 1, :, pl.ds(c0, cn)], zs.at[k, p - 1], zr.at[k, p - 1], dict(ctx=zdev(p) * 2 + c))
+    K = len(chunks)
+    for k in range(K):
+        ccopy(k).start()
+        lcopy(k).start()
+    def stage_core(k):
+        m, c0, cn = chunks[k]
+        lcopy(k).wait()
+        ccopy(k).wait_recv()
+        def add(b, _):
+            own[m][b, :, pl.ds(c0, cn)] = own[m][b, :, pl.ds(c0, cn)] + crecv[m][b, :, pl.ds(c0, cn)]
+            return _
+        lax.fori_loop(0, nb, add, 0)
+        for p in range(1, nf): ycopy(k, p).start()
+    def stage_y(k):
+        m, c0, cn = chunks[k]
+        for p in range(1, nf): ycopy(k, p).wait_recv()
+        if nf > 1:
+            def add(b, _):
+                acc = own[m][y * nz + b, :, pl.ds(c0, cn)].astype(jnp.float32)
+                for p in range(1, nf):
+                    acc = acc + yrecv[m][p - 1, b, :, pl.ds(c0, cn)].astype(jnp.float32)
+                own[m][y * nz + b, :, pl.ds(c0, cn)] = acc.astype(jnp.bfloat16)
+                return _
+            lax.fori_loop(0, nz, add, 0)
+        for p in range(1, nz): zcopy(k, p).start()
+    def stage_z(k):
+        m, c0, cn = chunks[k]
+        for p in range(1, nz): zcopy(k, p).wait_recv()
+        acc = own[m][y * nz + z, :, pl.ds(c0, cn)].astype(jnp.float32)
+        for p in range(1, nz):
+            acc = acc + zrecv[m][p - 1, :, pl.ds(c0, cn)].astype(jnp.float32)
+        outs[m][:, pl.ds(c0, cn)] = acc.astype(outs[m].dtype)
+    for s in range(K + 2):
+        if s < K: stage_core(s)
+        if 0 <= s - 1 < K: stage_y(s - 1)
+        if 0 <= s - 2 < K: stage_z(s - 2)
+    for k in range(K):
+        ccopy(k).wait_send()
+        for p in range(1, nf): ycopy(k, p).wait_send()
+        for p in range(1, nz): zcopy(k, p).wait_send()
+
+def reduce_scatter_blocks(nf, nz, mats, chunks, cid, out_dtype=jnp.float32, name="grads_scatter"):
+    n = len(mats); nb = nf * nz; K = len(chunks)
+    b16 = jnp.bfloat16
+    sh = [(m.shape[2], m.shape[3]) for m in mats]
+    scratch = [pltpu.VMEM((nb,) + s, b16) for s in sh] + [pltpu.VMEM((nb,) + s, b16) for s in sh] + [pltpu.VMEM((nz - 1,) + s, b16) for s in sh]
+    if nf > 1: scratch += [pltpu.VMEM((nf - 1, nz) + s, b16) for s in sh]
+    D = pltpu.SemaphoreType.DMA
+    scratch += [D((K,)), D((K,)), D((K,)), D((K, max(1, nf - 1))), D((K, max(1, nf - 1))), D((K, nz - 1)), D((K, nz - 1))]
+    return pl.pallas_call(
+        functools.partial(rs_body, nf, nz, chunks, n),
+        out_shape=[jax.ShapeDtypeStruct(s, out_dtype) for s in sh],
+        in_specs=[pl.BlockSpec(memory_space=pl.ANY)] * n,
+        out_specs=[pl.BlockSpec(memory_space=pltpu.VMEM)] * n,
+        scratch_shapes=scratch,
+        compiler_params=pltpu.CompilerParams(collective_id=cid, has_side_effects=True, vmem_limit_bytes=62 << 20),
+        name=name,
+    )(*mats)
+
+def swap_body(src_ref, dst_ref, ssem, rsem):
+    other = dict(tp=1 - lax.axis_index("tp"))
+    barrier = pltpu.get_barrier_semaphore()
+    pl.semaphore_signal(barrier, inc=1, device_id=other, device_id_type=MESHT)
+    pl.semaphore_wait(barrier, 1)
+    cp = pltpu.make_async_remote_copy(src_ref=src_ref, dst_ref=dst_ref, send_sem=ssem, recv_sem=rsem, device_id=other, device_id_type=MESHT)
+    cp.start()
+    cp.wait()
+
+def swap(v, cid):
+    return pl.pallas_call(
+        swap_body, out_shape=jax.ShapeDtypeStruct(v.shape, v.dtype),
+        in_specs=[pl.BlockSpec(memory_space=VMEM)], out_specs=pl.BlockSpec(memory_space=VMEM),
+        scratch_shapes=[pltpu.SemaphoreType.DMA, pltpu.SemaphoreType.DMA],
+        compiler_params=pltpu.CompilerParams(collective_id=cid, has_side_effects=True),
+        name="tp_swap_%d" % v.shape[0],
+    )(v)
+
+def run(body, outs, args, scratch=(), name=None):
+    return pl.pallas_call(
+        body, out_shape=[jax.ShapeDtypeStruct(s, d) for s, d in outs],
+        in_specs=[pl.BlockSpec(memory_space=VMEM)] * len(args),
+        out_specs=[pl.BlockSpec(memory_space=VMEM)] * len(outs),
+        scratch_shapes=list(scratch), name=name,
+        compiler_params=pltpu.CompilerParams(vmem_limit_bytes=60 << 20),
+    )(*args)
+
+def chunked(widths, width):
+    out = []
+    for m, w in enumerate(widths):
+        n = max(1, round(w / width))
+        c0 = 0
+        for i in range(n):
+            cn = (w // 128 // n + (1 if i < (w // 128) % n else 0)) * 128
+            out.append((m, c0, cn))
+            c0 += cn
+    return out
+
+def fast(tokens, lengths, attn_gain, w_query, w_key, w_value, w_out, ffn_gain, w_gate, w_up, w_down, cotangent):
+    micros, rows, width = tokens.shape
+    nf, nctx = lax.axis_size("fsdp"), lax.axis_size("ctx")
+    nz = nctx // 2
+    tp, t = lax.axis_index("tp"), lax.axis_index("ctx")
+    total = rows * nctx
+    nblk = total // 2 // rows + 1
+    shard = w_query.shape[0]
+    qw, ff = w_query.shape[1], w_gate.shape[1]
+    M = micros * rows
+    def kv3(w):
+        w = lax.dynamic_slice_in_dim(w, tp * 2 * HD, 3 * HD, axis=1)
+        return w[:, :2 * HD], w[:, 2 * HD:]
+    k01, k2 = kv3(w_key); v01, v2 = kv3(w_value)
+    sa = jnp.concatenate([w_query, k01, k2, v2, v01], axis=1)
+    gains = jnp.concatenate([jnp.broadcast_to(attn_gain[:, None], (shard, 64)), jnp.broadcast_to(ffn_gain[:, None], (shard, 64))], axis=1)
+    so = jnp.concatenate([w_out.T, gains], axis=1)
+    mats = [sa, so, w_gate, w_up, w_down.T]
+    widths = [m.shape[1] for m in mats]
+    full = all_gather_weights(nf, nz, mats, chunked(widths, 2000), cid=0)
+    A, O, G, U, Dn = [m.reshape(width, m.shape[2]) for m in full]
+    gain1 = O[:, qw].astype(F32)[None]
+    gain2 = O[:, qw + 64].astype(F32)[None]
+    O = O[:, :qw]
+    ends = jnp.cumsum(lengths[0], axis=1)
+    place = t * rows + jnp.arange(rows, dtype=jnp.int32)
+    begin = jnp.sum(jnp.where(place[None, :, None] >= ends[:, None, :], lengths[0][:, None, :], 0), axis=2).reshape(M, 1)
+    live = (jnp.tile(place, micros) < jnp.repeat(ends[:, -1], rows)).astype(F32)[:, None]
+    inverse = jnp.exp(jnp.arange(HD // 2, dtype=F32) * (-2.0 * math.log(THETA) / HD))
+    angle = (jnp.tile(place, micros)[:, None] - begin).astype(F32) * jnp.tile(inverse, 4)[None, :]
+    cos, sin = jnp.cos(angle), jnp.sin(angle)
+    begin = jnp.broadcast_to(begin, (M, 128))
+    live = jnp.broadcast_to(live, (M, 128))
+    x = tokens.reshape(M, width)
+    n1, q, kv = run(project, [((M, width), B16), ((M, qw), B16), ((M, 384), B16)], [x, gain1, A, cos, sin], name="project")
+    kvall, = all_gather_weights(1, nz, [kv], [(0, 0, 384)], cid=1, name="kv_gather")
+    pairs = qw // 128
+    keys = nblk * rows
+    ao, pr, part = run(functools.partial(attention, micros, rows, nblk),
+        [((M, qw), B16), ((micros * pairs, rows, 2 * keys), B16), ((M, width), B16)], [q, kvall, begin, O], name="attention")
+    peer = swap(part, 2)
+    hid, n2, gate, up, act, part2 = run(feed, [((M, width), F32), ((M, width), B16), ((M, ff), F32), ((M, ff), F32), ((M, ff), B16), ((M, width), B16)],
+        [x, part, peer, gain2, G, U, Dn], name="feed")
+    peer2 = swap(part2, 2)
+    output = (hid + (part2.astype(F32) + peer2.astype(F32))).astype(B16)
+    g, dpart, gg, gu, gd = run(feed_back, [((M, width), B16), ((M, width), B16), ((width, ff), B16), ((width, ff), B16), ((width, ff), B16)],
+        [cotangent.reshape(M, width), live, gate, up, act, n2, G, U, Dn], name="feed_back")
+    dpeer = swap(dpart, 2)
+    dh, go, gain2_part, dq, dkv = run(functools.partial(attention_back, micros, rows, nblk),
+        [((M, width), F32), ((width, qw), B16), ((8, width), F32), ((M, qw), F32), ((nctx, M, 384), B16)],
+        [g, dpart, dpeer, hid, gain2, q, kvall, O, ao, pr], scratch=[VMEM((M, qw), B16)], name="attention_back")
+    dkv_own, = reduce_scatter_blocks(1, nz, [dkv.reshape(nz, 2, M, 384)], [(0, 0, 384)], cid=3, out_dtype=F32, name="kv_scatter")
+    ga, npart = run(project_back, [((width, qw + 384), B16), ((M, width), B16)], [dq, dkv_own, cos, sin, n1, A], scratch=[VMEM((M, qw + 384), B16)], name="project_back")
+    npeer = swap(npart, 2)
+    dx, gain1_part = run(input_back, [((M, width), F32), ((8, width), F32)], [x, npart, npeer, dh, gain1], name="input_back")
+    gains_part = jnp.concatenate([jnp.broadcast_to(gain1_part[0].astype(B16)[:, None], (width, 64)), jnp.broadcast_to(gain2_part[0].astype(B16)[:, None], (width, 64))], axis=1)
+    go = jnp.concatenate([go, gains_part], axis=1)
+    grads = [m.reshape(nf * nz, 2, shard, m.shape[1]) for m in (gd, gg, gu, go, ga)]
+    rd, rg, ru, ro, ra = reduce_scatter_blocks(nf, nz, grads, chunked([m.shape[3] for m in grads], 1024), cid=4)
+    half = shard // 2
+    kvg = ra[:, qw:].reshape(2, half, 384)
+    mine = lax.dynamic_index_in_dim(kvg, tp, 0, keepdims=False)
+    theirs = swap(lax.dynamic_index_in_dim(kvg, 1 - tp, 0, keepdims=False), 5)
+    low, high = jnp.where(tp == 0, mine, theirs), jnp.where(tp == 0, theirs, mine)
+    def spread(lo, hi): return jnp.pad(lo, ((0, 0), (0, 128))) + jnp.pad(hi, ((0, 0), (128, 0)))
+    def ks(v): return v[:, :192]
+    def vs(v): return jnp.concatenate([v[:, 256:384], v[:, 192:256]], axis=1)
+    grad_key = spread(ks(low), ks(high))
+    grad_value = spread(vs(low), vs(high))
+    return (output.reshape(micros, rows, width), dx.reshape(micros, rows, width), ro[:, qw], ra[:, :qw], grad_key, grad_value,
+            ro[:, :qw].T, ro[:, qw + 64], rg, ru, rd.T)
+
+
 def solution(mesh):
     placed = (
         P(None, ("fsdp", "ctx"), None),
@@ -446,8 +982,12 @@
         P("tp", ("fsdp", "ctx")),
         P(None, ("fsdp", "ctx"), None),
     )
+    def chosen(*args):
+        fits = args[3].shape[0] % 16 == 0 and mesh.shape["tp"] == 2 and mesh.shape["ctx"] % 2 == 0
+        return (fast if fits else shards)(*args)
+
     return jax.shard_map(
-        shards,
+        chosen,
         mesh=mesh,
         in_specs=placed,
         out_specs=(

time: 1500 us -> 456 us (0.30)
  waiting for transfers between devices: 1030 us -> 0 us
  Pallas kernels: 0 us -> 423 us
  blocking collectives: 208 us -> 0 us
  matrix products: 127 us -> 0 us
  other arithmetic: 46.4 us -> 11.8 us
  local copies, waits for them, and re-layouts: 52.9 us -> 19 us
  between operations: 17.3 us -> 0.86 us
    reduce_scatter x5 -> x0, waiting for transfers between devices: 481 us -> none  [the longest x1 114 us: reduce_grads(): lax.psum_scatter(main_part[6], ('fsdp', 'ctx'), scatter_dimension=1, tile...]
    pallas_call x0 -> x16, Pallas kernels: none -> 423 us  [the longest x2 142 us: reduce_scatter_blocks(): pl.pallas_call(functools.partial(rs_body, nf, nz, chunks, n), out_shape=[...]
    unnamed x25 -> x0, waiting for transfers between devices: 331 us -> none
    all_gather x5 -> x0, waiting for transfers between devices: 146 us -> none  [the longest x1 52 us: collect(): lax.all_gather(w_gate, ('fsdp', 'ctx'), axis=0, tiled=True)]
    dot_general x64 -> x0, matrix products: 127 us -> none  [the longest x2 9.74 us: shards(): jnp.dot(active, down_full, preferred_element_type=f32).astype(jnp.bfloat16)]
    all_gather x6 -> x0, blocking collectives: 110 us -> none  [the longest x2 30 us: shards(): lax.all_gather(key_rot, 'ctx', axis=0, tiled=True)]
    unnamed x2 -> x0, blocking collectives: 97.8 us -> none
    psum x3 -> x0, waiting for transfers between devices: 70.9 us -> none  [the longest x1 39.6 us: shards(): lax.psum(jnp.dot(attended_low, out_full, preferred_element_type=f32).asty...]
  transfers between devices with their start and end apart: 19 -> 0, of which waited for: 17 -> 0; matrix products, arithmetic and copies ran while one was open for 11% -> 0% of each run, Pallas kernels for 0% -> 0%
where the time goes in v1:
time: 456 us; the launch traced here: 455 us
  Pallas kernels  423 us (93%)
  local copies, waits for them, and re-layouts  19 us (4%)
  other arithmetic  11.8 us (3%)
    pallas_call x2, Pallas kernels, reduce_scatter_blocks(): pl.pallas_call(functools.partial(rs_body, nf, nz, chunks, n), out_shape=[...  142 us
    pallas_call x2, Pallas kernels, all_gather_weights(): pl.pallas_call(functools.partial(ag_body, nf, nz, chunks, n), out_shape=[...  136 us
    pallas_call x5, Pallas kernels, swap(): pl.pallas_call(swap_body, out_shape=jax.ShapeDtypeStruct(v.shape, v.dtype...  79.5 us
    pallas_call x7, Pallas kernels, run(): pl.pallas_call(body, out_shape=[jax.ShapeDtypeStruct(s, d) for s, d in ou...  65.9 us

profile of v1, /device:TPU:0, one launch (start us, length us, event | category | flops | bytes accessed | tf_op | source)
XLA Modules:
  0.0 454.5 jit_solution(5398343647366188310)
XLA Ops:
  2.6 1.6 pad_maximum_fusion.1.refs_0_
  5.7 1.6 pad_maximum_fusion.2.refs_1_
  7.3 114.6 %weights_gather.1 = (bf16[16,80,1024]{2,1,0:T(8,128)(2,1)}, bf16[16,80,768]{2,1,0:T(8,128)(2,1)}, bf16[16,80,1792]{2,1,0:T(8,128)(2,1)}, bf16[16,80,1792]{2,1,0:T(8,128)(2,1)}, bf16[16,80,1792]{2,1,0:T(8,128)(2,1)}) custom-call(bf16[80,1024]{1,0:T(8,128)(2,1)} %pad_maximum_fusion.1.refs_0_, bf16[80,768]{1,0:T(8,128)(2,1)} %pad_maximum_fusion.2.refs_1_, ...), custom_call_target="tpu_custom_call" | custom-call | tf_op jit(solution)/shard_map/weights_gather/pallas_call | solution.py:753
  121.9 1.5 convert_reduce_fusion
  125.8 4.1 project.1
  130.0 21.1 %kv_gather.1.kvall_ref = bf16[8,256,384]{2,1,0:T(8,128)(2,1)} custom-call(bf16[256,384]{1,0:T(8,128)(2,1)} %get-tuple-element.50.refs_0_), custom_call_target="tpu_custom_call" | custom-call | tf_op jit(solution)/shard_map/kv_gather/pallas_call | solution.py:753
  153.2 9.1 %attention.1 = (bf16[256,640]{1,0:T(8,128)(2,1)}, bf16[10,128,1280]{2,1,0:T(8,128)(2,1)}, bf16[256,1280]{1,0:T(8,128)(2,1)}) custom-call(bf16[256,640]{1,0:T(8,128)(2,1)} %get-tuple-element.49.q_ref, bf16[8,256,384]{2,1,0:T(8,128)(2,1)} %kv_gather.1.kvall_ref, s32[256,128]{1,0:T(8,128)} %broadcast_in_dim.30.begin_ref, bf16[1280,640]{1,0:T(8,128)(2,1)} %slice.83.wo_ref), custom_call_target="tpu_custom_call" | custom-call | tf_op jit(solution)/shard_map/attention/pallas_call | solution.py:878
  162.3 19.0 %tp_swap_256.4.r1_ref = bf16[256,1280]{1,0:T(8,128)(2,1)} custom-call(bf16[256,1280]{1,0:T(8,128)(2,1)} %get-tuple-element.51.src_ref.p1_ref), custom_call_target="tpu_custom_call" | custom-call | tf_op jit(solution)/shard_map/tp_swap_256/pallas_call | solution.py:869
  181.9 10.6 %feed.1 = (f32[256,1280]{1,0:T(8,128)}, bf16[256,1280]{1,0:T(8,128)(2,1)}, f32[256,1792]{1,0:T(8,128)}, f32[256,1792]{1,0:T(8,128)}, bf16[256,1792]{1,0:T(8,128)(2,1)}, /*index=5*/bf16[256,1280]{1,0:T(8,128)(2,1)}) custom-call(bf16[256,1280]{1,0:T(8,128)(2,1)} %bitcast.46, bf16[256,1280]{1,0:T(8,128)(2,1)} %get-tuple-element.51.src_ref.p1_ref, ...), custom_call_target="tpu_custom_call" | custom-call | tf_op jit(solution)/shard_map/feed/pallas_call | solution.py:878
  192.5 18.2 %tp_swap_256.5 = bf16[256,1280]{1,0:T(8,128)(2,1)} custom-call(bf16[256,1280]{1,0:T(8,128)(2,1)} %get-tuple-element.56.src_ref), custom_call_target="tpu_custom_call" | custom-call | tf_op jit(solution)/shard_map/tp_swap_256/pallas_call | solution.py:869
  210.7 2.4 add_convert_fusion
  214.1 18.4 %feed_back.1 = (bf16[256,1280]{1,0:T(8,128)(2,1)}, bf16[256,1280]{1,0:T(8,128)(2,1)}, bf16[1280,1792]{1,0:T(8,128)(2,1)}, bf16[1280,1792]{1,0:T(8,128)(2,1)}, bf16[1280,1792]{1,0:T(8,128)(2,1)}) custom-call(bf16[256,1280]{1,0:T(8,128)(2,1)} %bitcast.55, f32[256,128]{1,0:T(8,128)} %broadcast_in_dim.32.live_ref, f32[256,1792]{1,0:T(8,128)} %get-tuple-element.57.gate_ref, ...), custom_call_target="tpu_custom_call" | custom-call | tf_op jit(solution)/shard_map/feed_back/pallas_call | solution.py:878
  232.6 17.2 %tp_swap_256.6.r_ref = bf16[256,1280]{1,0:T(8,128)(2,1)} custom-call(bf16[256,1280]{1,0:T(8,128)(2,1)} %get-tuple-element.62.src_ref.p_ref), custom_call_target="tpu_custom_call" | custom-call | tf_op jit(solution)/shard_map/tp_swap_256/pallas_call | solution.py:869
  249.8 14.1 %attention_back.1 = (f32[256,1280]{1,0:T(8,128)}, bf16[1280,640]{1,0:T(8,128)(2,1)}, f32[8,1280]{1,0:T(8,128)}, f32[256,640]{1,0:T(8,128)}, bf16[8,256,384]{2,1,0:T(8,128)(2,1)}) custom-call(bf16[256,1280]{1,0:T(8,128)(2,1)} %get-tuple-element.61.g_ref, bf16[256,1280]{1,0:T(8,128)(2,1)} %get-tuple-element.62.src_ref.p_ref, ...), custom_call_target="tpu_custom_call" | custom-call | tf_op jit(solution)/shard_map/attention_back/pallas_call | solution.py:878
  263.9 18.7 %kv_scatter.1.dkv_ref = f32[256,384]{1,0:T(8,128)} custom-call(bf16[4,2,256,384]{3,2,1,0:T(8,128)(2,1)} %bitcast.54), custom_call_target="tpu_custom_call" | custom-call | tf_op jit(solution)/shard_map/kv_scatter/pallas_call | solution.py:849
  282.6 5.7 %project_back.1 = (bf16[1280,1024]{1,0:T(8,128)(2,1)}, bf16[256,1280]{1,0:T(8,128)(2,1)}) custom-call(f32[256,640]{1,0:T(8,128)} %get-tuple-element.65.dq_ref, f32[256,384]{1,0:T(8,128)} %kv_scatter.1.dkv_ref, f32[256,128]{1,0:T(8,128)} %get-tuple-element.90.cos_ref, f32[256,128]{1,0:T(8,128)} %get-tuple-element.89.sin_ref, ...), custom_call_target="tpu_custom_call" | custom-call | tf_op jit(solution)/shard_map/project_back/pallas_call | solution.py:878
  288.4 19.4 %tp_swap_256.7.r_ref = bf16[256,1280]{1,0:T(8,128)(2,1)} custom-call(bf16[256,1280]{1,0:T(8,128)(2,1)} %get-tuple-element.68.src_ref.p_ref), custom_call_target="tpu_custom_call" | custom-call | tf_op jit(solution)/shard_map/tp_swap_256/pallas_call | solution.py:869
  307.8 3.7 input_back.1
  313.6 1.5 pad_maximum_fusion
  315.2 123.0 %grads_scatter.1 = (f32[80,1792]{1,0:T(8,128)}, f32[80,1792]{1,0:T(8,128)}, f32[80,1792]{1,0:T(8,128)}, f32[80,768]{1,0:T(8,128)}, f32[80,1024]{1,0:T(8,128)}) custom-call(bf16[8,2,80,1792]{3,2,1,0:T(8,128)(2,1)} %bitcast.50, bf16[8,2,80,1792]{3,2,1,0:T(8,128)(2,1)} %bitcast.48, bf16[8,2,80,1792]{3,2,1,0:T(8,128)(2,1)} %bitcast.49, ...), custom_call_target="tpu_custom_call" | custom-call | tf_op jit(solution)/shard_map/grads_scatter/pallas_call | solution.py:849
  438.2 1.6 slice_reduce_fusion
  439.8 1.6 slice.72
  443.1 5.7 %tp_swap_40.1 = f32[40,384]{1,0:T(8,128)} custom-call(f32[40,384]{1,0:T(8,128)} %dynamic-slice_bitcast_fusion.src_ref), custom_call_target="tpu_custom_call" | custom-call | tf_op jit(solution)/shard_map/tp_swap_40/pallas_call | solution.py:869
  450.5 1.6 slice_bitcast_fusion
  (58 shorter events, 17.3 us)
Async XLA Ops:
  0.6 0.8 copy-start
  0.7 123.5 %copy-start.8 = (s32[1,2,3]{2,1,0:T(2,128)S(1)}, s32[1,2,3]{2,1,0:T(2,128)}, u32[]{:S(2)}) copy-start(s32[1,2,3]{2,1,0:T(2,128)} %param.13) | copy-start | bytes 76
  125.8 26.0 %copy-start.3 = (bf16[16,80,768]{2,1,0:T(8,128)(2,1)S(1)}, bf16[16,80,768]{2,1,0:T(8,128)(2,1)}, u32[]{:S(2)}) copy-start(bf16[16,80,768]{2,1,0:T(8,128)(2,1)} %get-tuple-element.47) | copy-start | bytes 5898244
  192.5 18.2 %copy-start.2 = (f32[256,1280]{1,0:T(8,128)S(1)}, f32[256,1280]{1,0:T(8,128)}, u32[]{:S(2)}) copy-start(f32[256,1280]{1,0:T(8,128)} %get-tuple-element.55.hid_ref) | copy-start | bytes 3932164
  307.8 5.8 %copy-start.4 = (bf16[1280,640]{1,0:T(8,128)(2,1)S(1)}, bf16[1280,640]{1,0:T(8,128)(2,1)}, u32[]{:S(2)}) copy-start(bf16[1280,640]{1,0:T(8,128)(2,1)} %get-tuple-element.74) | copy-start | bytes 4915204
  315.2 134.6 %copy-start.9 = (pred[320]{0:T(512)(128)(4,1)S(1)}, pred[320]{0:T(512)(128)(4,1)}, u32[]{:S(2)}) copy-start(pred[320]{0:T(512)(128)(4,1)} %constant.32.clone.1) | copy-start | bytes 964
  438.2 13.9 %copy-start.7 = (f32[80,1792]{1,0:T(8,128)S(1)}, f32[80,1792]{1,0:T(8,128)}, u32[]{:S(2)}) copy-start(f32[80,1792]{1,0:T(8,128)} %get-tuple-element.112) | copy-start | bytes 1720324
  438.2 14.7 %copy-start.6 = (f32[80,1792]{1,0:T(8,128)S(1)}, f32[80,1792]{1,0:T(8,128)}, u32[]{:S(2)}) copy-start(f32[80,1792]{1,0:T(8,128)} %get-tuple-element.113) | copy-start | bytes 1720324
  441.5 12.3 %copy-start.5 = (f32[80,1792]{1,0:T(8,128)S(1)}, f32[80,1792]{1,0:T(8,128)}, u32[]{:S(2)}) copy-start(f32[80,1792]{1,0:T(8,128)} %get-tuple-element.82) | copy-start | bytes 1720324
  449.8 4.7 %copy-start.1 = (bf16[80,320]{1,0:T(8,128)(2,1)S(1)}, bf16[80,320]{1,0:T(8,128)(2,1)}, u32[]{:S(2)}) copy-start(bf16[80,320]{1,0:T(8,128)(2,1)} %param.17) | copy-start | bytes 153604

commit v2 on v0

--- a/solution.py
+++ b/solution.py
@@ -1,8 +1,11 @@
+import functools
 import math
 
 import jax
 import jax.numpy as jnp
 from jax import lax
+from jax.experimental import pallas as pl
+from jax.experimental.pallas import tpu as pltpu
 from jax.sharding import PartitionSpec as P
 
 H = 20
@@ -431,6 +434,592 @@
     )
 
 
+F32 = jnp.float32
+B16 = jnp.bfloat16
+HD = 64
+EPSILON = 1e-05
+THETA = 10000.0
+MASKED = -1e30
+SCALE = 1.0 / math.sqrt(HD)
+VMEM = pltpu.VMEM
+
+def nn(a, b): return lax.dot_general(a, b, (((1,), (0,)), ((), ())), preferred_element_type=F32)
+def nt(a, b): return lax.dot_general(a, b, (((1,), (1,)), ((), ())), preferred_element_type=F32)
+def tn(a, b): return lax.dot_general(a, b, (((0,), (0,)), ((), ())), preferred_element_type=F32)
+
+def lanes(shape): return lax.broadcasted_iota(jnp.int32, shape, len(shape) - 1)
+
+def rope(t, cos, sin):
+    low = lanes(t.shape) % 64 < 32
+    rot = jnp.where(low, -pltpu.roll(t, 96, 1), pltpu.roll(t, 32, 1))
+    return t * cos + rot * sin
+
+def rope_back(u, cos, sin):
+    low = lanes(u.shape) % 64 < 32
+    us = u * sin
+    return u * cos + jnp.where(low, pltpu.roll(us, 96, 1), -pltpu.roll(us, 32, 1))
+
+def rms(v): return lax.rsqrt(jnp.mean(v * v, axis=-1, keepdims=True) + EPSILON)
+
+def norm_back(v, r, gain, d):
+    s = gain * d
+    return r * s - v * (r * r * r) * jnp.mean(s * v, axis=-1, keepdims=True)
+
+def doubled(tile, which):
+    t = tile.astype(F32)
+    r = pltpu.roll(t, 64, 1)
+    low = lanes(t.shape) < 64
+    return (jnp.where(low, t, r) if which == 0 else jnp.where(low, r, t)).astype(B16)
+
+def window_start(t, nblk): return jnp.maximum(t - nblk + 1, 0)
+
+def window(kvall_ref, w0, nblk, m, rows, tile):
+    return jnp.concatenate([kvall_ref[w0 + b, m * rows:(m + 1) * rows, 128 * tile:128 * (tile + 1)] for b in range(nblk)], axis=0)
+
+def heads_kv(kvall_ref, w0, nblk, m, rows):
+    k01 = window(kvall_ref, w0, nblk, m, rows, 0)
+    k2v2 = window(kvall_ref, w0, nblk, m, rows, 1)
+    v01 = window(kvall_ref, w0, nblk, m, rows, 2)
+    ks = [doubled(k01, 0), doubled(k01, 1), doubled(k2v2, 0)]
+    vs = [doubled(v01, 0), doubled(v01, 1), doubled(k2v2, 1)]
+    return ks, vs
+
+def pick(group, p, tp):
+    a, b = p // 2, (p + 1) // 2
+    return group[a] if a == b else jnp.where(tp == 0, group[a], group[b])
+
+def stacked(head):
+    low = lanes(head.shape) < 64
+    zero = jnp.zeros_like(head)
+    return jnp.concatenate([jnp.where(low, head, zero), jnp.where(low, zero, head)], axis=0)
+
+def allowed_of(begin, row0, key0, rows, keys):
+    i = row0 + lax.broadcasted_iota(jnp.int32, (rows, keys), 0)
+    j = key0 + lax.broadcasted_iota(jnp.int32, (rows, keys), 1)
+    return (j <= i) & (j >= begin)
+
+MESHT = pl.DeviceIdType.MESH
+
+def n_slots(nf, nz):
+    return 3 + (nf - 1) + 2 * (nz - 1) * (2 + nf - 1) + (nf - 1) * nz
+
+def swap_body(src_ref, dst_ref, ssem, rsem):
+    other = dict(tp=1 - lax.axis_index("tp"))
+    barrier = pltpu.get_barrier_semaphore()
+    pl.semaphore_signal(barrier, inc=1, device_id=other, device_id_type=MESHT)
+    pl.semaphore_wait(barrier, 1)
+    cp = pltpu.make_async_remote_copy(src_ref=src_ref, dst_ref=dst_ref, send_sem=ssem, recv_sem=rsem, device_id=other, device_id_type=MESHT)
+    cp.start()
+    cp.wait()
+
+def swap(v, cid):
+    return pl.pallas_call(
+        swap_body, out_shape=jax.ShapeDtypeStruct(v.shape, v.dtype),
+        in_specs=[pl.BlockSpec(memory_space=VMEM)], out_specs=pl.BlockSpec(memory_space=VMEM),
+        scratch_shapes=[pltpu.SemaphoreType.DMA, pltpu.SemaphoreType.DMA],
+        compiler_params=pltpu.CompilerParams(collective_id=cid, has_side_effects=True),
+        name="tp_swap_%d" % v.shape[0],
+    )(v)
+
+def greet(t, z, c, nz, y, nf, all_z):
+    barrier = pltpu.get_barrier_semaphore()
+    def sig(**dev):
+        pl.semaphore_signal(barrier, inc=1, device_id=dev, device_id_type=MESHT)
+    sig(ctx=t + 1 - 2 * c)
+    sig(tp=1 - lax.axis_index("tp"))
+    for p in range(1, nf): sig(fsdp=lax.rem(y + p, nf))
+    if all_z:
+        for p in range(1, nz): sig(ctx=lax.rem(z + p, nz) * 2 + c)
+        pl.semaphore_wait(barrier, nf + nz)
+        return
+    @pl.when(z > 0)
+    def _(): sig(ctx=t - 2)
+    @pl.when(z < nz - 1)
+    def _(): sig(ctx=t + 2)
+    @pl.when((z > 0) & (z < nz - 1))
+    def _(): pl.semaphore_wait(barrier, 3 + nf)
+    @pl.when((z == 0) | (z == nz - 1))
+    def _(): pl.semaphore_wait(barrier, 2 + nf)
+
+class Gather:
+    def __init__(self, nf, nz, at, own_src, send_sem, recv_sem):
+        self.nf, self.nz, self.at, self.own_src, self.ss, self.rs = nf, nz, at, own_src, send_sem, recv_sem
+        self.y = lax.axis_index("fsdp") if nf > 1 else 0
+        self.t = lax.axis_index("ctx")
+        self.z, self.c = self.t // 2, lax.rem(self.t, 2)
+        self.sib = dict(ctx=self.t + 1 - 2 * self.c)
+        self.me = self.shard(self.y, self.z, self.c)
+        count = [0]
+        def new(n=1):
+            count[0] += n
+            return count[0] - n
+        self.ownL, self.ownR, self.ownC, self.ownY = new(), new(), new(), new(nf - 1)
+        self.zs = {(side, d): (new(), new(), new(nf - 1)) for d in range(1, nz) for side in (0, 1)}
+        self.yc = {(p, zz): new() for p in range(1, nf) for zz in range(nz)}
+
+    def shard(self, yy, zz, cc): return yy * self.nz * 2 + zz * 2 + cc
+    def ydev(self, p): return dict(fsdp=lax.rem(self.y + p, self.nf))
+    def copy(self, k, s, slot, dev, src=None):
+        return pltpu.make_async_remote_copy(src_ref=self.at(k, s) if src is None else src, dst_ref=self.at(k, s),
+            send_sem=self.ss.at[k, slot], recv_sem=self.rs.at[k, s], device_id=dev, device_id_type=MESHT)
+    def send(self, *a): self.copy(*a).start()
+    def got(self, k, s): self.copy(k, s, 0, self.sib).wait_recv()
+    def sent(self, k, slot): self.copy(k, self.me, slot, self.sib).wait_send()
+    def when_z(self, side, d):
+        z, nz = self.z, self.nz
+        return ((z >= d), (z < nz - 1), z - d, self.t + 2) if side == 0 else ((z + d <= nz - 1), (z > 0), z + d, self.t - 2)
+
+    def own(self, k):
+        src = self.own_src(k)
+        for p in range(1, self.nf): self.send(k, self.me, self.ownY + p - 1, self.ydev(p), src)
+        @pl.when(self.z > 0)
+        def _(): self.send(k, self.me, self.ownL, dict(ctx=self.t - 2), src)
+        @pl.when(self.z < self.nz - 1)
+        def _(): self.send(k, self.me, self.ownR, dict(ctx=self.t + 2), src)
+        self.send(k, self.me, self.ownC, self.sib, src)
+
+    def zstep(self, k, d, side):
+        ok, more, zz, far = self.when_z(side, d)
+        s = self.shard(self.y, zz, self.c)
+        sf, sc, sy = self.zs[(side, d)]
+        @pl.when(ok)
+        def _():
+            self.got(k, s)
+            if d < self.nz - 1:
+                @pl.when(more)
+                def _(): self.send(k, s, sf, dict(ctx=far))
+            for p in range(1, self.nf): self.send(k, s, sy + p - 1, self.ydev(p))
+            self.send(k, s, sc, self.sib)
+
+    def ystep(self, k, p, zz):
+        s = self.shard(lax.rem(self.y + self.nf - p, self.nf), zz, self.c)
+        self.got(k, s)
+        self.send(k, s, self.yc[(p, zz)], self.sib)
+
+    def Z(self, k): return [functools.partial(self.zstep, k, d, side) for d in range(1, self.nz) for side in (0, 1)]
+    def Zd(self, k, d): return [functools.partial(self.zstep, k, d, side) for side in (0, 1)]
+    def Y(self, k): return [functools.partial(self.ystep, k, p, zz) for p in range(1, self.nf) for zz in range(self.nz)]
+
+    def arrived(self, k):
+        for yy in range(self.nf):
+            for zz in range(self.nz):
+                self.got(k, self.shard(yy, zz, 1 - self.c))
+
+    def drain(self, k):
+        for p in range(1, self.nf): self.sent(k, self.ownY + p - 1)
+        @pl.when(self.z > 0)
+        def _(): self.sent(k, self.ownL)
+        @pl.when(self.z < self.nz - 1)
+        def _(): self.sent(k, self.ownR)
+        self.sent(k, self.ownC)
+        for d in range(1, self.nz):
+            for side in (0, 1):
+                ok, more, _zz, _far = self.when_z(side, d)
+                sf, sc, sy = self.zs[(side, d)]
+                @pl.when(ok)
+                def _():
+                    if d < self.nz - 1:
+                        @pl.when(more)
+                        def _(): self.sent(k, sf)
+                    for p in range(1, self.nf): self.sent(k, sy + p - 1)
+                    self.sent(k, sc)
+        for v in self.yc.values(): self.sent(k, v)
+
+def emit(*lists):
+    for steps in lists:
+        for step in steps: step()
+
+def front(nf, nz, micros, rows, nblk, chunks, shard,
+          x_ref, cos_ref, sin_ref, begin_ref, sa, so, sg, su, sd,
+          A, O, G, U, D, kvall_ref, n1_ref, q_ref, ao_ref, pr_ref, part_ref, peer_ref, gains_ref,
+          xr_ref, wss, wrs, lsem, kss, krs, pss, prs):
+    t = lax.axis_index("ctx"); tp = lax.axis_index("tp")
+    y = lax.axis_index("fsdp") if nf > 1 else 0
+    z, c = t // 2, lax.rem(t, 2)
+    greet(t, z, c, nz, y, nf, False)
+    shards, outs = [sa, so, sg, su, sd], [A, O, G, U, D]
+    def at(k, s):
+        m, c0, cn = chunks[k]
+        return outs[m].at[pl.ds(pl.multiple_of(s * shard, 16), shard), pl.ds(c0, cn)]
+    def own_src(k):
+        m, c0, cn = chunks[k]
+        return shards[m].at[:, pl.ds(c0, cn)]
+    W = Gather(nf, nz, at, own_src, wss, wrs)
+    V = Gather(1, nz, lambda k, s: kvall_ref.at[s], lambda k: kvall_ref.at[t], kss, krs)
+    K = len(chunks)
+    def local(m):
+        return pltpu.make_async_copy(shards[m], outs[m].at[pl.ds(pl.multiple_of(W.me * shard, 16), shard), :], lsem.at[m])
+    other = dict(tp=1 - tp)
+    def swap_part(m):
+        sl = pl.ds(m * rows, rows)
+        return pltpu.make_async_remote_copy(src_ref=part_ref.at[sl, :], dst_ref=peer_ref.at[sl, :], send_sem=pss.at[m], recv_sem=prs.at[m], device_id=other, device_id_type=MESHT)
+    for k in range(3): W.own(k)
+    for m in range(5): local(m).start()
+    x = x_ref[...].astype(F32)
+    xr_ref[...] = x * rms(x)
+    emit(W.Z(0))
+    W.own(3)
+    emit(W.Z(1), W.Y(0), W.Z(2), W.Y(1))
+    local(0).wait()
+    W.arrived(0); W.arrived(1)
+    qw = q_ref.shape[1]
+    sel = (lax.broadcasted_iota(jnp.int32, (8, 128), 1) == jnp.where(lax.broadcasted_iota(jnp.int32, (8, 128), 0) < 4, 0, 64)).astype(B16)
+    gains = nt(sel, A[:, qw + 384:qw + 512])
+    gains_ref[...] = gains
+    n1_ref[...] = (xr_ref[...] * gains[0:1, :]).astype(B16)
+    cos, sin = cos_ref[...], sin_ref[...]
+    lin = nn(n1_ref[...], A[:, qw:qw + 384])
+    low = lanes((lin.shape[0], 128)) < 64
+    mid = lin[:, 128:256]
+    kvall_ref[t, :, 0:128] = rope(lin[:, :128], cos, sin).astype(B16)
+    kvall_ref[t, :, 128:256] = jnp.where(low, rope(mid, cos, sin), mid).astype(B16)
+    kvall_ref[t, :, 256:384] = lin[:, 256:384].astype(B16)
+    z3, y2 = W.Z(3), W.Y(2)
+    emit(z3[:1])
+    V.own(0)
+    emit(z3[1:2])
+    lin = nn(n1_ref[...], A[:, :qw])
+    for i in range(qw // 128):
+        q_ref[:, 128 * i:128 * (i + 1)] = rope(lin[:, 128 * i:128 * (i + 1)], cos, sin).astype(B16)
+    W.own(4)
+    emit(z3[2:], V.Zd(0, 1), y2)
+    W.own(5)
+    z4 = W.Z(4)
+    emit(z4[:4])
+    for d in range(2, nz): emit(V.Zd(0, d), z4[2 * d:2 * d + 2])
+    emit(W.Y(3))
+    V.arrived(0)
+    local(1).wait()
+    W.arrived(2)
+    W.own(6)
+    pump = W.Z(5) + W.Y(4) + [functools.partial(W.own, 7)] + W.Z(6)
+    w0 = window_start(t, nblk)
+    keys = nblk * rows
+    pairs = qw // 128
+    done = 0
+    for m in range(micros):
+        sl = slice(m * rows, (m + 1) * rows)
+        ks, vs = heads_kv(kvall_ref, w0, nblk, m, rows)
+        ok = allowed_of(begin_ref[sl, :1], t * rows, w0 * rows, rows, keys)
+        for p in range(pairs):
+            kb = stacked(pick(ks, p, tp)); vb = stacked(pick(vs, p, tp))
+            s = nt(q_ref[sl, 128 * p:128 * (p + 1)], kb) * SCALE
+            halves = []
+            for h in range(2):
+                sh = jnp.where(ok, s[:, h * keys:(h + 1) * keys], MASKED)
+                e = jnp.exp(sh - jnp.max(sh, axis=-1, keepdims=True))
+                halves.append((e / jnp.sum(e, axis=-1, keepdims=True)).astype(B16))
+            pr = jnp.concatenate(halves, axis=1)
+            pr_ref[m * pairs + p] = pr
+            ao_ref[sl, 128 * p:128 * (p + 1)] = nn(pr, vb).astype(B16)
+            upto = len(pump) * (m * pairs + p + 1) // (micros * pairs)
+            emit(pump[done:upto])
+            done = upto
+        part_ref[sl, :] = nt(ao_ref[sl, :], O[...]).astype(B16)
+        swap_part(m).start()
+    emit(pump[done:])
+    W.own(8)
+    emit(W.Y(5), W.Z(7), W.Y(6), W.Z(8), W.Y(7), W.Y(8))
+    for k in range(3, K): W.arrived(k)
+    for m in range(2, 5): local(m).wait()
+    for m in range(micros): swap_part(m).wait()
+    for k in range(K): W.drain(k)
+    V.drain(0)
+
+def middle(x_ref, p1_ref, r1_ref, gains_ref, G_hbm, U_hbm, D_hbm, ct_ref, live_ref,
+           hid_ref, part_ref, g_ref, dpart_ref, gg_hbm, gu_hbm, gd_hbm,
+           G, U, D, gate_ref, up_ref, act_ref, n2_ref, gg, gu, gd, sem):
+    loads = [pltpu.make_async_copy(a, b, sem.at[i]) for i, (a, b) in enumerate(((G_hbm, G), (U_hbm, U), (D_hbm, D)))]
+    for cp in loads: cp.start()
+    hid = x_ref[...].astype(F32) + (p1_ref[...].astype(F32) + r1_ref[...].astype(F32))
+    hid_ref[...] = hid
+    n2_ref[...] = (hid * rms(hid) * gains_ref[4:5, :]).astype(B16)
+    g_ref[...] = (ct_ref[...].astype(F32) * live_ref[:, :1]).astype(B16)
+    loads[0].wait()
+    gate_ref[...] = nn(n2_ref[...], G[...])
+    loads[1].wait()
+    up_ref[...] = nn(n2_ref[...], U[...])
+    gate = gate_ref[...]
+    act_ref[...] = (gate * jax.nn.sigmoid(gate) * up_ref[...]).astype(B16)
+    stores = [pltpu.make_async_copy(b, a, sem.at[3 + i]) for i, (a, b) in enumerate(((gg_hbm, gg), (gu_hbm, gu), (gd_hbm, gd)))]
+    gd[...] = tn(g_ref[...], act_ref[...]).astype(B16)
+    stores[2].start()
+    loads[2].wait()
+    part_ref[...] = nt(act_ref[...], D[...]).astype(B16)
+    da = nn(g_ref[...], D[...])
+    gate = gate_ref[...]; up = up_ref[...]
+    sg = jax.nn.sigmoid(gate)
+    dgate = (da * up * sg * (1.0 + gate * (1.0 - sg))).astype(B16)
+    dup = (da * (gate * sg)).astype(B16)
+    gg[...] = tn(n2_ref[...], dgate).astype(B16)
+    stores[0].start()
+    gu[...] = tn(n2_ref[...], dup).astype(B16)
+    stores[1].start()
+    dpart_ref[...] = (nt(dgate, G[...]) + nt(dup, U[...])).astype(B16)
+    for cp in stores: cp.wait()
+
+def back(nf, nz, micros, rows, nblk, chunks, shard,
+         gd, gg, gu, g_ref, dpart_ref, part2_ref, hid_ref, gains_ref, q_ref, kvall_ref, O, A, ao_ref, pr_ref, n1_ref, cos_ref, sin_ref, x_ref,
+         rd, rg, ru, ro, ra, dx_ref, out_ref,
+         own_d, own_g, own_u, c_d, c_g, c_u, c_o, c_a, y_d, y_g, y_u, y_o, y_a, z_d, z_g, z_u, z_o, z_a,
+         go_ref, ga_ref, dh_ref, do_ref, dq_ref, dkv_ref, kc_ref, kz_ref, dl_ref, dpeer_ref, peer2_ref, npart_ref, npeer_ref,
+         lsem, cs, cr, ys, yr, zs, zr, kcs, kcr, kzs, kzr, ss, sr):
+    t = lax.axis_index("ctx"); tp = lax.axis_index("tp")
+    y = lax.axis_index("fsdp") if nf > 1 else 0
+    z, c = t // 2, lax.rem(t, 2)
+    nb = nf * nz
+    greet(t, z, c, nz, y, nf, True)
+    ins, outs = [gd, gg, gu, go_ref, ga_ref], [rd, rg, ru, ro, ra]
+    crecv, yrecv, zrecv = [c_d, c_g, c_u, c_o, c_a], [y_d, y_g, y_u, y_o, y_a], [z_d, z_g, z_u, z_o, z_a]
+    acc = [own_d, own_g, own_u, c_o, c_a]
+    sib, other = dict(ctx=t + 1 - 2 * c), dict(tp=1 - tp)
+    def zdev(p): return lax.rem(z + p, nz)
+    def remote(src, dst, s, r, dev):
+        return pltpu.make_async_remote_copy(src_ref=src, dst_ref=dst, send_sem=s, recv_sem=r, device_id=dev, device_id_type=MESHT)
+    def ccopy(k):
+        m, c0, cn = chunks[k]
+        return remote(ins[m].at[:, 1 - c, :, pl.ds(c0, cn)], crecv[m].at[:, :, pl.ds(c0, cn)], cs.at[k], cr.at[k], sib)
+    def lcopy(k):
+        m, c0, cn = chunks[k]
+        return pltpu.make_async_copy(ins[m].at[:, c, :, pl.ds(c0, cn)], acc[m].at[:, :, pl.ds(c0, cn)], lsem.at[k])
+    def ycopy(k, p):
+        m, c0, cn = chunks[k]
+        yy = lax.rem(y + p, nf)
+        return remote(acc[m].at[pl.ds(yy * nz, nz), :, pl.ds(c0, cn)], yrecv[m].at[p - 1, :, :, pl.ds(c0, cn)], ys.at[k, p - 1], yr.at[k, p - 1], dict(fsdp=yy))
+    def zcopy(k, p):
+        m, c0, cn = chunks[k]
+        return remote(acc[m].at[y * nz + zdev(p), :, pl.ds(c0, cn)], zrecv[m].at[p - 1, :, pl.ds(c0, cn)], zs.at[k, p - 1], zr.at[k, p - 1], dict(ctx=zdev(p) * 2 + c))
+    def stage_core(k):
+        m, c0, cn = chunks[k]
+        cols = pl.ds(c0, cn)
+        if m < 3: lcopy(k).wait()
+        ccopy(k).wait_recv()
+        def add(b, _):
+            first = acc[m][b, :, cols] if m < 3 else ins[m][b, c, :, cols]
+            acc[m][b, :, cols] = first + crecv[m][b, :, cols]
+            return _
+        lax.fori_loop(0, nb, add, 0)
+        for p in range(1, nf): ycopy(k, p).start()
+    def stage_y(k):
+        m, c0, cn = chunks[k]
+        cols = pl.ds(c0, cn)
+        for p in range(1, nf): ycopy(k, p).wait_recv()
+        def add(b, _):
+            total = acc[m][y * nz + b, :, cols].astype(F32)
+            for p in range(1, nf): total = total + yrecv[m][p - 1, b, :, cols].astype(F32)
+            acc[m][y * nz + b, :, cols] = total.astype(B16)
+            return _
+        lax.fori_loop(0, nz, add, 0)
+        for p in range(1, nz): zcopy(k, p).start()
+    def stage_z(k):
+        m, c0, cn = chunks[k]
+        cols = pl.ds(c0, cn)
+        for p in range(1, nz): zcopy(k, p).wait_recv()
+        total = acc[m][y * nz + z, :, cols].astype(F32)
+        for p in range(1, nz): total = total + zrecv[m][p - 1, :, cols].astype(F32)
+        outs[m][:, cols] = total
+    dswap = remote(dpart_ref, dpeer_ref, ss.at[0], sr.at[0], other)
+    oswap = remote(part2_ref, peer2_ref, ss.at[1], sr.at[1], other)
+    nswap = remote(npart_ref, npeer_ref, ss.at[2], sr.at[2], other)
+    K = len(chunks)
+    dswap.start()
+    for k in range(6):
+        ccopy(k).start(); lcopy(k).start()
+    dkv_ref[...] = jnp.zeros_like(dkv_ref)
+    stage_core(0); stage_core(1); stage_core(2)
+    dswap.wait_recv()
+    oswap.start()
+    dn2 = dpart_ref[...].astype(F32) + dpeer_ref[...].astype(F32)
+    hid = hid_ref[...]
+    r2 = rms(hid)
+    gain2 = jnp.sum(dn2 * hid * r2, axis=0, keepdims=True)
+    dh = g_ref[...].astype(F32) + norm_back(hid, r2, gains_ref[4:5, :], dn2)
+    dh_ref[...] = dh
+    db = dh.astype(B16)
+    do_ref[...] = nn(db, O[...]).astype(B16)
+    stage_y(0)
+    go = tn(db, ao_ref[...]).astype(B16)
+    for s in range(2 * nb): go_ref[s // 2, s % 2] = go[s * shard:(s + 1) * shard]
+    stage_core(3)
+    ccopy(6).start()
+    w0 = window_start(t, nblk)
+    keys = nblk * rows
+    pairs = q_ref.shape[1] // 128
+    low = lanes((keys, 128)) < 64
+    pump = [functools.partial(stage_y, 1), functools.partial(stage_z, 0), functools.partial(stage_core, 4)]
+    for m in range(micros):
+        sl = slice(m * rows, (m + 1) * rows)
+        ks, vs = heads_kv(kvall_ref, w0, nblk, m, rows)
+        dks = [jnp.zeros((keys, 128), F32) for _ in range(3)]
+        dvs = [jnp.zeros((keys, 128), F32) for _ in range(3)]
+        for p in range(pairs):
+            kb = stacked(pick(ks, p, tp)); vb = stacked(pick(vs, p, tp))
+            qt = q_ref[sl, 128 * p:128 * (p + 1)]
+            dot_ = do_ref[sl, 128 * p:128 * (p + 1)]
+            pr = pr_ref[m * pairs + p]
+            dp = nt(dot_, vb)
+            halves = []
+            for h in range(2):
+                ph = pr[:, h * keys:(h + 1) * keys].astype(F32)
+                dph = dp[:, h * keys:(h + 1) * keys]
+                delta = jnp.sum(ph * dph, axis=-1, keepdims=True)
+                halves.append((ph * (dph - delta)).astype(B16))
+            ds = jnp.concatenate(halves, axis=1)
+            dq_ref[sl, 128 * p:128 * (p + 1)] = nn(ds, kb) * SCALE
+            dkb = tn(ds, qt) * SCALE
+            dvb = tn(pr, dot_)
+            dk = jnp.where(low, dkb[:keys], dkb[keys:])
+            dv = jnp.where(low, dvb[:keys], dvb[keys:])
+            a, b = p // 2, (p + 1) // 2
+            if a == b:
+                dks[a] = dks[a] + dk; dvs[a] = dvs[a] + dv
+            else:
+                first = (tp == 0).astype(F32); second = 1.0 - first
+                dks[a] = dks[a] + dk * first; dvs[a] = dvs[a] + dv * first
+                dks[b] = dks[b] + dk * second; dvs[b] = dvs[b] + dv * second
+        def full(v): return v + pltpu.roll(v, 64, 1)
+        dk0, dk1, dk2 = [full(v) for v in dks]
+        dv0, dv1, dv2 = [full(v) for v in dvs]
+        tiles = [jnp.where(low, dk0, dk1), jnp.where(low, dk2, dv2), jnp.where(low, dv0, dv1)]
+        for b in range(nblk):
+            at = w0 + b
+            for i in range(3):
+                dkv_ref[at // 2, lax.rem(at, 2), m * rows:(m + 1) * rows, 128 * i:128 * (i + 1)] = tiles[i][b * rows:(b + 1) * rows].astype(B16)
+        if m == 0: emit(pump[:2])
+    kvc = remote(dkv_ref.at[:, 1 - c], kc_ref, kcs.at[0], kcr.at[0], sib)
+    def kvz(p): return remote(kc_ref.at[zdev(p)], kz_ref.at[p - 1], kzs.at[p - 1], kzr.at[p - 1], dict(ctx=zdev(p) * 2 + c))
+    kvc.start()
+    emit(pump[2:])
+    kvc.wait_recv()
+    def add_kv(b, _):
+        kc_ref[b] = kc_ref[b] + dkv_ref[b, c]
+        return _
+    lax.fori_loop(0, nz, add_kv, 0)
+    for p in range(1, nz): kvz(p).start()
+    stage_y(2); stage_z(1); stage_core(5)
+    oswap.wait_recv()
+    out_ref[...] = (hid_ref[...] + (part2_ref[...].astype(F32) + peer2_ref[...].astype(F32))).astype(B16)
+    stage_y(3); stage_z(2)
+    for p in range(1, nz): kvz(p).wait_recv()
+    dkv = kc_ref[z].astype(F32)
+    for p in range(1, nz): dkv = dkv + kz_ref[p - 1].astype(F32)
+    cos, sin = cos_ref[...], sin_ref[...]
+    qw = q_ref.shape[1]
+    for i in range(qw // 128):
+        dl_ref[:, 128 * i:128 * (i + 1)] = rope_back(dq_ref[:, 128 * i:128 * (i + 1)], cos, sin).astype(B16)
+    mid = dkv[:, 128:256]
+    dl_ref[:, qw:qw + 128] = rope_back(dkv[:, :128], cos, sin).astype(B16)
+    dl_ref[:, qw + 128:qw + 256] = jnp.where(lanes(mid.shape) < 64, rope_back(mid, cos, sin), mid).astype(B16)
+    dl_ref[:, qw + 256:qw + 384] = dkv[:, 256:384].astype(B16)
+    npart_ref[...] = nt(dl_ref[...], A[:, :qw + 384]).astype(B16)
+    nswap.start()
+    stage_core(6)
+    ga = tn(n1_ref[...], dl_ref[...]).astype(B16)
+    for s in range(2 * nb): ga_ref[s // 2, s % 2, :, :qw + 384] = ga[s * shard:(s + 1) * shard]
+    ccopy(7).start()
+    stage_y(4); stage_z(3)
+    stage_core(7)
+    stage_y(5); stage_z(4)
+    nswap.wait_recv()
+    x = x_ref[...].astype(F32)
+    r1 = rms(x)
+    dn1 = npart_ref[...].astype(F32) + npeer_ref[...].astype(F32)
+    gain1 = jnp.sum(dn1 * x * r1, axis=0, keepdims=True)
+    both = jnp.where(lax.broadcasted_iota(jnp.int32, (8, x.shape[1]), 0) < 4, gain1, gain2).astype(B16)
+    sel = ((lanes((8, 128)) < 64) & (lax.broadcasted_iota(jnp.int32, (8, 128), 0) == 0)) | ((lanes((8, 128)) >= 64) & (lax.broadcasted_iota(jnp.int32, (8, 128), 0) == 4))
+    gcol = tn(both, sel.astype(B16)).astype(B16)
+    for s in range(2 * nb): ga_ref[s // 2, s % 2, :, qw + 384:qw + 512] = gcol[s * shard:(s + 1) * shard]
+    ccopy(8).start()
+    dx_ref[...] = dh_ref[...] + norm_back(x, r1, gains_ref[0:1, :], dn1)
+    stage_core(8)
+    stage_y(6); stage_z(5); stage_y(7); stage_z(6); stage_y(8); stage_z(7); stage_z(8)
+    for cp in (dswap, oswap, nswap, kvc): cp.wait_send()
+    for p in range(1, nz): kvz(p).wait_send()
+    for k in range(K):
+        ccopy(k).wait_send()
+        for p in range(1, nf): ycopy(k, p).wait_send()
+        for p in range(1, nz): zcopy(k, p).wait_send()
+
+def fast(tokens, lengths, attn_gain, w_query, w_key, w_value, w_out, ffn_gain, w_gate, w_up, w_down, cotangent):
+    micros, rows, width = tokens.shape
+    nf, nctx = lax.axis_size("fsdp"), lax.axis_size("ctx")
+    nz = nctx // 2
+    nb = nf * nz
+    tp, t = lax.axis_index("tp"), lax.axis_index("ctx")
+    total = rows * nctx
+    nblk = total // 2 // rows + 1
+    shard = w_query.shape[0]
+    qw, ff = w_query.shape[1], w_gate.shape[1]
+    M = micros * rows
+    def kv3(w):
+        w = lax.dynamic_slice_in_dim(w, tp * 2 * HD, 3 * HD, axis=1)
+        return w[:, :2 * HD], w[:, 2 * HD:]
+    k01, k2 = kv3(w_key); v01, v2 = kv3(w_value)
+    gains = [jnp.broadcast_to(v[:, None], (shard, 64)) for v in (attn_gain, ffn_gain)]
+    sa = jnp.concatenate([w_query, k01, k2, v2, v01] + gains, axis=1)
+    aw = qw + 512
+    ends = jnp.cumsum(lengths[0], axis=1)
+    place = t * rows + jnp.arange(rows, dtype=jnp.int32)
+    begin = jnp.sum(jnp.where(place[None, :, None] >= ends[:, None, :], lengths[0][:, None, :], 0), axis=2).reshape(M, 1)
+    live = (jnp.tile(place, micros) < jnp.repeat(ends[:, -1], rows)).astype(F32)[:, None]
+    inverse = jnp.exp(jnp.arange(HD // 2, dtype=F32) * (-2.0 * math.log(THETA) / HD))
+    angle = (jnp.tile(place, micros)[:, None] - begin).astype(F32) * jnp.tile(inverse, 4)[None, :]
+    cos, sin = jnp.cos(angle), jnp.sin(angle)
+    begin = jnp.broadcast_to(begin, (M, 128))
+    live = jnp.broadcast_to(live, (M, 128))
+    x = tokens.reshape(M, width)
+    pairs = qw // 128
+    keys = nblk * rows
+    half = ff // 2
+    S = pltpu.SemaphoreType.DMA
+    inv, ina = pl.BlockSpec(memory_space=VMEM), pl.BlockSpec(memory_space=pl.ANY)
+    ns = nb * 2
+    wide = [(m, h * half, half) for m in (2, 3, 4) for h in range(2)]
+    chunks = [(0, 0, qw), (0, qw, 512), (1, 0, qw)] + wide
+    outs = [((width, aw), B16), ((width, qw), B16), ((width, ff), B16), ((width, ff), B16), ((width, ff), B16), ((nctx, M, 384), B16),
+        ((M, width), B16), ((M, qw), B16), ((M, qw), B16), ((micros * pairs, rows, 2 * keys), B16), ((M, width), B16), ((M, width), B16), ((8, width), F32)]
+    A, O, G, U, Dn, kvall, n1, q, ao, pr, part, peer, gains = pl.pallas_call(
+        functools.partial(front, nf, nz, micros, rows, nblk, chunks, shard),
+        out_shape=[jax.ShapeDtypeStruct(s, d) for s, d in outs],
+        in_specs=[inv] * 9, out_specs=[inv, inv, ina, ina, ina] + [inv] * 8,
+        scratch_shapes=[VMEM((M, width), F32), S((9, n_slots(nf, nz))), S((9, ns)), S((5,)), S((1, n_slots(1, nz))), S((1, nctx)), S((micros,)), S((micros,))],
+        compiler_params=pltpu.CompilerParams(collective_id=0, has_side_effects=True, vmem_limit_bytes=60 << 20), name="front",
+    )(x, cos, sin, begin, sa, w_out.T, w_gate, w_up, w_down.T)
+    outs = [((M, width), F32), ((M, width), B16), ((M, width), B16), ((M, width), B16)] + [((width, ff), B16)] * 3
+    hid, part2, g, dpart, gg, gu, gd = pl.pallas_call(
+        middle, out_shape=[jax.ShapeDtypeStruct(s, d) for s, d in outs],
+        in_specs=[inv] * 4 + [ina] * 3 + [inv] * 2, out_specs=[inv] * 4 + [ina] * 3,
+        scratch_shapes=[VMEM((width, ff), B16)] * 3 + [VMEM((M, ff), F32)] * 2 + [VMEM((M, ff), B16), VMEM((M, width), B16)] + [VMEM((width, ff), B16)] * 3 + [S((6,))],
+        compiler_params=pltpu.CompilerParams(vmem_limit_bytes=60 << 20), name="middle",
+    )(x, part, peer, gains, G, U, Dn, cotangent.reshape(M, width), live)
+    chunks = [(m, h * half, half) for m in range(3) for h in range(2)] + [(3, 0, qw), (4, 0, qw), (4, qw, 512)]
+    wd = [ff, ff, ff, qw, aw]
+    K = len(chunks)
+    outs = [((shard, w), F32) for w in wd] + [((M, width), F32), ((M, width), B16)]
+    scratch = [VMEM((nb, shard, w), B16) for w in wd[:3]] + [VMEM((nb, shard, w), B16) for w in wd] + [VMEM((nf - 1, nz, shard, w), B16) for w in wd] + [VMEM((nz - 1, shard, w), B16) for w in wd]
+    scratch += [VMEM((nb, 2, shard, qw), B16), VMEM((nb, 2, shard, aw), B16), VMEM((M, width), F32), VMEM((M, qw), B16), VMEM((M, qw), F32), VMEM((nz, 2, M, 384), B16),
+        VMEM((nz, M, 384), B16), VMEM((nz - 1, M, 384), B16), VMEM((M, qw + 384), B16)] + [VMEM((M, width), B16)] * 4
+    scratch += [S((K,)), S((K,)), S((K,)), S((K, nf - 1)), S((K, nf - 1)), S((K, nz - 1)), S((K, nz - 1)), S((1,)), S((1,)), S((nz - 1,)), S((nz - 1,)), S((3,)), S((3,))]
+    rd, rg, ru, ro, ra, dx, output = pl.pallas_call(
+        functools.partial(back, nf, nz, micros, rows, nblk, chunks, shard),
+        out_shape=[jax.ShapeDtypeStruct(s, d) for s, d in outs],
+        in_specs=[ina] * 3 + [inv] * 15, out_specs=[inv] * 7, scratch_shapes=scratch,
+        compiler_params=pltpu.CompilerParams(collective_id=4, has_side_effects=True, vmem_limit_bytes=63 << 20), name="back",
+    )(*[m.reshape(nb, 2, shard, ff) for m in (gd, gg, gu)], g, dpart, part2, hid, gains, q, kvall, O, A, ao, pr, n1, cos, sin, x)
+    hs = shard // 2
+    kvg = ra[:, qw:qw + 384].reshape(2, hs, 384)
+    mine = lax.dynamic_index_in_dim(kvg, tp, 0, keepdims=False)
+    theirs = swap(lax.dynamic_index_in_dim(kvg, 1 - tp, 0, keepdims=False), 5)
+    low, high = jnp.where(tp == 0, mine, theirs), jnp.where(tp == 0, theirs, mine)
+    def spread(lo, hi): return jnp.pad(lo, ((0, 0), (0, 128))) + jnp.pad(hi, ((0, 0), (128, 0)))
+    def ks(v): return v[:, :192]
+    def vs(v): return jnp.concatenate([v[:, 256:384], v[:, 192:256]], axis=1)
+    grad_key = spread(ks(low), ks(high))
+    grad_value = spread(vs(low), vs(high))
+    return (output.reshape(micros, rows, width), dx.reshape(micros, rows, width), ra[:, qw + 384], ra[:, :qw], grad_key, grad_value,
+            ro.T, ra[:, qw + 448], rg, ru, rd.T)
+
+
 def solution(mesh):
     placed = (
         P(None, ("fsdp", "ctx"), None),
@@ -446,8 +1035,12 @@
         P("tp", ("fsdp", "ctx")),
         P(None, ("fsdp", "ctx"), None),
     )
+    def chosen(*args):
+        fits = args[3].shape[0] % 16 == 0 and mesh.shape["tp"] == 2 and mesh.shape["fsdp"] == 2 and mesh.shape["ctx"] % 2 == 0
+        return (fast if fits else shards)(*args)
+
     return jax.shard_map(
-        shards,
+        chosen,
         mesh=mesh,
         in_specs=placed,
         out_specs=(

time: 1500 us -> 328 us (0.22)
  waiting for transfers between devices: 1030 us -> 0 us
  Pallas kernels: 0 us -> 301 us
  blocking collectives: 208 us -> 0 us
  matrix products: 127 us -> 0 us
  other arithmetic: 46.4 us -> 3.78 us
  local copies, waits for them, and re-layouts: 52.9 us -> 19.6 us
  between operations: 17.3 us -> 0.97 us
    reduce_scatter x5 -> x0, waiting for transfers between devices: 481 us -> none  [the longest x1 114 us: reduce_grads(): lax.psum_scatter(main_part[6], ('fsdp', 'ctx'), scatter_dimension=1, tile...]
    unnamed x25 -> x0, waiting for transfers between devices: 331 us -> none
    pallas_call x0 -> x4, Pallas kernels: none -> 301 us  [the longest x1 145 us: fast(): pl.pallas_call(functools.partial(back, nf, nz, micros, rows, nblk, chunks...]
    all_gather x5 -> x0, waiting for transfers between devices: 146 us -> none  [the longest x1 52 us: collect(): lax.all_gather(w_gate, ('fsdp', 'ctx'), axis=0, tiled=True)]
    dot_general x64 -> x0, matrix products: 127 us -> none  [the longest x2 9.74 us: shards(): jnp.dot(active, down_full, preferred_element_type=f32).astype(jnp.bfloat16)]
    all_gather x6 -> x0, blocking collectives: 110 us -> none  [the longest x2 30 us: shards(): lax.all_gather(key_rot, 'ctx', axis=0, tiled=True)]
    unnamed x2 -> x0, blocking collectives: 97.8 us -> none
    psum x3 -> x0, waiting for transfers between devices: 70.9 us -> none  [the longest x1 39.6 us: shards(): lax.psum(jnp.dot(attended_low, out_full, preferred_element_type=f32).asty...]
  transfers between devices with their start and end apart: 19 -> 0, of which waited for: 17 -> 0; matrix products, arithmetic and copies ran while one was open for 11% -> 0% of each run, Pallas kernels for 0% -> 0%
where the time goes in v2:
time: 328 us; the launch traced here: 325 us
  Pallas kernels  301 us (92%)
  local copies, waits for them, and re-layouts  19.6 us (6%)
  other arithmetic  3.78 us (1%)
    pallas_call x1, Pallas kernels, fast(): pl.pallas_call(functools.partial(back, nf, nz, micros, rows, nblk, chunks...  145 us
    pallas_call x1, Pallas kernels, fast(): pl.pallas_call(functools.partial(front, nf, nz, micros, rows, nblk, chunk...  122 us
    pallas_call x1, Pallas kernels, fast(): pl.pallas_call(middle, out_shape=[jax.ShapeDtypeStruct(s, d) for s, d in...  28.7 us
    unnamed x20, local copies, waits for them, and re-layouts  7.04 us

profile of v2, /device:TPU:0, one launch (start us, length us, event | category | flops | bytes accessed | tf_op | source)
XLA Modules:
  0.0 325.3 jit_solution(17730519533975067482)
XLA Ops:
  0.7 0.8 copy-done
  1.6 0.8 constant_dynamic-slice_fusion
  2.4 0.9 constant_dynamic-slice_fusion.1
  3.2 0.7 broadcast_in_dim.25
  4.0 0.7 broadcast_in_dim.44
  4.7 1.7 concatenate.9.sa
  6.4 0.8 reduce_window_sum.11
  7.3 0.8 copy.24
  8.3 1.2 multiply_sine_fusion
  9.5 0.8 broadcast_in_dim.24.begin_ref
  10.3 121.7 %front.1 = (bf16[1280,1152]{1,0:T(8,128)(2,1)}, bf16[1280,640]{1,0:T(8,128)(2,1)}, bf16[1280,1792]{1,0:T(8,128)(2,1)}, bf16[1280,1792]{1,0:T(8,128)(2,1)}, bf16[...) custom-call(bf16[256,1280]{1,0:T(8,128)(2,1)} %bitcast.27, ...), custom_call_target="tpu_custom_call" | custom-call | tf_op jit(solution)/shard_map/front/pallas_call | solution.py:981
  132.3 0.8 broadcast_in_dim.46.live_ref
  133.0 28.7 %middle.1 = (f32[256,1280]{1,0:T(8,128)}, bf16[256,1280]{1,0:T(8,128)(2,1)}, bf16[256,1280]{1,0:T(8,128)(2,1)}, bf16[256,1280]{1,0:T(8,128)(2,1)}, bf16[1280,179...) custom-call(bf16[256,1280]{1,0:T(8,128)(2,1)} %bitcast.28, ...), custom_call_target="tpu_custom_call" | custom-call | tf_op jit(solution)/shard_map/middle/pallas_call | solution.py:989
  161.8 144.8 %back.1 = (f32[80,1792]{1,0:T(8,128)}, f32[80,1792]{1,0:T(8,128)}, f32[80,1792]{1,0:T(8,128)}, f32[80,640]{1,0:T(8,128)}, f32[80,1152]{1,0:T(8,128)}, /*index=5*/f32[256,1280]{1,0:T(8,128)}, bf16[256,1280]{1,0:T(8,128)(2,1)}) custom-call(bf16[8,2,80,1792]{3,2,1,0:T(8,128)(2,1)} %bitcast.32, bf16[8,2,80,1792]{3,2,1,0:T(8,128)(2,1)} %bitcast.30, ...), custom_call_target="tpu_custom_call" | custom-call | tf_op jit(solution)/shard_map/back/pallas_call | solution.py:1003
  306.6 1.1 slice.48
  308.3 5.7 %tp_swap_40.1 = f32[40,384]{1,0:T(8,128)} custom-call(f32[40,384]{1,0:T(8,128)} %dynamic-slice_bitcast_fusion.src_ref), custom_call_target="tpu_custom_call" | custom-call | tf_op jit(solution)/shard_map/tp_swap_40/pallas_call | solution.py:516
  314.0 0.8 bitcast_select_fusion
  315.7 1.6 slice.47
  317.3 1.6 slice_reduce_fusion
  318.9 2.0 copy.31
  320.9 1.1 copy.32
  322.7 0.8 copy.34
  323.5 0.8 copy.35
  324.3 0.8 copy.36
  (31 shorter events, 2.8 us)
Async XLA Ops:
  0.6 0.8 copy-start
  161.7 153.3 %copy-start.6 = (pred[320]{0:T(512)(128)(4,1)S(1)}, pred[320]{0:T(512)(128)(4,1)}, u32[]{:S(2)}) copy-start(pred[320]{0:T(512)(128)(4,1)} %constant.32.clone.1) | copy-start | bytes 964
  306.6 14.3 %copy-start.1 = (f32[256,1280]{1,0:T(8,128)S(1)}, f32[256,1280]{1,0:T(8,128)}, u32[]{:S(2)}) copy-start(f32[256,1280]{1,0:T(8,128)} %get-tuple-element.59) | copy-start | bytes 3932164
  306.6 15.4 %copy-start.5 = (f32[80,640]{1,0:T(8,128)S(1)}, f32[80,640]{1,0:T(8,128)}, u32[]{:S(2)}) copy-start(f32[80,640]{1,0:T(8,128)} %get-tuple-element.61) | copy-start | bytes 614404
  306.6 16.1 %copy-start.4 = (f32[80,1792]{1,0:T(8,128)S(1)}, f32[80,1792]{1,0:T(8,128)}, u32[]{:S(2)}) copy-start(f32[80,1792]{1,0:T(8,128)} %get-tuple-element.92) | copy-start | bytes 1720324
  314.9 8.6 %copy-start.3 = (f32[80,1792]{1,0:T(8,128)S(1)}, f32[80,1792]{1,0:T(8,128)}, u32[]{:S(2)}) copy-start(f32[80,1792]{1,0:T(8,128)} %get-tuple-element.93) | copy-start | bytes 1720324
  318.9 5.4 %copy-start.2 = (f32[80,1792]{1,0:T(8,128)S(1)}, f32[80,1792]{1,0:T(8,128)}, u32[]{:S(2)}) copy-start(f32[80,1792]{1,0:T(8,128)} %get-tuple-element.64) | copy-start | bytes 1720324

commit v3 on v2

--- a/solution.py
+++ b/solution.py
@@ -542,6 +542,7 @@
     def _(): pl.semaphore_wait(barrier, 2 + nf)
 
 class Gather:
+    y_first = ()
     def __init__(self, nf, nz, at, own_src, send_sem, recv_sem):
         self.nf, self.nz, self.at, self.own_src, self.ss, self.rs = nf, nz, at, own_src, send_sem, recv_sem
         self.y = lax.axis_index("fsdp") if nf > 1 else 0
@@ -571,12 +572,15 @@
 
     def own(self, k):
         src = self.own_src(k)
-        for p in range(1, self.nf): self.send(k, self.me, self.ownY + p - 1, self.ydev(p), src)
+        if k not in self.y_first: self.own_y(k)
         @pl.when(self.z > 0)
         def _(): self.send(k, self.me, self.ownL, dict(ctx=self.t - 2), src)
         @pl.when(self.z < self.nz - 1)
         def _(): self.send(k, self.me, self.ownR, dict(ctx=self.t + 2), src)
         self.send(k, self.me, self.ownC, self.sib, src)
+
+    def own_y(self, k):
+        for p in range(1, self.nf): self.send(k, self.me, self.ownY + p - 1, self.ydev(p), self.own_src(k))
 
     def zstep(self, k, d, side):
         ok, more, zz, far = self.when_z(side, d)
@@ -596,8 +600,63 @@
         self.got(k, s)
         self.send(k, s, self.yc[(p, zz)], self.sib)
 
+    def to_z(self, k, s, slot):
+        @pl.when(self.z > 0)
+        def _(): self.send(k, s, slot, dict(ctx=self.t - 2))
+        @pl.when(self.z < self.nz - 1)
+        def _(): self.send(k, s, slot + 1, dict(ctx=self.t + 2))
+    def peer_slot(self, p): return 2 + self.nf + 3 * (p - 1)
+    def far_slot(self, p, d, side): return 2 + self.nf + 3 * (self.nf - 1) + 2 * ((p * (self.nz - 1) + d - 1) * 2 + side)
+    def peer(self, p): return lax.rem(self.y + p, self.nf)
+    def first_y(self, k):
+        for p in range(1, self.nf):
+            s = self.shard(self.peer(p), self.z, self.c)
+            self.got(k, s)
+            self.to_z(k, s, self.peer_slot(p))
+            self.send(k, s, self.peer_slot(p) + 2, self.sib)
+    def then_z(self, k, d):
+        for side in (0, 1):
+            ok, more, zz, far = self.when_z(side, d)
+            @pl.when(ok)
+            def _():
+                for p in range(self.nf):
+                    s = self.shard(self.peer(p), zz, self.c)
+                    f = self.far_slot(p, d, side)
+                    self.got(k, s)
+                    if d < self.nz - 1:
+                        @pl.when(more)
+                        def _(): self.send(k, s, f, dict(ctx=far))
+                    self.send(k, s, f + 1, self.sib)
+    def YZ(self, k): return [functools.partial(self.first_y, k)] + [functools.partial(self.then_z, k, d) for d in range(1, self.nz)]
+    def drain_yz(self, k):
+        for p in range(1, self.nf): self.sent(k, self.ownY + p - 1)
+        self.sent(k, self.ownC)
+        for p in range(1, self.nf): self.sent(k, self.peer_slot(p) + 2)
+        for edge, own, i in ((self.z > 0, self.ownL, 0), (self.z < self.nz - 1, self.ownR, 1)):
+            @pl.when(edge)
+            def _():
+                self.sent(k, own)
+                for p in range(1, self.nf): self.sent(k, self.peer_slot(p) + i)
+        for d in range(1, self.nz):
+            for side in (0, 1):
+                ok, more, _zz, _far = self.when_z(side, d)
+                @pl.when(ok)
+                def _():
+                    for p in range(self.nf):
+                        if d < self.nz - 1:
+                            @pl.when(more)
+                            def _(): self.sent(k, self.far_slot(p, d, side))
+                        self.sent(k, self.far_slot(p, d, side) + 1)
+
     def Z(self, k): return [functools.partial(self.zstep, k, d, side) for d in range(1, self.nz) for side in (0, 1)]
-    def Zd(self, k, d): return [functools.partial(self.zstep, k, d, side) for side in (0, 1)]
+    def hop(self, k, d):
+        if k in self.y_first:
+            if d == 1: self.first_y(k)
+            self.then_z(k, d)
+        else:
+            for side in (0, 1): self.zstep(k, d, side)
+    def last(self, k):
+        if k not in self.y_first: emit(self.Y(k))
     def Y(self, k): return [functools.partial(self.ystep, k, p, zz) for p in range(1, self.nf) for zz in range(self.nz)]
 
     def arrived(self, k):
@@ -629,44 +688,125 @@
     for steps in lists:
         for step in steps: step()
 
+class KeysGather(Gather):
+    far = 2
+    def own(self):
+        @pl.when(self.z < self.nz - 1)
+        def _(): self.send(0, self.me, self.ownR, dict(ctx=self.t + 2))
+        self.send(0, self.me, self.ownC, self.sib)
+    def step(self, d):
+        s = self.shard(0, self.z - d, self.c)
+        sf, sc, _y = self.zs[(0, d)]
+        @pl.when(self.z >= d)
+        def _():
+            self.got(0, s)
+            if d < self.far:
+                @pl.when(self.z < self.nz - 1)
+                def _(): self.send(0, s, sf, dict(ctx=self.t + 2))
+            self.send(0, s, sc, self.sib)
+    def arrived(self):
+        for d in range(self.far + 1):
+            @pl.when(self.z >= d)
+            def _(): self.got(0, self.shard(0, self.z - d, 1 - self.c))
+    def drain(self):
+        @pl.when(self.z < self.nz - 1)
+        def _(): self.sent(0, self.ownR)
+        self.sent(0, self.ownC)
+        for d in range(1, self.far + 1):
+            sf, sc, _y = self.zs[(0, d)]
+            @pl.when(self.z >= d)
+            def _():
+                if d < self.far:
+                    @pl.when(self.z < self.nz - 1)
+                    def _(): self.sent(0, sf)
+                self.sent(0, sc)
+
+def kv_tile(tp, wk, wv):
+    n = wk.shape[1]
+    i, l = lax.broadcasted_iota(jnp.int32, (n, 384), 0), lax.broadcasted_iota(jnp.int32, (n, 384), 1)
+    first = tp * 2 * HD
+    ek = (i == first + l) & (l < 3 * HD)
+    ev = ((i == first + l - 4 * HD) & (l >= 4 * HD)) | ((i == first + l - HD) & (l >= 3 * HD) & (l < 4 * HD))
+    return nn(wk, ek.astype(F32).astype(B16)) + nn(wv, ev.astype(F32).astype(B16))
+
+def half_rows(first, second):
+    return jnp.where(lax.broadcasted_iota(jnp.int32, (8, first.shape[1]), 0) < 4, first, second)
+
+def half_select():
+    low = lanes((8, 128)) < 64
+    r = lax.broadcasted_iota(jnp.int32, (8, 128), 0)
+    return ((low & (r == 0)) | ((lanes((8, 128)) >= 64) & (r == 4))).astype(F32).astype(B16)
+
 def front(nf, nz, micros, rows, nblk, chunks, shard,
-          x_ref, cos_ref, sin_ref, begin_ref, sa, so, sg, su, sd,
-          A, O, G, U, D, kvall_ref, n1_ref, q_ref, ao_ref, pr_ref, part_ref, peer_ref, gains_ref,
-          xr_ref, wss, wrs, lsem, kss, krs, pss, prs):
+          x_hbm, ct_hbm, len_ref, g1_ref, g2_ref, wq, wk, wv, so, sg, su, sd,
+          A_hbm, O_hbm, kvall_hbm, n1_hbm, q_hbm, ao_hbm, pr_hbm, gains_hbm, cos_hbm, sin_hbm, g_hbm, hid_hbm, part2_hbm, dpart_hbm, gd_hbm, n2T_hbm, dgate_hbm, dup_hbm,
+          A, O, kvall_ref, n1_ref, q_ref, ao_ref, pr_ref, gains_ref, cos_ref, sin_ref, g_ref, hid_ref, part2_ref, dpart_ref, gT, n2T, G, U, D, gd, dgate_ref, dup_ref, part_ref, peer_ref, gate_ref, up_ref, act_ref, n2_ref, psum_ref, dsum_ref, begin_ref, skv, x_ref, ct_ref, xsem, wss, wrs, lsem, kss, krs, pss, prs, osem):
     t = lax.axis_index("ctx"); tp = lax.axis_index("tp")
     y = lax.axis_index("fsdp") if nf > 1 else 0
     z, c = t // 2, lax.rem(t, 2)
+    qw = q_ref.shape[1]
+    first = [pltpu.make_async_copy(a, b, xsem.at[i]) for i, (a, b) in enumerate(((ct_hbm, ct_ref), (x_hbm, x_ref)))]
+    for cp in first: cp.start()
     greet(t, z, c, nz, y, nf, False)
-    shards, outs = [sa, so, sg, su, sd], [A, O, G, U, D]
+    shards, outs = [None, so, sg, su, sd], [A, O, G, U, D]
     def at(k, s):
         m, c0, cn = chunks[k]
         return outs[m].at[pl.ds(pl.multiple_of(s * shard, 16), shard), pl.ds(c0, cn)]
     def own_src(k):
         m, c0, cn = chunks[k]
-        return shards[m].at[:, pl.ds(c0, cn)]
+        return (wq, skv)[k] if m == 0 else shards[m].at[:, pl.ds(c0, cn)]
     W = Gather(nf, nz, at, own_src, wss, wrs)
-    V = Gather(1, nz, lambda k, s: kvall_ref.at[s], lambda k: kvall_ref.at[t], kss, krs)
+    W.y_first = (8,)
+    V = KeysGather(1, nz, lambda k, s: kvall_ref.at[s], None, kss, krs)
     K = len(chunks)
-    def local(m):
-        return pltpu.make_async_copy(shards[m], outs[m].at[pl.ds(pl.multiple_of(W.me * shard, 16), shard), :], lsem.at[m])
+    def local(k):
+        return pltpu.make_async_copy(own_src(k), at(k, W.me), lsem.at[k])
     other = dict(tp=1 - tp)
     def swap_part(m):
         sl = pl.ds(m * rows, rows)
         return pltpu.make_async_remote_copy(src_ref=part_ref.at[sl, :], dst_ref=peer_ref.at[sl, :], send_sem=pss.at[m], recv_sem=prs.at[m], device_id=other, device_id_type=MESHT)
-    for k in range(3): W.own(k)
-    for m in range(5): local(m).start()
+    saved = []
+    def save(a, b):
+        saved.append(pltpu.make_async_copy(a, b, osem.at[len(saved)]))
+        saved[-1].start()
+    W.own(0)
+    skv[:, :384] = kv_tile(tp, wk[...], wv[...]).astype(B16)
+    skv[:, 384:] = tn(half_rows(g1_ref[...].astype(F32), g2_ref[...].astype(F32)).astype(B16), half_select()).astype(B16)
+    for b in range(2 * nz):
+        @pl.when((b // 2 > z) | (b // 2 < z - V.far))
+        def _(): kvall_ref[b] = jnp.zeros(kvall_ref.shape[1:], B16)
+    W.own(1); W.own(2)
+    for k in W.y_first: W.own_y(k)
+    for k in range(K): local(k).start()
+    for cp in first: cp.wait()
+    place = t * rows + lax.broadcasted_iota(jnp.int32, (rows, 128), 0)
+    inverse = jnp.exp((lanes((1, 128)) % (HD // 2)).astype(F32) * (-2.0 * math.log(THETA) / HD))
+    for m in range(micros):
+        sl = slice(m * rows, (m + 1) * rows)
+        begin, end = jnp.zeros((rows, 128), jnp.int32), 0
+        for i in range(len_ref.shape[1]):
+            end = end + len_ref[m, i]
+            begin = begin + jnp.where(place >= end, len_ref[m, i], 0)
+        begin_ref[sl, :] = begin
+        angle = (place - begin).astype(F32) * inverse
+        cos_ref[sl, :] = jnp.cos(angle)
+        sin_ref[sl, :] = jnp.sin(angle)
+        live = jnp.where(place < end, 1.0, 0.0)
+        g_ref[sl, :] = (ct_ref[sl, :].astype(F32) * live[:, :1]).astype(B16)
     x = x_ref[...].astype(F32)
-    xr_ref[...] = x * rms(x)
-    emit(W.Z(0))
-    W.own(3)
-    emit(W.Z(1), W.Y(0), W.Z(2), W.Y(1))
-    local(0).wait()
+    hid_ref[...] = x * rms(x)
+    gT[...] = jnp.transpose(g_ref[...].astype(F32)).astype(B16)
+    save(g_ref, g_hbm); save(cos_ref, cos_hbm); save(sin_ref, sin_hbm)
+    hop, last = W.hop, W.last
+    hop(0, 1); W.own(3); hop(1, 1); hop(0, 2); hop(2, 1); hop(1, 2); hop(0, 3); last(0); hop(2, 2); hop(1, 3); last(1)
+    local(0).wait(); local(1).wait()
     W.arrived(0); W.arrived(1)
-    qw = q_ref.shape[1]
+    save(A, A_hbm)
     sel = (lax.broadcasted_iota(jnp.int32, (8, 128), 1) == jnp.where(lax.broadcasted_iota(jnp.int32, (8, 128), 0) < 4, 0, 64)).astype(B16)
     gains = nt(sel, A[:, qw + 384:qw + 512])
     gains_ref[...] = gains
-    n1_ref[...] = (xr_ref[...] * gains[0:1, :]).astype(B16)
+    save(gains_ref, gains_hbm)
+    n1_ref[...] = (hid_ref[...] * gains[0:1, :]).astype(B16)
     cos, sin = cos_ref[...], sin_ref[...]
     lin = nn(n1_ref[...], A[:, qw:qw + 384])
     low = lanes((lin.shape[0], 128)) < 64
@@ -674,25 +814,25 @@
     kvall_ref[t, :, 0:128] = rope(lin[:, :128], cos, sin).astype(B16)
     kvall_ref[t, :, 128:256] = jnp.where(low, rope(mid, cos, sin), mid).astype(B16)
     kvall_ref[t, :, 256:384] = lin[:, 256:384].astype(B16)
-    z3, y2 = W.Z(3), W.Y(2)
-    emit(z3[:1])
-    V.own(0)
-    emit(z3[1:2])
+    hop(3, 1)
+    V.own()
+    save(n1_ref, n1_hbm)
+    hop(2, 3)
     lin = nn(n1_ref[...], A[:, :qw])
     for i in range(qw // 128):
         q_ref[:, 128 * i:128 * (i + 1)] = rope(lin[:, 128 * i:128 * (i + 1)], cos, sin).astype(B16)
-    W.own(4)
-    emit(z3[2:], V.Zd(0, 1), y2)
-    W.own(5)
-    z4 = W.Z(4)
-    emit(z4[:4])
-    for d in range(2, nz): emit(V.Zd(0, d), z4[2 * d:2 * d + 2])
-    emit(W.Y(3))
-    V.arrived(0)
-    local(1).wait()
+    save(q_ref, q_hbm)
+    W.own(4); hop(3, 2); hop(4, 1); last(2)
+    V.step(1)
+    hop(3, 3); W.own(5); hop(4, 2); hop(5, 1); last(3)
+    V.step(2)
+    V.arrived()
+    save(kvall_ref, kvall_hbm)
+    local(2).wait()
     W.arrived(2)
-    W.own(6)
-    pump = W.Z(5) + W.Y(4) + [functools.partial(W.own, 7)] + W.Z(6)
+    save(O, O_hbm)
+    P_ = functools.partial
+    pump = [P_(W.own, 6), P_(hop, 4, 3), P_(hop, 5, 2), P_(hop, 6, 1), P_(W.own, 7), P_(hop, 5, 3), P_(hop, 6, 2), P_(hop, 7, 1)]
     w0 = window_start(t, nblk)
     keys = nblk * rows
     pairs = qw // 128
@@ -717,53 +857,86 @@
             done = upto
         part_ref[sl, :] = nt(ao_ref[sl, :], O[...]).astype(B16)
         swap_part(m).start()
-    emit(pump[done:])
-    W.own(8)
-    emit(W.Y(5), W.Z(7), W.Y(6), W.Z(8), W.Y(7), W.Y(8))
-    for k in range(3, K): W.arrived(k)
-    for m in range(2, 5): local(m).wait()
-    for m in range(micros): swap_part(m).wait()
-    for k in range(K): W.drain(k)
-    V.drain(0)
-
-def middle(x_ref, p1_ref, r1_ref, gains_ref, G_hbm, U_hbm, D_hbm, ct_ref, live_ref,
-           hid_ref, part_ref, g_ref, dpart_ref, gg_hbm, gu_hbm, gd_hbm,
-           G, U, D, gate_ref, up_ref, act_ref, n2_ref, gg, gu, gd, sem):
-    loads = [pltpu.make_async_copy(a, b, sem.at[i]) for i, (a, b) in enumerate(((G_hbm, G), (U_hbm, U), (D_hbm, D)))]
-    for cp in loads: cp.start()
-    hid = x_ref[...].astype(F32) + (p1_ref[...].astype(F32) + r1_ref[...].astype(F32))
+    save(ao_ref, ao_hbm); save(pr_ref, pr_hbm)
+    W.own(8); last(4); hop(6, 3); hop(7, 2); hop(8, 1); last(5); W.own(9)
+    W.arrived(3); W.arrived(4); W.arrived(5)
+    for k in (3, 4, 5): local(k).wait()
+    for m in range(micros): swap_part(m).wait_recv()
+    hid = x_ref[...].astype(F32) + (part_ref[...].astype(F32) + peer_ref[...].astype(F32))
     hid_ref[...] = hid
-    n2_ref[...] = (hid * rms(hid) * gains_ref[4:5, :]).astype(B16)
-    g_ref[...] = (ct_ref[...].astype(F32) * live_ref[:, :1]).astype(B16)
-    loads[0].wait()
-    gate_ref[...] = nn(n2_ref[...], G[...])
-    loads[1].wait()
-    up_ref[...] = nn(n2_ref[...], U[...])
-    gate = gate_ref[...]
-    act_ref[...] = (gate * jax.nn.sigmoid(gate) * up_ref[...]).astype(B16)
-    stores = [pltpu.make_async_copy(b, a, sem.at[3 + i]) for i, (a, b) in enumerate(((gg_hbm, gg), (gu_hbm, gu), (gd_hbm, gd)))]
-    gd[...] = tn(g_ref[...], act_ref[...]).astype(B16)
-    stores[2].start()
-    loads[2].wait()
-    part_ref[...] = nt(act_ref[...], D[...]).astype(B16)
-    da = nn(g_ref[...], D[...])
-    gate = gate_ref[...]; up = up_ref[...]
-    sg = jax.nn.sigmoid(gate)
-    dgate = (da * up * sg * (1.0 + gate * (1.0 - sg))).astype(B16)
-    dup = (da * (gate * sg)).astype(B16)
-    gg[...] = tn(n2_ref[...], dgate).astype(B16)
-    stores[0].start()
-    gu[...] = tn(n2_ref[...], dup).astype(B16)
-    stores[1].start()
-    dpart_ref[...] = (nt(dgate, G[...]) + nt(dup, U[...])).astype(B16)
-    for cp in stores: cp.wait()
+    n2 = hid * rms(hid) * gains[4:5, :]
+    n2_ref[...] = n2.astype(B16)
+    n2T[...] = jnp.transpose(n2).astype(B16)
+    save(hid_ref, hid_hbm)
+    save(n2T, n2T_hbm)
+    def forward(j, _):
+        cols = pl.ds(pl.multiple_of(j * 256, 256), 256)
+        gate = nn(n2_ref[...], G[:, cols])
+        up = nn(n2_ref[...], U[:, cols])
+        gate_ref[:, cols] = gate
+        up_ref[:, cols] = up
+        act = (gate * jax.nn.sigmoid(gate) * up).astype(B16)
+        act_ref[:, cols] = act
+        gd[:, cols] = nn(gT[...], act).astype(B16)
+        return _
+    def backward(j, _):
+        cols = pl.ds(pl.multiple_of(j * 256, 256), 256)
+        da = nn(g_ref[...], D[:, cols])
+        gate = gate_ref[:, cols]; up = up_ref[:, cols]
+        sg = jax.nn.sigmoid(gate)
+        dgate = (da * up * sg * (1.0 + gate * (1.0 - sg))).astype(B16)
+        dup = (da * (gate * sg)).astype(B16)
+        dgate_ref[:, cols] = dgate
+        dup_ref[:, cols] = dup
+        dsum_ref[...] += nt(dgate, G[:, cols]) + nt(dup, U[:, cols])
+        psum_ref[...] += nt(act_ref[:, cols], D[:, cols])
+        return _
+    def save_cols(a, b, c0, cn): save(a.at[:, pl.ds(c0, cn)], b.at[:, pl.ds(c0, cn)])
+    tiles = [c // 256 for _m, _c0, c in chunks]
+    ff = G.shape[1]
+    dsum_ref[...] = jnp.zeros_like(dsum_ref)
+    psum_ref[...] = jnp.zeros_like(psum_ref)
+    lax.fori_loop(0, tiles[3], forward, 0)
+    hop(7, 3); hop(8, 2); hop(9, 1); W.own(10); last(6)
+    W.arrived(6); local(6).wait()
+    lax.fori_loop(tiles[3], ff // 256, forward, 0)
+    save(gd, gd_hbm)
+    hop(8, 3); hop(9, 2); hop(10, 1)
+    def back_tiles(k):
+        last(k)
+        W.arrived(k); local(k).wait()
+        _m, c0, cn = chunks[k]
+        lax.fori_loop(c0 // 256, (c0 + cn) // 256, backward, 0)
+        save_cols(dgate_ref, dgate_hbm, c0, cn); save_cols(dup_ref, dup_hbm, c0, cn)
+    order = (8, 7) if 8 in W.y_first else (7, 8)
+    back_tiles(order[0])
+    hop(9, 3); hop(10, 2)
+    back_tiles(order[1])
+    hop(10, 3)
+    back_tiles(9); back_tiles(10)
+    dpart_ref[...] = dsum_ref[...].astype(B16)
+    save(dpart_ref, dpart_hbm)
+    part2_ref[...] = psum_ref[...].astype(B16)
+    save(part2_ref, part2_hbm)
+    for m in range(micros): swap_part(m).wait_send()
+    for k in range(K): (W.drain_yz if k in W.y_first else W.drain)(k)
+    V.drain()
+    for cp in saved: cp.wait()
 
 def back(nf, nz, micros, rows, nblk, chunks, shard,
-         gd, gg, gu, g_ref, dpart_ref, part2_ref, hid_ref, gains_ref, q_ref, kvall_ref, O, A, ao_ref, pr_ref, n1_ref, cos_ref, sin_ref, x_ref,
-         rd, rg, ru, ro, ra, dx_ref, out_ref,
-         own_d, own_g, own_u, c_d, c_g, c_u, c_o, c_a, y_d, y_g, y_u, y_o, y_a, z_d, z_g, z_u, z_o, z_a,
-         go_ref, ga_ref, dh_ref, do_ref, dq_ref, dkv_ref, kc_ref, kz_ref, dl_ref, dpeer_ref, peer2_ref, npart_ref, npeer_ref,
+         gd, *refs):
+    given, results, refs = refs[:18], refs[18:26], refs[26:]
+    back_body(nf, nz, micros, rows, nblk, chunks, shard, gd, given, results, *refs)
+
+def back_body(nf, nz, micros, rows, nblk, chunks, shard, gd, given,
+         results,
+         own_d, gg, gu, c_d, c_g, c_u, c_o, c_a, y_d, y_g, y_u, y_o, y_a, z_d, z_g, z_u, z_o, z_a,
+         zx_ref, go_ref, ga_ref, do_ref, dq_ref, dkv_ref, kc_ref, kz_ref, dl_ref, dpeer_ref, peer2_ref, npeer_ref,
+         g_ref, dpart_ref, part2_ref, hid_ref, gains_ref, q_ref, kvall_ref, O, A, ao_ref, pr_ref, n1_ref, cos_ref, sin_ref, x_ref, n2T, dgate_ref, dup_ref, gsem,
+         rd, rg, ru, ro, ra, dx_ref, kvx_ref, osem,
          lsem, cs, cr, ys, yr, zs, zr, kcs, kcr, kzs, kzr, ss, sr):
+    kz_ref[...] = jnp.zeros_like(kz_ref)
+    dh_ref, npart_ref, out_ref = dx_ref, dpart_ref, part2_ref
     t = lax.axis_index("ctx"); tp = lax.axis_index("tp")
     y = lax.axis_index("fsdp") if nf > 1 else 0
     z, c = t // 2, lax.rem(t, 2)
@@ -771,9 +944,11 @@
     greet(t, z, c, nz, y, nf, True)
     ins, outs = [gd, gg, gu, go_ref, ga_ref], [rd, rg, ru, ro, ra]
     crecv, yrecv, zrecv = [c_d, c_g, c_u, c_o, c_a], [y_d, y_g, y_u, y_o, y_a], [z_d, z_g, z_u, z_o, z_a]
-    acc = [own_d, own_g, own_u, c_o, c_a]
+    acc = [own_d, c_g, c_u, c_o, c_a]
     sib, other = dict(ctx=t + 1 - 2 * c), dict(tp=1 - tp)
-    def zdev(p): return lax.rem(z + p, nz)
+    inner = (z == 1) | (z == 2)
+    zin, zed = jnp.where(z < 2, 1, 2), jnp.where(z < 2, 0, 3)
+    zoi, zoe = 3 - zin, 3 - zed
     def remote(src, dst, s, r, dev):
         return pltpu.make_async_remote_copy(src_ref=src, dst_ref=dst, send_sem=s, recv_sem=r, device_id=dev, device_id_type=MESHT)
     def ccopy(k):
@@ -786,16 +961,17 @@
         m, c0, cn = chunks[k]
         yy = lax.rem(y + p, nf)
         return remote(acc[m].at[pl.ds(yy * nz, nz), :, pl.ds(c0, cn)], yrecv[m].at[p - 1, :, :, pl.ds(c0, cn)], ys.at[k, p - 1], yr.at[k, p - 1], dict(fsdp=yy))
-    def zcopy(k, p):
+    def zcopy(k, block, i, slot):
         m, c0, cn = chunks[k]
-        return remote(acc[m].at[y * nz + zdev(p), :, pl.ds(c0, cn)], zrecv[m].at[p - 1, :, pl.ds(c0, cn)], zs.at[k, p - 1], zr.at[k, p - 1], dict(ctx=zdev(p) * 2 + c))
+        return lambda dest: remote(acc[m].at[y * nz + block, :, pl.ds(c0, cn)], zrecv[m].at[slot, :, pl.ds(c0, cn)], zs.at[k, i], zr.at[k, slot], dict(ctx=dest * 2 + c))
+    def zgot(k, slot): zcopy(k, z, 0, slot)(zoi).wait_recv()
     def stage_core(k):
         m, c0, cn = chunks[k]
         cols = pl.ds(c0, cn)
-        if m < 3: lcopy(k).wait()
+        if m < 1: lcopy(k).wait()
         ccopy(k).wait_recv()
         def add(b, _):
-            first = acc[m][b, :, cols] if m < 3 else ins[m][b, c, :, cols]
+            first = acc[m][b, :, cols] if m < 1 else ins[m][b, c, :, cols]
             acc[m][b, :, cols] = first + crecv[m][b, :, cols]
             return _
         lax.fori_loop(0, nb, add, 0)
@@ -810,24 +986,115 @@
             acc[m][y * nz + b, :, cols] = total.astype(B16)
             return _
         lax.fori_loop(0, nz, add, 0)
-        for p in range(1, nz): zcopy(k, p).start()
+        @pl.when(inner)
+        def _(): zcopy(k, zed, 0, 0)(zed).start()
+        @pl.when(jnp.logical_not(inner))
+        def _():
+            zcopy(k, zoi, 0, 2)(zin).start()
+            zcopy(k, zoe, 1, 3)(zin).start()
+            zcopy(k, zin, 2, 0)(zin).start()
+    def stage_m(k):
+        m, c0, cn = chunks[k]
+        cols = pl.ds(c0, cn)
+        @pl.when(inner)
+        def _():
+            for block, slot in ((zoi, 2), (zoe, 3)):
+                zgot(k, slot)
+                acc[m][y * nz + block, :, cols] = (acc[m][y * nz + block, :, cols].astype(F32) + zrecv[m][slot, :, cols].astype(F32)).astype(B16)
+                zcopy(k, block, slot - 1, 1)(block).start()
     def stage_z(k):
         m, c0, cn = chunks[k]
         cols = pl.ds(c0, cn)
-        for p in range(1, nz): zcopy(k, p).wait_recv()
-        total = acc[m][y * nz + z, :, cols].astype(F32)
-        for p in range(1, nz): total = total + zrecv[m][p - 1, :, cols].astype(F32)
-        outs[m][:, cols] = total
-    dswap = remote(dpart_ref, dpeer_ref, ss.at[0], sr.at[0], other)
-    oswap = remote(part2_ref, peer2_ref, ss.at[1], sr.at[1], other)
+        zgot(k, 0); zgot(k, 1)
+        outs[m][:, cols] = acc[m][y * nz + z, :, cols].astype(F32) + zrecv[m][0, :, cols].astype(F32) + zrecv[m][1, :, cols].astype(F32)
+    def xcopy(q, block, i, slot):
+        m, c0, cn = chunks[0]
+        dst = zx_ref.at[slot] if q else zrecv[m].at[slot, :, pl.ds(c0, cn)]
+        return lambda dest: remote(acc[m].at[lax.rem(y + q, nf) * nz + block, :, pl.ds(c0, cn)], dst, zs.at[0, 3 * q + i], zr.at[0, 4 * q + slot], dict(ctx=dest * 2 + c))
+    def xgot(q, slot): xcopy(q, z, 0, slot)(zoi).wait_recv()
+    def xycopy():
+        m, c0, cn = chunks[0]
+        yy = lax.rem(y + 1, nf)
+        return remote(acc[m].at[yy * nz + z, :, pl.ds(c0, cn)], yrecv[m].at[0, 0, :, pl.ds(c0, cn)], ys.at[0, 0], yr.at[0, 0], dict(fsdp=yy))
+    def stage_xcore():
+        m, c0, cn = chunks[0]
+        cols = pl.ds(c0, cn)
+        lcopy(0).wait()
+        ccopy(0).wait_recv()
+        def add(b, _):
+            acc[m][b, :, cols] = acc[m][b, :, cols] + crecv[m][b, :, cols]
+            return _
+        lax.fori_loop(0, nb, add, 0)
+        @pl.when(inner)
+        def _():
+            for q in (1, 0): xcopy(q, zed, 0, 0)(zed).start()
+        @pl.when(jnp.logical_not(inner))
+        def _():
+            for q in (1, 0):
+                xcopy(q, zoi, 0, 2)(zin).start()
+                xcopy(q, zoe, 1, 3)(zin).start()
+                xcopy(q, zin, 2, 0)(zin).start()
+    def stage_xm():
+        m, c0, cn = chunks[0]
+        cols = pl.ds(c0, cn)
+        @pl.when(inner)
+        def _():
+            for q in (1, 0):
+                at = lax.rem(y + q, nf) * nz
+                for block, slot in ((zoi, 2), (zoe, 3)):
+                    xgot(q, slot)
+                    got = zx_ref[slot] if q else zrecv[m][slot, :, cols]
+                    acc[m][at + block, :, cols] = (acc[m][at + block, :, cols].astype(F32) + got.astype(F32)).astype(B16)
+                    xcopy(q, block, slot - 1, 1)(block).start()
+    def stage_xz():
+        m, c0, cn = chunks[0]
+        cols = pl.ds(c0, cn)
+        xgot(1, 0); xgot(1, 1)
+        at = lax.rem(y + 1, nf) * nz + z
+        acc[m][at, :, cols] = (acc[m][at, :, cols].astype(F32) + zx_ref[0].astype(F32) + zx_ref[1].astype(F32)).astype(B16)
+        xycopy().start()
+    def stage_xy():
+        m, c0, cn = chunks[0]
+        cols = pl.ds(c0, cn)
+        xgot(0, 0); xgot(0, 1)
+        total = acc[m][y * nz + z, :, cols].astype(F32) + zrecv[m][0, :, cols].astype(F32) + zrecv[m][1, :, cols].astype(F32)
+        xycopy().wait_recv()
+        outs[m][:, cols] = total + yrecv[m][0, 0, :, cols].astype(F32)
+    dswap = remote(given[1], dpeer_ref, ss.at[0], sr.at[0], other)
+    oswap = remote(given[2], peer2_ref, ss.at[1], sr.at[1], other)
     nswap = remote(npart_ref, npeer_ref, ss.at[2], sr.at[2], other)
     K = len(chunks)
+    held = (g_ref, dpart_ref, part2_ref, hid_ref, gains_ref, q_ref, kvall_ref, O, A, ao_ref, pr_ref, n1_ref, cos_ref, sin_ref, x_ref, n2T, dgate_ref, dup_ref)
+    loads = [pltpu.make_async_copy(a, b, gsem.at[i]) for i, (a, b) in enumerate(zip(given, held))]
+    def need(*which):
+        for i in which: loads[i].wait()
+    saves = [pltpu.make_async_copy(a, b, osem.at[i]) for i, (a, b) in enumerate(zip((rd, rg, ru, ro, ra, dx_ref, out_ref, kvx_ref), results))]
     dswap.start()
-    for k in range(6):
+    for k in (1, 0, 2):
         ccopy(k).start(); lcopy(k).start()
+    def weights(ref, d_ref):
+        def tile(j, _):
+            cols = pl.ds(pl.multiple_of(j * 256, 256), 256)
+            v = nn(n2T[...], d_ref[:, cols]).astype(B16)
+            for s in range(2 * nb): ref[s // 2, s % 2, :, cols] = v[s * shard:(s + 1) * shard]
+            return _
+        lax.fori_loop(0, d_ref.shape[1] // 256, tile, 0)
+    stage_core(1)
+    for i in (15, 16, 17): loads[i].start()
+    stage_xcore()
+    for i in (1, 3, 0, 4, 7, 9, 5, 6, 10, 2, 12, 13, 8, 11, 14): loads[i].start()
+    need(15, 16)
+    weights(gg, dgate_ref)
+    stage_core(2)
+    ccopy(3).start(); ccopy(4).start()
     dkv_ref[...] = jnp.zeros_like(dkv_ref)
-    stage_core(0); stage_core(1); stage_core(2)
+    need(17)
+    weights(gu, dup_ref)
+    stage_core(3)
+    for k in (5, 6, 7): ccopy(k).start()
+    stage_y(1)
     dswap.wait_recv()
+    need(0, 1, 3, 4, 7)
     oswap.start()
     dn2 = dpart_ref[...].astype(F32) + dpeer_ref[...].astype(F32)
     hid = hid_ref[...]
@@ -837,16 +1104,18 @@
     dh_ref[...] = dh
     db = dh.astype(B16)
     do_ref[...] = nn(db, O[...]).astype(B16)
-    stage_y(0)
+    stage_y(2)
+    need(9)
     go = tn(db, ao_ref[...]).astype(B16)
     for s in range(2 * nb): go_ref[s // 2, s % 2] = go[s * shard:(s + 1) * shard]
-    stage_core(3)
-    ccopy(6).start()
+    ccopy(8).start()
+    stage_core(4)
+    stage_xm()
+    need(5, 6, 10)
     w0 = window_start(t, nblk)
     keys = nblk * rows
     pairs = q_ref.shape[1] // 128
     low = lanes((keys, 128)) < 64
-    pump = [functools.partial(stage_y, 1), functools.partial(stage_z, 0), functools.partial(stage_core, 4)]
     for m in range(micros):
         sl = slice(m * rows, (m + 1) * rows)
         ks, vs = heads_kv(kvall_ref, w0, nblk, m, rows)
@@ -885,24 +1154,30 @@
             at = w0 + b
             for i in range(3):
                 dkv_ref[at // 2, lax.rem(at, 2), m * rows:(m + 1) * rows, 128 * i:128 * (i + 1)] = tiles[i][b * rows:(b + 1) * rows].astype(B16)
-        if m == 0: emit(pump[:2])
+        if m == 0: stage_m(1); stage_m(2); stage_z(1)
     kvc = remote(dkv_ref.at[:, 1 - c], kc_ref, kcs.at[0], kcr.at[0], sib)
-    def kvz(p): return remote(kc_ref.at[zdev(p)], kz_ref.at[p - 1], kzs.at[p - 1], kzr.at[p - 1], dict(ctx=zdev(p) * 2 + c))
+    def kvz(p): return remote(kc_ref.at[z - p], kz_ref.at[p - 1], kzs.at[p - 1], kzr.at[p - 1], dict(ctx=t - 2 * p))
+    def kv_each(act):
+        for p in range(1, 3):
+            @pl.when(z >= p)
+            def _(): act(kvz(p))
+    def kv_got():
+        for p in range(1, 3):
+            @pl.when(z + p < nz)
+            def _(): remote(kc_ref.at[z], kz_ref.at[p - 1], kzs.at[p - 1], kzr.at[p - 1], sib).wait_recv()
     kvc.start()
-    emit(pump[2:])
+    stage_y(3); stage_xz(); stage_core(5)
     kvc.wait_recv()
     def add_kv(b, _):
         kc_ref[b] = kc_ref[b] + dkv_ref[b, c]
         return _
     lax.fori_loop(0, nz, add_kv, 0)
-    for p in range(1, nz): kvz(p).start()
-    stage_y(2); stage_z(1); stage_core(5)
-    oswap.wait_recv()
-    out_ref[...] = (hid_ref[...] + (part2_ref[...].astype(F32) + peer2_ref[...].astype(F32))).astype(B16)
-    stage_y(3); stage_z(2)
-    for p in range(1, nz): kvz(p).wait_recv()
-    dkv = kc_ref[z].astype(F32)
-    for p in range(1, nz): dkv = dkv + kz_ref[p - 1].astype(F32)
+    kv_each(lambda cp: cp.start())
+    stage_z(2); stage_m(3); stage_y(4); stage_xy(); saves[0].start()
+    stage_z(3); stage_core(6)
+    kv_got()
+    dkv = kc_ref[z].astype(F32) + kz_ref[0].astype(F32) + kz_ref[1].astype(F32)
+    need(8, 11, 12, 13)
     cos, sin = cos_ref[...], sin_ref[...]
     qw = q_ref.shape[1]
     for i in range(qw // 128):
@@ -913,32 +1188,88 @@
     dl_ref[:, qw + 256:qw + 384] = dkv[:, 256:384].astype(B16)
     npart_ref[...] = nt(dl_ref[...], A[:, :qw + 384]).astype(B16)
     nswap.start()
-    stage_core(6)
+    stage_core(8)
     ga = tn(n1_ref[...], dl_ref[...]).astype(B16)
     for s in range(2 * nb): ga_ref[s // 2, s % 2, :, :qw + 384] = ga[s * shard:(s + 1) * shard]
-    ccopy(7).start()
-    stage_y(4); stage_z(3)
-    stage_core(7)
-    stage_y(5); stage_z(4)
+    ccopy(9).start()
+    stage_m(4); stage_y(5); stage_z(4); saves[1].start()
+    oswap.wait_recv()
+    need(2)
+    out_ref[...] = (hid_ref[...] + (part2_ref[...].astype(F32) + peer2_ref[...].astype(F32))).astype(B16)
+    saves[6].start()
+    stage_core(9)
+    stage_m(5); stage_y(6)
     nswap.wait_recv()
+    need(14)
     x = x_ref[...].astype(F32)
     r1 = rms(x)
     dn1 = npart_ref[...].astype(F32) + npeer_ref[...].astype(F32)
     gain1 = jnp.sum(dn1 * x * r1, axis=0, keepdims=True)
-    both = jnp.where(lax.broadcasted_iota(jnp.int32, (8, x.shape[1]), 0) < 4, gain1, gain2).astype(B16)
-    sel = ((lanes((8, 128)) < 64) & (lax.broadcasted_iota(jnp.int32, (8, 128), 0) == 0)) | ((lanes((8, 128)) >= 64) & (lax.broadcasted_iota(jnp.int32, (8, 128), 0) == 4))
-    gcol = tn(both, sel.astype(B16)).astype(B16)
+    gcol = tn(half_rows(gain1, gain2).astype(B16), half_select()).astype(B16)
     for s in range(2 * nb): ga_ref[s // 2, s % 2, :, qw + 384:qw + 512] = gcol[s * shard:(s + 1) * shard]
-    ccopy(8).start()
+    ccopy(10).start()
     dx_ref[...] = dh_ref[...] + norm_back(x, r1, gains_ref[0:1, :], dn1)
-    stage_core(8)
-    stage_y(6); stage_z(5); stage_y(7); stage_z(6); stage_y(8); stage_z(7); stage_z(8)
+    saves[5].start()
+    stage_core(10); stage_core(7)
+    stage_z(5); stage_m(6); stage_y(8); stage_z(6)
+    stage_m(8); stage_y(9); stage_z(8); saves[3].start()
+    stage_m(9); stage_y(10); stage_z(9)
+    stage_m(10); stage_y(7); stage_m(7); stage_z(10)
+    hs = shard // 2
+    kswap = remote(ra.at[pl.ds(pl.multiple_of((1 - tp) * hs, 8), hs), pl.ds(qw, 384)], kvx_ref, ss.at[3], sr.at[3], other)
+    kswap.start()
+    saves[4].start()
+    stage_z(7)
+    saves[2].start()
+    kswap.wait()
+    saves[7].start()
+    for cp in saves: cp.wait()
     for cp in (dswap, oswap, nswap, kvc): cp.wait_send()
-    for p in range(1, nz): kvz(p).wait_send()
+    kv_each(lambda cp: cp.wait_send())
     for k in range(K):
         ccopy(k).wait_send()
+        if k == 0:
+            xycopy().wait_send()
+            for q in range(2):
+                for i in range(3): xcopy(q, z, i, 0)(zoi).wait_send()
+            continue
         for p in range(1, nf): ycopy(k, p).wait_send()
-        for p in range(1, nz): zcopy(k, p).wait_send()
+        for i in range(3): zcopy(k, z, i, 0)(zoi).wait_send()
+
+def finish(qw, *refs):
+    given, refs = refs[:8], refs[8:]
+    o_out, dx_out, gg1, gq, gk, gv, go, gg2, gg, gu, gd, rd, rg, ru, ro, ra, dx_ref, out_ref, kvx_ref, k_ref, v_ref, gr1, gr2, isem, sem = refs
+    tp = lax.axis_index("tp")
+    hs = kvx_ref.shape[0]
+    loads = [pltpu.make_async_copy(a, b, isem.at[i]) for i, (a, b) in enumerate(zip(given, (rd, rg, ru, ro, ra, dx_ref, out_ref, kvx_ref)))]
+    order = (4, 7, 5, 0, 1, 2, 6, 3)
+    for i in order: loads[i].start()
+    copies = []
+    def store(a, b):
+        copies.append(pltpu.make_async_copy(a, b, sem.at[len(copies)]))
+        copies[-1].start()
+    loads[4].wait()
+    store(ra.at[:, pl.ds(0, qw)], gq)
+    loads[7].wait()
+    mine = ra[pl.ds(pl.multiple_of(tp * hs, 8), hs), qw:qw + 384]
+    theirs = kvx_ref[...]
+    lo, hi = jnp.where(tp == 0, mine, theirs), jnp.where(tp == 0, theirs, mine)
+    low = lanes((hs, 128)) < 64
+    def tile(v, i): return v[:, 128 * i:128 * (i + 1)]
+    k_ref[:, :128] = tile(lo, 0)
+    k_ref[:, 128:256] = jnp.where(low, tile(lo, 1) + tile(hi, 0), tile(hi, 0))
+    k_ref[:, 256:320] = tile(hi, 1)[:, :64]
+    v_ref[:, :128] = tile(lo, 2)
+    v_ref[:, 128:256] = jnp.where(low, pltpu.roll(tile(lo, 1), 64, 1) + tile(hi, 2), tile(hi, 2))
+    v_ref[:, 256:320] = pltpu.roll(tile(hi, 1), 64, 1)[:, :64]
+    rowsT = jnp.transpose(ra[:, qw + 384:qw + 512])
+    gr1[...] = rowsT[0:1, :]
+    gr2[...] = rowsT[64:65, :]
+    for i, a, b in ((5, dx_ref, dx_out), (0, rd, gd), (1, rg, gg), (2, ru, gu), (6, out_ref, o_out), (3, ro, go)):
+        loads[i].wait()
+        store(a, b)
+    for a, b in ((k_ref, gk), (v_ref, gv), (gr1, gg1), (gr2, gg2)): store(a, b)
+    for cp in copies: cp.wait()
 
 def fast(tokens, lengths, attn_gain, w_query, w_key, w_value, w_out, ffn_gain, w_gate, w_up, w_down, cotangent):
     micros, rows, width = tokens.shape
@@ -951,73 +1282,52 @@
     shard = w_query.shape[0]
     qw, ff = w_query.shape[1], w_gate.shape[1]
     M = micros * rows
-    def kv3(w):
-        w = lax.dynamic_slice_in_dim(w, tp * 2 * HD, 3 * HD, axis=1)
-        return w[:, :2 * HD], w[:, 2 * HD:]
-    k01, k2 = kv3(w_key); v01, v2 = kv3(w_value)
-    gains = [jnp.broadcast_to(v[:, None], (shard, 64)) for v in (attn_gain, ffn_gain)]
-    sa = jnp.concatenate([w_query, k01, k2, v2, v01] + gains, axis=1)
     aw = qw + 512
-    ends = jnp.cumsum(lengths[0], axis=1)
-    place = t * rows + jnp.arange(rows, dtype=jnp.int32)
-    begin = jnp.sum(jnp.where(place[None, :, None] >= ends[:, None, :], lengths[0][:, None, :], 0), axis=2).reshape(M, 1)
-    live = (jnp.tile(place, micros) < jnp.repeat(ends[:, -1], rows)).astype(F32)[:, None]
-    inverse = jnp.exp(jnp.arange(HD // 2, dtype=F32) * (-2.0 * math.log(THETA) / HD))
-    angle = (jnp.tile(place, micros)[:, None] - begin).astype(F32) * jnp.tile(inverse, 4)[None, :]
-    cos, sin = jnp.cos(angle), jnp.sin(angle)
-    begin = jnp.broadcast_to(begin, (M, 128))
-    live = jnp.broadcast_to(live, (M, 128))
     x = tokens.reshape(M, width)
     pairs = qw // 128
     keys = nblk * rows
-    half = ff // 2
     S = pltpu.SemaphoreType.DMA
     inv, ina = pl.BlockSpec(memory_space=VMEM), pl.BlockSpec(memory_space=pl.ANY)
     ns = nb * 2
-    wide = [(m, h * half, half) for m in (2, 3, 4) for h in range(2)]
-    chunks = [(0, 0, qw), (0, qw, 512), (1, 0, qw)] + wide
-    outs = [((width, aw), B16), ((width, qw), B16), ((width, ff), B16), ((width, ff), B16), ((width, ff), B16), ((nctx, M, 384), B16),
-        ((M, width), B16), ((M, qw), B16), ((M, qw), B16), ((micros * pairs, rows, 2 * keys), B16), ((M, width), B16), ((M, width), B16), ((8, width), F32)]
-    A, O, G, U, Dn, kvall, n1, q, ao, pr, part, peer, gains = pl.pallas_call(
+    big = ff // 512 * 256 + 256 * (ff // 256 % 2)
+    small = ff - big
+    chunks = [(0, 0, qw), (0, qw, 512), (1, 0, qw), (2, 0, big), (3, 0, big), (2, big, small), (3, big, small), (4, 0, ff - 1280), (4, ff - 1280, 512), (4, ff - 768, 512), (4, ff - 256, 256)]
+    outs = [((width, aw), B16), ((width, qw), B16), ((nctx, M, 384), B16), ((M, width), B16), ((M, qw), B16), ((M, qw), B16), ((micros * pairs, rows, 2 * keys), B16),
+        ((8, width), F32), ((M, 128), F32), ((M, 128), F32), ((M, width), B16), ((M, width), F32), ((M, width), B16), ((M, width), B16)] + [((width, ff), B16), ((width, M), B16), ((M, ff), B16), ((M, ff), B16)]
+    smem = pl.BlockSpec(memory_space=pltpu.SMEM)
+    slots = 32
+    A, O, kvall, n1, q, ao, pr, gains, cos, sin, g, hid, part2, dpart, gd, n2T, dgate, dup = pl.pallas_call(
         functools.partial(front, nf, nz, micros, rows, nblk, chunks, shard),
         out_shape=[jax.ShapeDtypeStruct(s, d) for s, d in outs],
-        in_specs=[inv] * 9, out_specs=[inv, inv, ina, ina, ina] + [inv] * 8,
-        scratch_shapes=[VMEM((M, width), F32), S((9, n_slots(nf, nz))), S((9, ns)), S((5,)), S((1, n_slots(1, nz))), S((1, nctx)), S((micros,)), S((micros,))],
-        compiler_params=pltpu.CompilerParams(collective_id=0, has_side_effects=True, vmem_limit_bytes=60 << 20), name="front",
-    )(x, cos, sin, begin, sa, w_out.T, w_gate, w_up, w_down.T)
-    outs = [((M, width), F32), ((M, width), B16), ((M, width), B16), ((M, width), B16)] + [((width, ff), B16)] * 3
-    hid, part2, g, dpart, gg, gu, gd = pl.pallas_call(
-        middle, out_shape=[jax.ShapeDtypeStruct(s, d) for s, d in outs],
-        in_specs=[inv] * 4 + [ina] * 3 + [inv] * 2, out_specs=[inv] * 4 + [ina] * 3,
-        scratch_shapes=[VMEM((width, ff), B16)] * 3 + [VMEM((M, ff), F32)] * 2 + [VMEM((M, ff), B16), VMEM((M, width), B16)] + [VMEM((width, ff), B16)] * 3 + [S((6,))],
-        compiler_params=pltpu.CompilerParams(vmem_limit_bytes=60 << 20), name="middle",
-    )(x, part, peer, gains, G, U, Dn, cotangent.reshape(M, width), live)
-    chunks = [(m, h * half, half) for m in range(3) for h in range(2)] + [(3, 0, qw), (4, 0, qw), (4, qw, 512)]
+        in_specs=[ina, ina, smem, inv, inv, ina, inv, inv] + [ina] * 4, out_specs=[ina] * 18,
+        scratch_shapes=[VMEM(s, d) for s, d in outs[:14]] + [VMEM((width, M), B16)] * 2 + [VMEM((width, ff), B16)] * 4 + [VMEM((M, ff), B16)] * 2 + [VMEM((M, width), B16)] * 2 + [VMEM((M, ff), F32)] * 2 + [VMEM((M, ff), B16), VMEM((M, width), B16)] + [VMEM((M, width), F32)] * 2
+            + [VMEM((M, 128), jnp.int32), VMEM((shard, 512), B16)] + [VMEM((M, width), B16)] * 2 + [S((2,)), S((11, slots)), S((11, ns)), S((11,)), S((1, n_slots(1, nz))), S((1, nctx)), S((micros,)), S((micros,)), S((24,))],
+        compiler_params=pltpu.CompilerParams(collective_id=0, has_side_effects=True, vmem_limit_bytes=63 << 20), name="front",
+    )(x, cotangent.reshape(M, width), lengths[0], attn_gain.reshape(1, shard), ffn_gain.reshape(1, shard), w_query, w_key, w_value, w_out.T, w_gate, w_up, w_down.T)
+    chunks = [(0, 0, 512), (0, 512, 256), (0, 768, ff - 768), (1, 0, big), (1, big, small), (2, 0, big), (2, big, small - 256), (2, ff - 256, 256), (3, 0, qw), (4, 0, qw), (4, qw, 512)]
     wd = [ff, ff, ff, qw, aw]
     K = len(chunks)
-    outs = [((shard, w), F32) for w in wd] + [((M, width), F32), ((M, width), B16)]
-    scratch = [VMEM((nb, shard, w), B16) for w in wd[:3]] + [VMEM((nb, shard, w), B16) for w in wd] + [VMEM((nf - 1, nz, shard, w), B16) for w in wd] + [VMEM((nz - 1, shard, w), B16) for w in wd]
-    scratch += [VMEM((nb, 2, shard, qw), B16), VMEM((nb, 2, shard, aw), B16), VMEM((M, width), F32), VMEM((M, qw), B16), VMEM((M, qw), F32), VMEM((nz, 2, M, 384), B16),
-        VMEM((nz, M, 384), B16), VMEM((nz - 1, M, 384), B16), VMEM((M, qw + 384), B16)] + [VMEM((M, width), B16)] * 4
-    scratch += [S((K,)), S((K,)), S((K,)), S((K, nf - 1)), S((K, nf - 1)), S((K, nz - 1)), S((K, nz - 1)), S((1,)), S((1,)), S((nz - 1,)), S((nz - 1,)), S((3,)), S((3,))]
-    rd, rg, ru, ro, ra, dx, output = pl.pallas_call(
+    hs = shard // 2
+    outs = [((shard, w), F32) for w in wd] + [((M, width), F32), ((M, width), B16), ((hs, 384), F32)]
+    scratch = [VMEM((nb, shard, ff), B16)] + [VMEM((nb, 2, shard, ff), B16)] * 2 + [VMEM((nb, shard, w), B16) for w in wd] + [VMEM((nf - 1, nz, shard, w), B16) for w in wd] + [VMEM((4, shard, w), B16) for w in wd]
+    scratch += [VMEM((4, shard, 512), B16), VMEM((nb, 2, shard, qw), B16), VMEM((nb, 2, shard, aw), B16), VMEM((M, qw), B16), VMEM((M, qw), F32), VMEM((nz, 2, M, 384), B16),
+        VMEM((nz, M, 384), B16), VMEM((2, M, 384), B16), VMEM((M, qw + 384), B16)] + [VMEM((M, width), B16)] * 3
+    given = [g, dpart, part2, hid, gains, q, kvall, O, A, ao, pr, n1, cos, sin, x, n2T, dgate, dup]
+    scratch += [VMEM(v.shape, v.dtype) for v in given] + [S((18,))] + [VMEM(s, d) for s, d in outs[:6] + outs[7:]] + [S((8,))]
+    scratch += [S((K,)), S((K,)), S((K,)), S((K, nf - 1)), S((K, nf - 1)), S((K, 6)), S((K, 8)), S((1,)), S((1,)), S((2,)), S((2,)), S((4,)), S((4,))]
+    ends = pl.pallas_call(
         functools.partial(back, nf, nz, micros, rows, nblk, chunks, shard),
         out_shape=[jax.ShapeDtypeStruct(s, d) for s, d in outs],
-        in_specs=[ina] * 3 + [inv] * 15, out_specs=[inv] * 7, scratch_shapes=scratch,
-        compiler_params=pltpu.CompilerParams(collective_id=4, has_side_effects=True, vmem_limit_bytes=63 << 20), name="back",
-    )(*[m.reshape(nb, 2, shard, ff) for m in (gd, gg, gu)], g, dpart, part2, hid, gains, q, kvall, O, A, ao, pr, n1, cos, sin, x)
-    hs = shard // 2
-    kvg = ra[:, qw:qw + 384].reshape(2, hs, 384)
-    mine = lax.dynamic_index_in_dim(kvg, tp, 0, keepdims=False)
-    theirs = swap(lax.dynamic_index_in_dim(kvg, 1 - tp, 0, keepdims=False), 5)
-    low, high = jnp.where(tp == 0, mine, theirs), jnp.where(tp == 0, theirs, mine)
-    def spread(lo, hi): return jnp.pad(lo, ((0, 0), (0, 128))) + jnp.pad(hi, ((0, 0), (128, 0)))
-    def ks(v): return v[:, :192]
-    def vs(v): return jnp.concatenate([v[:, 256:384], v[:, 192:256]], axis=1)
-    grad_key = spread(ks(low), ks(high))
-    grad_value = spread(vs(low), vs(high))
-    return (output.reshape(micros, rows, width), dx.reshape(micros, rows, width), ra[:, qw + 384], ra[:, :qw], grad_key, grad_value,
-            ro.T, ra[:, qw + 448], rg, ru, rd.T)
+        in_specs=[ina] * 19, out_specs=[ina] * 8, scratch_shapes=scratch,
+        compiler_params=pltpu.CompilerParams(collective_id=4, has_side_effects=True, vmem_limit_bytes=67043328), name="back",
+    )(gd.reshape(nb, 2, shard, ff), *given)
+    outs = [((M, width), B16), ((M, width), F32), ((1, shard), F32), ((shard, qw), F32), ((hs, 5 * HD), F32), ((hs, 5 * HD), F32), ((shard, qw), F32), ((1, shard), F32)] + [((shard, ff), F32)] * 3
+    output, dx, gain1, gq, gk, gv, go, gain2, gg, gu, gd = pl.pallas_call(
+        functools.partial(finish, qw), out_shape=[jax.ShapeDtypeStruct(s, d) for s, d in outs],
+        in_specs=[ina] * 8, out_specs=[ina] * 11,
+        scratch_shapes=[VMEM(v.shape, v.dtype) for v in ends] + [VMEM((hs, 5 * HD), F32)] * 2 + [VMEM((1, shard), F32)] * 2 + [S((8,)), S((11,))], name="finish",
+    )(*ends)
+    return (output.reshape(micros, rows, width), dx.reshape(micros, rows, width), gain1.reshape(shard), gq, gk, gv, go.T, gain2.reshape(shard), gg, gu, gd.T)
 
 
 def solution(mesh):
@@ -1036,7 +1346,7 @@
         P(None, ("fsdp", "ctx"), None),
     )
     def chosen(*args):
-        fits = args[3].shape[0] % 16 == 0 and mesh.shape["tp"] == 2 and mesh.shape["fsdp"] == 2 and mesh.shape["ctx"] % 2 == 0
+        fits = args[3].shape[0] % 16 == 0 and mesh.shape["tp"] == 2 and mesh.shape["fsdp"] == 2 and mesh.shape["ctx"] == 8
         return (fast if fits else shards)(*args)
 
     return jax.shard_map(

time: 328 us -> 237 us (0.72)
  Pallas kernels: 301 us -> 235 us
  local copies, waits for them, and re-layouts: 19.6 us -> 0 us
  other arithmetic: 3.78 us -> 0 us
    pallas_call x1, Pallas kernels: 145 us -> 112 us  [fast(): pl.pallas_call(functools.partial(back, nf, nz, micros, rows, nblk, chunks...]
    pallas_call x2 -> x1, Pallas kernels: 34.4 us -> 3.58 us  [fast(): pl.pallas_call(functools.partial(finish, qw), out_shape=[jax.ShapeDtypeSt...]
    unnamed x20 -> x0, local copies, waits for them, and re-layouts: 7.04 us -> none
    slice x11 -> x0, local copies, waits for them, and re-layouts: 6.25 us -> none  [the longest x2 1.67 us: kv3(): return (w[:, :2 * HD], w[:, 2 * HD:])]
where the time goes in v3:
time: 237 us; the launch traced here: 236 us
  Pallas kernels  235 us (99%)
    pallas_call x1, Pallas kernels, fast(): pl.pallas_call(functools.partial(front, nf, nz, micros, rows, nblk, chunk...  119 us
    pallas_call x1, Pallas kernels, fast(): pl.pallas_call(functools.partial(back, nf, nz, micros, rows, nblk, chunks...  112 us

profile of v3, /device:TPU:0, one launch (start us, length us, event | category | flops | bytes accessed | tf_op | source)
XLA Modules:
  0.0 236.3 jit_solution(3385315580562376192)
XLA Ops:
  0.6 119.5 %front.1 = (bf16[1280,1152]{1,0:T(8,128)(2,1)}, bf16[1280,640]{1,0:T(8,128)(2,1)}, bf16[8,256,384]{2,1,0:T(8,128)(2,1)}, bf16[256,1280]{1,0:T(8,128)(2,1)}, bf16...) custom-call(bf16[256,1280]{1,0:T(8,128)(2,1)} %bitcast.15, ...), custom_call_target="tpu_custom_call" | custom-call | tf_op jit(solution)/shard_map/front/pallas_call | solution.py:1299
  120.1 112.4 %back.1 = (f32[80,1792]{1,0:T(8,128)}, f32[80,1792]{1,0:T(8,128)}, f32[80,1792]{1,0:T(8,128)}, f32[80,640]{1,0:T(8,128)}, f32[80,1152]{1,0:T(8,128)}, /*index=5*...) custom-call(bf16[8,2,80,1792]{3,2,1,0:T(8,128)(2,1)} %bitcast.14, ...), custom_call_target="tpu_custom_call" | custom-call | tf_op jit(solution)/shard_map/back/pallas_call | solution.py:1318
  232.5 3.6 %finish.1 = (bf16[256,1280]{1,0:T(8,128)(2,1)}, f32[256,1280]{1,0:T(8,128)}, f32[1,80]{1,0:T(1,128)}, f32[80,640]{1,0:T(8,128)}, f32[40,320]{1,0:T(8,128)}, /*in...) custom-call(f32[80,1792]{1,0:T(8,128)} %get-tuple-element.66.refs_0_, ...), custom_call_target="tpu_custom_call" | custom-call | tf_op jit(solution)/shard_map/finish/pallas_call | solution.py:1325

commit v4 on v3

--- a/solution.py
+++ b/solution.py
@@ -858,9 +858,9 @@
         part_ref[sl, :] = nt(ao_ref[sl, :], O[...]).astype(B16)
         swap_part(m).start()
     save(ao_ref, ao_hbm); save(pr_ref, pr_hbm)
-    W.own(8); last(4); hop(6, 3); hop(7, 2); hop(8, 1); last(5); W.own(9)
-    W.arrived(3); W.arrived(4); W.arrived(5)
-    for k in (3, 4, 5): local(k).wait()
+    W.own(8); last(4); hop(6, 3); hop(7, 2); hop(8, 1); W.own(9)
+    W.arrived(3); W.arrived(4)
+    for k in (3, 4): local(k).wait()
     for m in range(micros): swap_part(m).wait_recv()
     hid = x_ref[...].astype(F32) + (part_ref[...].astype(F32) + peer_ref[...].astype(F32))
     hid_ref[...] = hid
@@ -897,6 +897,8 @@
     dsum_ref[...] = jnp.zeros_like(dsum_ref)
     psum_ref[...] = jnp.zeros_like(psum_ref)
     lax.fori_loop(0, tiles[3], forward, 0)
+    last(5)
+    W.arrived(5); local(5).wait()
     hop(7, 3); hop(8, 2); hop(9, 1); W.own(10); last(6)
     W.arrived(6); local(6).wait()
     lax.fori_loop(tiles[3], ff // 256, forward, 0)

time: 237 us -> 237 us (level)
  no operation moved by 1% of the time
where the time goes in v4:
time: 237 us
  Pallas kernels  236 us (100%)
    pallas_call x1, Pallas kernels, fast(): pl.pallas_call(functools.partial(front, nf, nz, micros, rows, nblk, chunk...  119 us
    pallas_call x1, Pallas kernels, fast(): pl.pallas_call(functools.partial(back, nf, nz, micros, rows, nblk, chunks...  114 us

profile of v4, /device:TPU:0, one launch (start us, length us, event | category | flops | bytes accessed | tf_op | source)
XLA Modules:
  0.0 237.2 jit_solution(14493298179692269921)
XLA Ops:
  0.6 119.2 %front.1 = (bf16[1280,1152]{1,0:T(8,128)(2,1)}, bf16[1280,640]{1,0:T(8,128)(2,1)}, bf16[8,256,384]{2,1,0:T(8,128)(2,1)}, bf16[256,1280]{1,0:T(8,128)(2,1)}, bf16...) custom-call(bf16[256,1280]{1,0:T(8,128)(2,1)} %bitcast.15, ...), custom_call_target="tpu_custom_call" | custom-call | tf_op jit(solution)/shard_map/front/pallas_call | solution.py:1301
  119.9 113.6 %back.1 = (f32[80,1792]{1,0:T(8,128)}, f32[80,1792]{1,0:T(8,128)}, f32[80,1792]{1,0:T(8,128)}, f32[80,640]{1,0:T(8,128)}, f32[80,1152]{1,0:T(8,128)}, /*index=5*...) custom-call(bf16[8,2,80,1792]{3,2,1,0:T(8,128)(2,1)} %bitcast.14, ...), custom_call_target="tpu_custom_call" | custom-call | tf_op jit(solution)/shard_map/back/pallas_call | solution.py:1320
  233.5 3.6 %finish.1 = (bf16[256,1280]{1,0:T(8,128)(2,1)}, f32[256,1280]{1,0:T(8,128)}, f32[1,80]{1,0:T(1,128)}, f32[80,640]{1,0:T(8,128)}, f32[40,320]{1,0:T(8,128)}, /*in...) custom-call(f32[80,1792]{1,0:T(8,128)} %get-tuple-element.66.refs_0_, ...), custom_call_target="tpu_custom_call" | custom-call | tf_op jit(solution)/shard_map/finish/pallas_call | solution.py:1327
